TPU v7x, 128 devices: a whole 4x4x4 slice. The times are simulated.
128 devices in a mesh: rows: 32 (over x, z, core), cols: 4 (over y).
Axes of the slice: x: 4, y: 4, z: 4, core: 2. Of those that a mesh axis runs over, the one named last changes fastest.
Arguments:
- points: float32 [98304, 1024], P('rows', 'cols'), may hold values from -80 to 80
- codes: int32 [128, 98304], P('cols', 'rows'), may hold values from 0 to 255, as said below
- rotation: float32 [1024, 1024], P('rows', 'cols'), may hold values from -0.16 to 1.16
Outputs:
- new_rotation: float32 [1024, 1024], P('rows', 'cols')
- centroids: float32 [128, 2048], P('cols')
Inputs may be any that keep to these rules, and one draw needn't show every extreme that they name: For every subspace, the first 256 vectors hold each of the 256 codes once.
All inputs are finite; a program needn't handle non-finite values.
Results may differ from a plain program's by a relative error of at most 0.00011.
Values sent between devices are 32-bit elements; how exact they have to be, the bound alone decides.
No kernel may reach another device: no remote copies, remote signals or barrier semaphores. Data moves between devices by JAX's collectives and lax.ppermute only.
A program may use at most 128 MiB of HBM per device.

v0:
```python
import jax
import jax.numpy as jnp
from jax import lax
from jax.sharding import PartitionSpec as P

D = 1024
K = 256
NS_ITERS = 6
SUB = 8


def contract_rows(left, right):
    return lax.dot_general(
        left,
        right,
        (((0,), (0,)), ((), ())),
        precision=lax.Precision.HIGHEST,
        preferred_element_type=jnp.float32,
    )


def matmul_high(left, right):
    return jnp.dot(left, right, precision=lax.Precision.HIGHEST, preferred_element_type=jnp.float32)


def gram_parts(current):
    row_block = lax.all_gather(current, "cols", axis=1, tiled=True)
    partial_gram = contract_rows(row_block, current)
    return (row_block, lax.psum(partial_gram, "rows"))


def shards(points, codes, rotation):
    gathered = lax.all_gather(points, "cols", axis=1, tiled=True)
    column_panel = lax.all_gather(rotation, "rows", axis=0, tiled=True)
    rotated = matmul_high(gathered, column_panel)
    local_subspaces = codes.shape[0]
    vector_count = rotated.shape[0]
    panel_width = rotated.shape[1]
    batch_size = 4
    turn_count = local_subspaces // batch_size
    code_range = jnp.arange(K, dtype=jnp.int32)
    rotated_groups = rotated.reshape(vector_count, turn_count, batch_size, SUB).transpose(
        1, 2, 0, 3
    )
    code_groups = codes.reshape(turn_count, batch_size, vector_count)

    def local_totals(carry, item):
        block_values, code_block = item
        indicator = (code_block[:, :, None] == code_range[None, None, :]).astype(jnp.float32)
        value_sums = jnp.einsum(
            "gnk,gns->gks",
            indicator,
            block_values,
            precision=lax.Precision.HIGHEST,
            preferred_element_type=jnp.float32,
        )
        return (carry, (value_sums, jnp.sum(indicator, axis=1)))

    unused, (value_totals, code_totals) = lax.scan(local_totals, 0.0, (rotated_groups, code_groups))
    value_totals = value_totals.reshape(local_subspaces, K * SUB)
    code_totals = code_totals.reshape(local_subspaces, K)
    owned_values, owned_counts = (
        lax.psum_scatter(value_totals, "rows", scatter_dimension=0, tiled=True),
        lax.psum_scatter(code_totals, "rows", scatter_dimension=0, tiled=True),
    )
    owned_centers = (owned_values.reshape(-1, K, SUB) / owned_counts[:, :, None]).reshape(
        -1, K * SUB
    )
    centroids = lax.all_gather(owned_centers, "rows", axis=0, tiled=True)
    center_groups = centroids.reshape(turn_count, batch_size, K, SUB)

    def rebuild(carry, item):
        code_block, center_block = item
        indicator = (code_block[:, :, None] == code_range[None, None, :]).astype(jnp.float32)
        return (
            carry,
            jnp.einsum(
                "gnk,gks->gns",
                indicator,
                center_block,
                precision=lax.Precision.HIGHEST,
                preferred_element_type=jnp.float32,
            ),
        )

    unused, rebuilt = lax.scan(rebuild, 0.0, (code_groups, center_groups))
    approx = rebuilt.transpose(2, 0, 1, 3).reshape(vector_count, panel_width)
    cross_block = lax.psum_scatter(
        contract_rows(gathered, approx), "rows", scatter_dimension=0, tiled=True
    )
    square_total = lax.psum(jnp.sum(cross_block * cross_block), ("rows", "cols"))
    iterate = 1.7 * cross_block / jnp.sqrt(square_total + 1e-06)
    for step_index in range(NS_ITERS):
        row_block, gram_panel = gram_parts(iterate)
        iterate = 1.5 * iterate - 0.5 * matmul_high(row_block, gram_panel)
    return (iterate * D**0.5, centroids)


def solution(mesh):
    in_specs = (P("rows", "cols"), P("cols", "rows"), P("rows", "cols"))
    out_specs = (P("rows", "cols"), P("cols", None))
    return jax.shard_map(shards, mesh=mesh, in_specs=in_specs, out_specs=out_specs, check_vma=False)
```

profile of v0, /device:TPU:1, one launch (start us, length us, event | category | flops | bytes accessed | tf_op | source)
XLA Modules:
  0.0 1367.0 jit_solution(11022926561968581953)
XLA Ops:
  8.9 48.0 %all-gather.6.cloned.1.call-done = f32[1024,256]{1,0:T(8,128)} async-done(((f32[32,256]{1,0:T(8,128)}), f32[1024,256]{1,0:T(8,128)}) %all-gather.6.cloned.1.call-update) | async-done | bytes 1048592 | tf_op jit(solution)/shard_map/all_gather | solution.py:34
  56.8 119.1 %all-gather.4.cloned.1.call-done = f32[3072,1024]{1,0:T(8,128)} async-done(((f32[3072,256]{1,0:T(8,128)}), f32[3072,1024]{1,0:T(8,128)}) %all-gather.4.cloned.1.call-update) | async-done | bytes 12582928 | tf_op jit(solution)/shard_map/all_gather | solution.py:33
  175.9 13.8 %fusion.28 = f32[3072,256]{0,1:T(8,128)S(1)} fusion(f32[3072,1024]{1,0:T(8,128)} %all-gather.4.cloned.1.call-done, f32[1024,256]{1,0:T(8,128)} %all-gather.6.cloned.1.call-done), kind=kOutput, calls=%fused_computation.43 | convolution fusion | flops 9663676416 | bytes 16777216 | tf_op jit(solution)/shard_map/dot_general | solution.py:23
  189.7 63.4 %while.24 = (s32[]{:T(128)}, f32[8,4,256,8]{2,3,1,0:T(8,128)}, f32[8,4,256]{2,1,0:T(4,128)}, s32[8,4,3072]{2,1,0:T(4,128)S(1)}, f32[8,4,3072,8]{2,3,1,0:T(8,128)S(1)}, /*index=5*/s32[]{:T(128)}) while((s32[]{:T(128)}, f32[8,4,256,8]{2,3,1,0:T(8,128)}, f32[8,4,256]{2,1,0:T(4,128)}, s32[8,4,3072]{2,1,0:T(4,128)S(1)}, ...), condition=%wide.region_2.3_spmd.clone, body=%wide.region_0.2_spmd.clone.sunk | while | flops 314571776 | bytes 636489 | solution.py:59
  189.8 5.1 fusion.69
  194.8 2.3 fusion.70
  197.7 5.0 fusion.69
  202.7 2.3 fusion.70
  205.6 5.0 fusion.69
  210.7 2.3 fusion.70
  213.5 5.0 fusion.69
  218.6 2.3 fusion.70
  221.5 5.0 fusion.69
  226.5 2.3 fusion.70
  229.4 5.0 fusion.69
  237.3 5.0 fusion.69
  245.2 5.0 fusion.69
  253.1 3.5 copy.22
  256.6 4.7 reshape.46
  262.8 123.3 %all-reduce.1 = f32[32,256]{1,0:T(8,128)S(1)} all-reduce(f32[32,256]{1,0:T(8,128)S(1)} %reshape.47), channel_id=3, replica_groups=mesh['rows'=32,'cols'=4] {'rows'}, use_global_device_ids=true, to_apply=%region_4.5.clone | all-reduce | flops 8192 | bytes 65536
  388.6 27.5 %all-gather = f32[32,1,2048]{2,1,0:T(1,128)S(1)} all-gather(f32[1,1,2048]{2,1,0:T(1,128)S(1)} %fusion.27), channel_id=1, replica_groups=mesh['rows'=32,'cols'=4] {'rows'}, dimensions={0}, use_global_device_ids=true | all-gather | bytes 270336 | tf_op jit(solution)/shard_map/all_gather | solution.py:69
  416.7 3.7 reshape.48
  420.4 2.8 copy.23
  423.1 59.3 %while.25 = (s32[]{:T(128)}, f32[8,4,3072,8]{2,3,1,0:T(8,128)}, s32[8,4,3072]{2,1,0:T(4,128)S(1)}, f32[8,4,256,8]{2,3,1,0:T(8,128)S(1)}, s32[]{:T(128)}) while((s32[]{:T(128)}, f32[8,4,3072,8]{2,3,1,0:T(8,128)}, s32[8,4,3072]{2,1,0:T(4,128)S(1)}, f32[8,4,256,8]{2,3,1,0:T(8,128)S(1)}, s32[]{:T(128)}) %tuple.73), condition=%wide.region_6.7_spmd.clone, body=%wide.region_5.6_spmd.clone.sunk | while | flops 305135616 | bytes 574529 | solution.py:86
  423.2 7.4 fusion.72
  430.6 7.4 fusion.72
  438.0 7.4 fusion.72
  445.4 7.4 fusion.72
  452.8 7.4 fusion.72
  460.2 7.4 fusion.72
  467.6 7.4 fusion.72
  475.0 7.4 fusion.72
  482.4 13.6 convolution_bitcast_fusion
  497.5 75.2 %reduce-scatter.4.cloned.1.call-done = f32[32,256]{1,0:T(8,128)} async-done(((f32[1024,256]{1,0:T(8,128)}), f32[32,256]{1,0:T(8,128)}) %reduce-scatter.4.cloned.1.call-update) | async-done | bytes 32784 | tf_op jit(solution)/shard_map/reduce_scatter | solution.py:88
  574.1 65.9 %psum.49 = f32[]{:T(128)} all-reduce(f32[]{:T(128)} %multiply_reduce_fusion), channel_id=1, replica_groups=mesh['rows'=32,'cols'=4] {'rows','cols'}, use_global_device_ids=true, to_apply=%region_9.10 | all-reduce | flops 1 | bytes 8 | tf_op jit(solution)/shard_map/psum | solution.py:91
  641.5 9.1 all_gather.30
  652.7 104.8 %all-reduce.10.cloned.1.call-done = f32[1024,256]{1,0:T(8,128)} async-done(((f32[1024,256]{1,0:T(8,128)}), f32[1024,256]{1,0:T(8,128)}) %all-reduce.10.cloned.1.call-update) | async-done | bytes 1048592 | tf_op jit(solution)/shard_map/psum | solution.py:29
  759.3 9.6 all_gather.31
  771.1 106.4 %all-reduce.12.cloned.1.call-done = f32[1024,256]{1,0:T(8,128)} async-done(((f32[1024,256]{1,0:T(8,128)}), f32[1024,256]{1,0:T(8,128)}) %all-reduce.12.cloned.1.call-update) | async-done | bytes 1048592 | tf_op jit(solution)/shard_map/psum | solution.py:29
  879.3 9.8 all_gather.32
  891.3 106.4 %all-reduce.14.cloned.1.call-done = f32[1024,256]{1,0:T(8,128)} async-done(((f32[1024,256]{1,0:T(8,128)}), f32[1024,256]{1,0:T(8,128)}) %all-reduce.14.cloned.1.call-update) | async-done | bytes 1048592 | tf_op jit(solution)/shard_map/psum | solution.py:29
  999.5 9.6 all_gather.33
  1011.3 106.4 %all-reduce.16.cloned.1.call-done = f32[1024,256]{1,0:T(8,128)} async-done(((f32[1024,256]{1,0:T(8,128)}), f32[1024,256]{1,0:T(8,128)}) %all-reduce.16.cloned.1.call-update) | async-done | bytes 1048592 | tf_op jit(solution)/shard_map/psum | solution.py:29
  1119.5 9.6 all_gather.34
  1131.3 106.4 %all-reduce.18.cloned.1.call-done = f32[1024,256]{1,0:T(8,128)} async-done(((f32[1024,256]{1,0:T(8,128)}), f32[1024,256]{1,0:T(8,128)}) %all-reduce.18.cloned.1.call-update) | async-done | bytes 1048592 | tf_op jit(solution)/shard_map/psum | solution.py:29
  1239.5 9.6 all_gather.35
  1252.0 105.7 %all-reduce.20.cloned.1.call-done = f32[1024,256]{1,0:T(8,128)} async-done(((f32[1024,256]{1,0:T(8,128)}), f32[1024,256]{1,0:T(8,128)}) %all-reduce.20.cloned.1.call-update) | async-done | bytes 1048592 | tf_op jit(solution)/shard_map/psum | solution.py:29
  1357.7 2.4 fusion.21
  (79 shorter events, 44.0 us)
Async XLA Ops:
  7.2 1.6 copy-start
  7.2 49.6 %all-gather.6.cloned.1.call-start = ((), (), s32[]{:S(2)}) async-start(), calls=%async_computation.2 | async-start | bytes 1081344 | tf_op jit(solution)/shard_map/all_gather | solution.py:34
  7.9 168.0 %all-gather.4.cloned.1.call-start = ((), (), s32[]{:S(2)}) async-start(), calls=%async_computation.1 | async-start | bytes 15728640 | tf_op jit(solution)/shard_map/all_gather | solution.py:33
  8.7 378.4 %all-reduce.22.cloned.1.call-start = ((), (), s32[]{:S(2)}) async-start(), calls=%async_computation.10 | async-start | bytes 524288
  256.6 4.8 copy-start.1
  261.3 311.4 %reduce-scatter.4.cloned.1.call-start = ((), (), s32[]{:S(2)}) async-start(), calls=%async_computation.9 | async-start | bytes 1081344 | tf_op jit(solution)/shard_map/reduce_scatter | solution.py:88
  497.4 260.1 %all-reduce.10.cloned.1.call-start = ((), (), s32[]{:S(2)}) async-start(), calls=%async_computation.3 | async-start | bytes 2097152 | tf_op jit(solution)/shard_map/psum | solution.py:29
  652.7 224.8 %all-reduce.12.cloned.1.call-start = ((), (), s32[]{:S(2)}) async-start(), calls=%async_computation.4 | async-start | bytes 2097152 | tf_op jit(solution)/shard_map/psum | solution.py:29
  771.0 226.7 %all-reduce.14.cloned.1.call-start = ((), (), s32[]{:S(2)}) async-start(), calls=%async_computation.5 | async-start | bytes 2097152 | tf_op jit(solution)/shard_map/psum | solution.py:29
  891.2 226.5 %all-reduce.16.cloned.1.call-start = ((), (), s32[]{:S(2)}) async-start(), calls=%async_computation.6 | async-start | bytes 2097152 | tf_op jit(solution)/shard_map/psum | solution.py:29
  1011.2 226.5 %all-reduce.18.cloned.1.call-start = ((), (), s32[]{:S(2)}) async-start(), calls=%async_computation.7 | async-start | bytes 2097152 | tf_op jit(solution)/shard_map/psum | solution.py:29
  1131.2 226.5 %all-reduce.20.cloned.1.call-start = ((), (), s32[]{:S(2)}) async-start(), calls=%async_computation.8 | async-start | bytes 2097152 | tf_op jit(solution)/shard_map/psum | solution.py:29
Sparse Core Ops, SparseCore 0:
  10.3 46.5 all-gather.5
  58.5 117.3 all-gather.3
  261.4 102.5 all-reduce.21
  497.5 75.0 reduce-scatter.3
  652.8 104.6 all-reduce.9
  771.2 106.2 all-reduce.11
  891.4 106.3 all-reduce.13
  1011.4 106.2 all-reduce.15
  1131.3 106.3 all-reduce.17
  1251.4 106.2 all-reduce.19
where the time goes:
time: 1370 us
  waiting for transfers between devices  880 us (64%)
  blocking collectives  274 us (20%)
  matrix products  151 us (11%)
  local copies, waits for them, and re-layouts  24.9 us (2%)
  other arithmetic  21.8 us (2%)
  between operations  15 us (1%)
    psum x6, waiting for transfers between devices, gram_parts(): return (row_block, lax.psum(partial_gram, 'rows'))  636 us
    unnamed x1, blocking collectives  123 us
    all_gather x1, waiting for transfers between devices, shards(): gathered = lax.all_gather(points, 'cols', axis=1, tiled=True)  119 us
    reduce_scatter x1, waiting for transfers between devices, shards(): lax.psum_scatter(contract_rows(gathered, approx), 'rows', scatter_dimensi...  75.2 us
    psum x1, blocking collectives, shards(): lax.psum(jnp.sum(cross_block * cross_block), ('rows', 'cols'))  65.9 us
    dot_general x8, matrix products, rebuild(): jnp.einsum('gnk,gks->gns', indicator, center_block, precision=lax.Precisi...  59.2 us
    all_gather x6, blocking collectives, gram_parts(): row_block = lax.all_gather(current, 'cols', axis=1, tiled=True)  57.4 us
    all_gather x1, waiting for transfers between devices, shards(): column_panel = lax.all_gather(rotation, 'rows', axis=0, tiled=True)  48 us
  transfers between devices with their start and end apart: 10, of which 9 were waited for; matrix products, arithmetic and copies ran while one was open for 0% of the time, Pallas kernels for 0%

commit v1 on v0

v1 whole, which is shorter than its diff:
```python
import jax
import jax.numpy as jnp
from jax import lax
from jax.experimental import pallas as pl
from jax.experimental.pallas import tpu as pltpu
from jax.sharding import Mesh, PartitionSpec as P

D = 1024
M = 128
K = 256
NS_ITERS = 6
SUB = 8
ROWS = ("x", "z", "core")
OWNERS = ("y", "x", "z", "core")
BF16 = jnp.bfloat16
F32 = jnp.float32
NN = (((1,), (0,)), ((), ()))
NT = (((1,), (1,)), ((), ()))


def split(value):
    high = value.astype(BF16)
    return high, (value - high.astype(F32)).astype(BF16)


def mxu(left, right, dims):
    return lax.dot_general(left, right, dims, preferred_element_type=F32)


def dot3(left_high, left_low, right_high, right_low, dims):
    return (
        mxu(left_high, right_high, dims)
        + mxu(left_high, right_low, dims)
        + mxu(left_low, right_high, dims)
    )


def spread_to(value, axes, count):
    copies = jnp.broadcast_to(value[None], (count,) + value.shape)
    return lax.all_to_all(copies, axes, 0, 0, tiled=True)


def sums_kernel(y_ref, pts_ref, rot_ref, c0, c1, c2, c3, out_ref, rotated_ref, ph_ref, pl_ref):
    count = pts_ref.shape[0]
    ph, plo = split(pts_ref[...])
    ph_ref[...] = ph
    pl_ref[...] = plo
    y = y_ref[0]

    def rotate(j, carry):
        panel = rot_ref[:, pl.ds(pl.multiple_of(j * 256, 256), 256)].T
        rh, rl = split(panel)
        part = dot3(rh, rl, ph_ref[...], pl_ref[...], NT)
        rotated_ref[pl.ds(j * 32, 32)] = part.reshape(32, SUB, count)
        return carry

    lax.fori_loop(0, D // 256, rotate, 0)

    step = 512
    rows16 = lax.broadcasted_iota(jnp.int32, (16, step), 0).astype(F32)
    marks = [(rows16 + 16.0 * t).astype(BF16) for t in range(4)]
    one = jnp.ones((16, step), BF16)
    zero = jnp.zeros((16, step), BF16)
    lane = lax.broadcasted_iota(jnp.int32, (SUB, 128), 1)
    for i, codes_ref in enumerate((c0, c1, c2, c3)):
        block = lax.rem(y + 4 - i, 4)

        def group(eight, half_group, codes_ref, block):
            total = jnp.zeros((256, 256), F32)
            g = eight * 2 + half_group
            for n in range(0, count, step):
                lefts, rights = [], []
                rows = codes_ref[pl.ds(pl.multiple_of(eight * 8, 8), 8), n : n + step]
                for mm in range(4):
                    row = rows[half_group * 4 + mm : half_group * 4 + mm + 1]
                    low = jnp.broadcast_to((row & 63).astype(F32), (16, step)).astype(BF16)
                    top = jnp.broadcast_to((row >> 6).astype(F32), (16, step)).astype(BF16)
                    value = rotated_ref[block * 32 + g * 4 + mm, :, n : n + step]
                    high = value.astype(BF16).astype(F32)
                    both = jnp.concatenate([high, value - high], axis=0).astype(BF16)
                    for t in range(4):
                        lefts.append(jnp.where(top == jnp.full((16, step), t, BF16), both, zero))
                        rights.append(jnp.where(low == marks[t], one, zero))
                total += mxu(
                    jnp.concatenate(lefts, axis=0), jnp.concatenate(rights, axis=0), NT
                )
            for mm in range(4):
                slab = total[mm * 64 : mm * 64 + 64, (mm // 2) * 128 : (mm // 2) * 128 + 128]
                parts = [
                    slab[t * 16 : t * 16 + 8] + slab[t * 16 + 8 : t * 16 + 16] for t in range(4)
                ]
                for half in range(2):
                    even, odd = parts[half * 2], parts[half * 2 + 1]
                    if mm % 2 == 0:
                        odd = pltpu.roll(odd, 64, axis=1)
                    else:
                        even = pltpu.roll(even, 64, axis=1)
                    out_ref[block * 32 + g * 4 + mm, :, half * 128 : half * 128 + 128] = jnp.where(
                        lane < 64, even, odd
                    )

        def eight_rows(eight, carry, codes_ref=codes_ref, block=block):
            group(eight, 0, codes_ref, block)
            group(eight, 1, codes_ref, block)
            return carry

        lax.fori_loop(0, 4, eight_rows, 0)


def code_sums(y, points, panel, codes):
    count = points.shape[0]
    vmem = pl.BlockSpec(memory_space=pltpu.VMEM)
    return pl.pallas_call(
        sums_kernel,
        out_shape=jax.ShapeDtypeStruct((M, SUB, K), F32),
        in_specs=[pl.BlockSpec(memory_space=pltpu.SMEM)] + [vmem] * 6,
        out_specs=vmem,
        scratch_shapes=[
            pltpu.VMEM((M, SUB, count), F32),
            pltpu.VMEM((count, 256), BF16),
            pltpu.VMEM((count, 256), BF16),
        ],
        compiler_params=pltpu.CompilerParams(vmem_limit_bytes=56 * 1024 * 1024),
        name="code_sums",
    )(y, points, panel, *codes)


def cross_kernel(y_ref, pts_ref, tab_ref, c0, c1, c2, c3, out_ref, ah_ref, al_ref, ph_ref, pl_ref):
    count = pts_ref.shape[0]
    ph, plo = split(pts_ref[...])
    ph_ref[...] = ph
    pl_ref[...] = plo
    y = y_ref[0]
    for i, codes_ref in enumerate((c0, c1, c2, c3)):
        block = lax.rem(y + 4 - i, 4)

        def pair(eight, two, codes_ref, block):
            g = eight * 4 + two
            tables = [tab_ref[block * 32 + g * 2 + mm] for mm in range(2)]
            for n in range(0, count, 128):
                found = []
                rows = codes_ref[pl.ds(pl.multiple_of(eight * 8, 8), 8), n : n + 128]
                for mm in range(2):
                    row = rows[two * 2 + mm : two * 2 + mm + 1]
                    index = jnp.broadcast_to(row, (SUB, 128))
                    table = tables[mm]
                    inner = index & 127
                    first = jnp.take_along_axis(
                        table[:, :128], inner, axis=1, mode="promise_in_bounds"
                    )
                    second = jnp.take_along_axis(
                        table[:, 128:], inner, axis=1, mode="promise_in_bounds"
                    )
                    found.append(jnp.where(index < 128, first, second))
                high, low = split(jnp.concatenate(found, axis=0))
                ah_ref[pl.ds(pl.multiple_of(g * 16, 16), 16), n : n + 128] = high
                al_ref[pl.ds(pl.multiple_of(g * 16, 16), 16), n : n + 128] = low

        def eight_rows(eight, carry, codes_ref=codes_ref, block=block):
            for two in range(4):
                pair(eight, two, codes_ref, block)
            return carry

        lax.fori_loop(0, 4, eight_rows, 0)
        out_ref[pl.ds(pl.multiple_of(block * 256, 256), 256), :] = dot3(
            ah_ref[...], al_ref[...], ph_ref[...], pl_ref[...], NN
        )


def cross_part(y, points, table, codes):
    count = points.shape[0]
    vmem = pl.BlockSpec(memory_space=pltpu.VMEM)
    return pl.pallas_call(
        cross_kernel,
        out_shape=jax.ShapeDtypeStruct((D, 256), F32),
        in_specs=[pl.BlockSpec(memory_space=pltpu.SMEM)] + [vmem] * 6,
        out_specs=vmem,
        scratch_shapes=[
            pltpu.VMEM((256, count), BF16),
            pltpu.VMEM((256, count), BF16),
            pltpu.VMEM((count, 256), BF16),
            pltpu.VMEM((count, 256), BF16),
        ],
        compiler_params=pltpu.CompilerParams(vmem_limit_bytes=56 * 1024 * 1024),
        name="cross_part",
    )(y, points, table, *codes)


def shards(points, codes, rotation):
    y = lax.axis_index("y")
    y_scalar = y.astype(jnp.int32).reshape(1)
    all_codes = [codes] + [
        lax.ppermute(codes, "y", [(s, (s + i) % 4) for s in range(4)]) for i in (1, 2, 3)
    ]
    swapped = lax.ppermute(
        rotation, ("x", "y"), [(a * 4 + b, b * 4 + a) for a in range(4) for b in range(4)]
    )
    pieces = spread_to(swapped, ROWS, 32).reshape(4, 8, 32, 256)
    panel = pieces.transpose(1, 2, 0, 3).reshape(256, D)
    local_counts = jnp.sum(
        (codes[:, :, None] == jnp.arange(K, dtype=jnp.int32)).astype(F32), axis=1
    )
    counts = lax.psum(local_counts, ROWS)

    sums = code_sums(y_scalar, points, panel, all_codes)
    owned = jnp.sum(lax.all_to_all(sums, OWNERS, 0, 0, tiled=True), axis=0)
    own_row = lax.axis_index(ROWS)
    own_counts = lax.dynamic_slice_in_dim(counts, own_row, 1, axis=0)
    centers = owned / own_counts
    table = spread_to(centers, OWNERS, 128)
    mine = lax.dynamic_slice_in_dim(table, y * 32, 32, axis=0)
    centroids = mine.transpose(0, 2, 1).reshape(32, K * SUB)

    cross = cross_part(y_scalar, points, table, all_codes)
    block = jnp.sum(
        lax.all_to_all(cross.reshape(32, 32, 256), ROWS, 0, 0, tiled=True), axis=0
    )
    whole = spread_to(block, ROWS + ("y",), 128)
    whole = whole.reshape(32, 4, 32, 256).transpose(0, 2, 1, 3).reshape(D, D)
    iterate = 1.7 * whole / jnp.sqrt(jnp.sum(whole * whole) + 1e-06)
    for step_index in range(NS_ITERS):
        gram = lax.dot_general(iterate, iterate, NT, precision=lax.Precision.HIGH, preferred_element_type=F32)
        iterate = 1.5 * iterate - 0.5 * lax.dot_general(
            gram, iterate, NN, precision=lax.Precision.HIGH, preferred_element_type=F32
        )
    out = lax.dynamic_slice(iterate, (y * 256, own_row * 32), (256, 32)).T
    return (out * D**0.5, centroids)


def solution(mesh):
    grid = Mesh(mesh.devices.reshape(4, 4, 2, 4), ("x", "z", "core", "y"))
    in_specs = (P(ROWS, "y"), P("y", ROWS), P(ROWS, "y"))
    out_specs = (P(ROWS, "y"), P("y", None))
    return jax.shard_map(shards, mesh=grid, in_specs=in_specs, out_specs=out_specs, check_vma=False)
```

time: 1370 us -> 486 us (0.35)
  waiting for transfers between devices: 880 us -> 68.3 us
  blocking collectives: 274 us -> 175 us
  matrix products: 151 us -> 92.9 us
  Pallas kernels: 0 us -> 57.9 us
  starting transfers between devices: 0.41 us -> 35.7 us
    psum x6 -> x0, waiting for transfers between devices: 636 us -> none  [gram_parts(): return (row_block, lax.psum(partial_gram, 'rows'))]
    all_gather x2 -> x0, waiting for transfers between devices: 167 us -> none  [the longest x1 119 us: shards(): gathered = lax.all_gather(points, 'cols', axis=1, tiled=True)]
    unnamed x1 -> x0, blocking collectives: 123 us -> none
    all_gather x7 -> x0, blocking collectives: 84.9 us -> none  [the longest x6 57.4 us: gram_parts(): row_block = lax.all_gather(current, 'cols', axis=1, tiled=True)]
    reduce_scatter x1 -> x0, waiting for transfers between devices: 75.2 us -> none  [shards(): lax.psum_scatter(contract_rows(gathered, approx), 'rows', scatter_dimensi...]
    all_to_all x0 -> x3, waiting for transfers between devices: none -> 64.6 us  [the longest x2 64.6 us: spread_to(): return lax.all_to_all(copies, axes, 0, 0, tiled=True)]
    psum x1, blocking collectives: 65.9 us -> 124 us  [shards(): counts = lax.psum(local_counts, ROWS)]
    pallas_call x0 -> x2, Pallas kernels: none -> 57.9 us  [the longest x1 30.5 us: cross_part(): pl.pallas_call(cross_kernel, out_shape=jax.ShapeDtypeStruct((D, 256), F32...]
  transfers between devices with their start and end apart: 10 -> 7, of which waited for: 9 -> 3; matrix products, arithmetic and copies ran while one was open for 0% -> 5% of each run, Pallas kernels for 0% -> 0%
where the time goes in v1:
time: 486 us; the launch traced here: 478 us
  blocking collectives  175 us (36%)
  matrix products  92.9 us (19%)
  waiting for transfers between devices  68.3 us (14%)
  Pallas kernels  57.9 us (12%)
  starting transfers between devices  35.7 us (7%)
  other arithmetic  26.4 us (5%)
  local copies, waits for them, and re-layouts  20.6 us (4%)
    psum x1, blocking collectives, shards(): counts = lax.psum(local_counts, ROWS)  124 us
    all_to_all x2, waiting for transfers between devices, spread_to(): return lax.all_to_all(copies, axes, 0, 0, tiled=True)  64.6 us
    dot_general x6, matrix products, shards(): lax.dot_general(gram, iterate, NN, precision=lax.Precision.HIGH, preferre...  47.3 us
    dot_general x6, matrix products, shards(): lax.dot_general(iterate, iterate, NT, precision=lax.Precision.HIGH, prefe...  45.6 us
    pallas_call x1, Pallas kernels, cross_part(): pl.pallas_call(cross_kernel, out_shape=jax.ShapeDtypeStruct((D, 256), F32...  30.5 us
    all_to_all x1, blocking collectives, spread_to(): return lax.all_to_all(copies, axes, 0, 0, tiled=True)  28.9 us
    pallas_call x1, Pallas kernels, code_sums(): pl.pallas_call(sums_kernel, out_shape=jax.ShapeDtypeStruct((M, SUB, K), F...  27.4 us
    all_to_all x2, starting transfers between devices, spread_to(): return lax.all_to_all(copies, axes, 0, 0, tiled=True)  23.3 us
  transfers between devices with their start and end apart: 7, of which 3 were waited for; matrix products, arithmetic and copies ran while one was open for 5% of the time, Pallas kernels for 0%

profile of v1, /device:TPU:1, one launch (start us, length us, event | category | flops | bytes accessed | tf_op | source)
XLA Modules:
  0.0 478.4 jit_solution(13834698323625539990)
XLA Ops:
  0.6 1.4 collective-permute-start
  2.0 0.0 collective-permute-done
  2.0 1.1 broadcast_in_dim.6
  3.2 17.9 %all-to-all-start = ((f32[32,32,256]{2,1,0:T(8,128)}), f32[32,32,256]{2,1,0:T(8,128)S(1)}, u32[]{:S(2)}, u32[]{:S(2)}) async-start(f32[32,32,256]{2,1,0:T(8,128)} %broadcast_in_dim.6), calls=%async_computation | async-start | bytes 2097152 | tf_op jit(solution)/shard_map/all_to_all | solution.py:40
  21.1 1.3 collective-permute-start.3
  22.4 1.6 collective-permute-start.2
  24.0 14.0 %all-to-all-done = f32[32,32,256]{2,1,0:T(8,128)S(1)} async-done(((f32[32,32,256]{2,1,0:T(8,128)}), f32[32,32,256]{2,1,0:T(8,128)S(1)}, u32[]{:S(2)}, u32[]{:S(2)}) %all-to-all-start) | async-done | bytes 1048608 | tf_op jit(solution)/shard_map/all_to_all | solution.py:40
  38.0 0.7 copy.10
  38.7 1.2 copy.15
  39.9 0.0 collective-permute-done.3.c3
  39.9 0.0 collective-permute-done.2.c2
  39.9 3.7 collective-permute-done.1.c1
  43.6 0.8 copy-done.4
  44.3 27.4 %code_sums.1 = f32[128,8,256]{2,1,0:T(8,128)} custom-call(s32[1]{0:T(128)} %bitcast.y_ref, f32[3072,256]{1,0:T(8,128)} %pts_ref.3, f32[256,1024]{1,0:T(8,128)} %bitcast.52, s32[32,3072]{1,0:T(8,128)} %c0.3, s32[32,3072]{1,0:T(8,128)} %copy-done.4, s32[32,3072]{1,0:T(8,128)} %copy-done.3, s32[32,3072]{1,0:T(8,128)} %copy-done.2), custom_call_target="tpu_custom_call" | custom-call | tf_op jit(solution)/shard_map/code_sums/pallas_call | solution.py:113
  71.7 8.1 %all-to-all-start.1 = ((f32[128,8,256]{2,1,0:T(8,128)}), f32[128,8,256]{2,1,0:T(8,128)S(1)}, u32[]{:S(2)}, u32[]{:S(2)}) async-start(f32[128,8,256]{2,1,0:T(8,128)} %code_sums.1), calls=%async_computation.1 | async-start | bytes 2097152 | tf_op jit(solution)/shard_map/all_to_all | solution.py:206
  79.9 19.0 %convert_reduce_fusion = f32[32,256]{1,0:T(8,128)S(1)} fusion(s32[32,3072]{1,0:T(8,128)S(1)} %copy-done.1), kind=kLoop, calls=%fused_computation | loop fusion | flops 75489280 | bytes 425984 | tf_op jit(solution)/shard_map/reduce_sum | solution.py:200
  98.9 123.9 %psum.7 = f32[32,256]{1,0:T(8,128)S(1)} all-reduce(f32[32,256]{1,0:T(8,128)S(1)} %convert_reduce_fusion), channel_id=1, replica_groups=mesh['x'=4,'z'=4,'core'=2,'y'=4] {'x','z','core'}, use_global_device_ids=true, to_apply=%region_2.0 | all-reduce | flops 8192 | bytes 65536 | tf_op jit(solution)/shard_map/psum | solution.py:203
  222.8 0.1 reduce_sum.36
  222.9 0.1 broadcast_in_dim.7
  223.0 28.9 %all_to_all.25.tab_ref = f32[128,8,256]{2,1,0:T(8,128)} all-to-all(f32[128,8,256]{2,1,0:T(8,128)S(1)} %broadcast_in_dim.7), channel_id=1, replica_groups=mesh['x'=4,'z'=4,'core'=2,'y'=4] {'y','x','z','core'}, dimensions={0} | all-to-all | bytes 2097152 | tf_op jit(solution)/shard_map/all_to_all | solution.py:40
  251.9 30.5 %cross_part.1 = f32[1024,256]{1,0:T(8,128)} custom-call(s32[1]{0:T(128)} %bitcast.y_ref, f32[3072,256]{1,0:T(8,128)} %pts_ref.3, f32[128,8,256]{2,1,0:T(8,128)} %all_to_all.25.tab_ref, s32[32,3072]{1,0:T(8,128)} %c0.3, s32[32,3072]{1,0:T(8,128)} %copy-done.4, s32[32,3072]{1,0:T(8,128)} %copy-done.3, s32[32,3072]{1,0:T(8,128)} %copy-done.2), custom_call_target="tpu_custom_call" | custom-call | tf_op jit(solution)/shard_map/cross_part/pallas_call | solution.py:173
  282.4 21.8 %all_to_all.26 = f32[32,32,256]{2,1,0:T(8,128)S(1)} all-to-all(f32[32,32,256]{2,1,0:T(8,128)} %bitcast.53), channel_id=1, replica_groups=mesh['x'=4,'z'=4,'core'=2,'y'=4] {'x','z','core'}, dimensions={0} | all-to-all | bytes 2097152 | tf_op jit(solution)/shard_map/all_to_all | solution.py:216
  304.2 0.1 reduce_sum.38
  304.2 2.5 broadcast_in_dim.8
  306.7 5.4 %all-to-all-start.4 = ((f32[128,32,256]{2,1,0:T(8,128)}), f32[128,32,256]{2,1,0:T(8,128)}, u32[]{:S(2)}, u32[]{:S(2)}) async-start(f32[128,32,256]{2,1,0:T(8,128)} %broadcast_in_dim.8), calls=%async_computation.4 | async-start | bytes 8388608 | tf_op jit(solution)/shard_map/all_to_all | solution.py:40
  312.1 1.0 dynamic-slice_bitcast_fusion
  313.1 0.4 copy.13
  313.5 1.0 copy.14
  314.5 50.6 %all-to-all-done.4 = f32[128,32,256]{2,1,0:T(8,128)} async-done(((f32[128,32,256]{2,1,0:T(8,128)}), f32[128,32,256]{2,1,0:T(8,128)}, u32[]{:S(2)}, u32[]{:S(2)}) %all-to-all-start.4) | async-done | bytes 4194336 | tf_op jit(solution)/shard_map/all_to_all | solution.py:40
  365.2 3.9 multiply_reduce_fusion
  369.7 2.7 multiply_divide_fusion
  372.4 3.6 copy.11
  376.0 1.0 copy.16
  377.0 1.9 copy-done
  379.0 8.3 %fusion.3 = f32[1024,1024]{1,0:T(8,128)} fusion(f32[1024,1024]{1,0:T(8,128)S(1)} %bitcast.44), kind=kOutput, calls=%fused_computation.17 | convolution fusion | flops 6442450944 | bytes 8388608 | tf_op jit(solution)/shard_map/dot_general | solution.py:222
  387.3 5.4 %copy.12 = f32[1024,1024]{0,1:T(8,128)} copy(f32[1024,1024]{1,0:T(8,128)} %bitcast.45) | data formatting | bytes 8388608 | tf_op jit(solution)/shard_map/div | solution.py:220
  392.7 10.7 %multiply_subtract_fusion.4 = f32[1024,1024]{0,1:T(8,128)S(1)} fusion(f32[1024,1024]{0,1:T(8,128)} %copy.12, f32[1024,1024]{1,0:T(8,128)} %fusion.3, f32[1024,1024]{1,0:T(8,128)} %bitcast.46), kind=kOutput, calls=%fused_computation.6 | convolution fusion | flops 6445596672 | bytes 16777216 | tf_op jit(solution)/shard_map/dot_general | solution.py:223
  403.3 7.4 %fusion.4 = f32[1024,1024]{1,0:T(8,128)S(1)} fusion(f32[1024,1024]{0,1:T(8,128)S(1)} %multiply_subtract_fusion.4), kind=kOutput, calls=%fused_computation.18 | convolution fusion | flops 6442450944 | bytes 8388608 | tf_op jit(solution)/shard_map/dot_general | solution.py:222
  410.7 7.5 %multiply_subtract_fusion.3 = f32[1024,1024]{0,1:T(8,128)S(1)} fusion(f32[1024,1024]{0,1:T(8,128)S(1)} %multiply_subtract_fusion.4, f32[1024,1024]{1,0:T(8,128)S(1)} %fusion.4), kind=kOutput, calls=%fused_computation.5 | convolution fusion | flops 6445596672 | bytes 12582912 | tf_op jit(solution)/shard_map/dot_general | solution.py:223
  418.2 7.4 %fusion.5 = f32[1024,1024]{1,0:T(8,128)S(1)} fusion(f32[1024,1024]{0,1:T(8,128)S(1)} %multiply_subtract_fusion.3), kind=kOutput, calls=%fused_computation.19 | convolution fusion | flops 6442450944 | bytes 8388608 | tf_op jit(solution)/shard_map/dot_general | solution.py:222
  425.5 7.6 %multiply_subtract_fusion.2 = f32[1024,1024]{0,1:T(8,128)S(1)} fusion(f32[1024,1024]{0,1:T(8,128)S(1)} %multiply_subtract_fusion.3, f32[1024,1024]{1,0:T(8,128)S(1)} %fusion.5), kind=kOutput, calls=%fused_computation.4 | convolution fusion | flops 6445596672 | bytes 12582912 | tf_op jit(solution)/shard_map/dot_general | solution.py:223
  433.2 7.4 %fusion.6 = f32[1024,1024]{1,0:T(8,128)S(1)} fusion(f32[1024,1024]{0,1:T(8,128)S(1)} %multiply_subtract_fusion.2), kind=kOutput, calls=%fused_computation.20 | convolution fusion | flops 6442450944 | bytes 8388608 | tf_op jit(solution)/shard_map/dot_general | solution.py:222
  440.5 7.4 %multiply_subtract_fusion.1 = f32[1024,1024]{0,1:T(8,128)S(1)} fusion(f32[1024,1024]{0,1:T(8,128)S(1)} %multiply_subtract_fusion.2, f32[1024,1024]{1,0:T(8,128)S(1)} %fusion.6), kind=kOutput, calls=%fused_computation.3 | convolution fusion | flops 6445596672 | bytes 12582912 | tf_op jit(solution)/shard_map/dot_general | solution.py:223
  448.0 7.6 %fusion.7 = f32[1024,1024]{1,0:T(8,128)S(1)} fusion(f32[1024,1024]{0,1:T(8,128)S(1)} %multiply_subtract_fusion.1), kind=kOutput, calls=%fused_computation.21 | convolution fusion | flops 6442450944 | bytes 8388608 | tf_op jit(solution)/shard_map/dot_general | solution.py:222
  455.6 7.2 %multiply_subtract_fusion = f32[1024,1024]{0,1:T(8,128)S(1)} fusion(f32[1024,1024]{0,1:T(8,128)S(1)} %multiply_subtract_fusion.1, f32[1024,1024]{1,0:T(8,128)S(1)} %fusion.7), kind=kOutput, calls=%fused_computation.2 | convolution fusion | flops 6445596672 | bytes 12582912 | tf_op jit(solution)/shard_map/dot_general | solution.py:223
  462.8 7.6 %fusion.8 = f32[1024,1024]{1,0:T(8,128)S(1)} fusion(f32[1024,1024]{0,1:T(8,128)S(1)} %multiply_subtract_fusion), kind=kOutput, calls=%fused_computation.22 | convolution fusion | flops 6442450944 | bytes 8388608 | tf_op jit(solution)/shard_map/dot_general | solution.py:222
  470.4 6.8 %fusion.9 = f32[1024,1024]{0,1:T(8,128)S(1)} fusion(f32[1024,1024]{1,0:T(8,128)S(1)} %fusion.8, f32[1024,1024]{0,1:T(8,128)S(1)} %multiply_subtract_fusion), kind=kOutput, calls=%fused_computation.23 | convolution fusion | flops 6442450944 | bytes 12582912 | tf_op jit(solution)/shard_map/dot_general | solution.py:223
  477.3 0.6 fusion.2
  (12 shorter events, 0.0 us)
Async XLA Ops:
  0.6 1.4 collective-permute-start
  3.2 34.9 %all-to-all-start = ((f32[32,32,256]{2,1,0:T(8,128)}), f32[32,32,256]{2,1,0:T(8,128)S(1)}, u32[]{:S(2)}, u32[]{:S(2)}) async-start(f32[32,32,256]{2,1,0:T(8,128)} %broadcast_in_dim.6), calls=%async_computation | async-start | bytes 2097152 | tf_op jit(solution)/shard_map/all_to_all | solution.py:40
  21.1 18.8 %collective-permute-start.3 = (s32[32,3072]{1,0:T(8,128)}, s32[32,3072]{1,0:T(8,128)S(1)}, u32[]{:S(2)}, u32[]{:S(2)}) collective-permute-start(s32[32,3072]{1,0:T(8,128)} %c0.3), channel_id=1, source_target_pairs={{0,3},{1,0},{2,1},{3,2},{4,7},{5,4},{6,5},{7,6},{8,11},{9,8},{10,9... | collective-permute-start | bytes 1179656 | tf_op jit(solution)/shard_map/ppermute | solution.py:193
  22.4 17.5 %collective-permute-start.2 = (s32[32,3072]{1,0:T(8,128)}, s32[32,3072]{1,0:T(8,128)S(1)}, u32[]{:S(2)}, u32[]{:S(2)}) collective-permute-start(s32[32,3072]{1,0:T(8,128)} %c0.3), channel_id=1, source_target_pairs={{0,2},{1,3},{2,0},{3,1},{4,6},{5,7},{6,4},{7,5},{8,10},{9,11},{10,... | collective-permute-start | bytes 1179656 | tf_op jit(solution)/shard_map/ppermute | solution.py:193
  24.0 19.6 %collective-permute-start.1 = (s32[32,3072]{1,0:T(8,128)}, s32[32,3072]{1,0:T(8,128)S(1)}, u32[]{:S(2)}, u32[]{:S(2)}) collective-permute-start(s32[32,3072]{1,0:T(8,128)} %c0.3), channel_id=1, source_target_pairs={{0,1},{1,2},{2,3},{3,0},{4,5},{5,6},{6,7},{7,4},{8,9},{9,10},{10,1... | collective-permute-start | bytes 1179656 | tf_op jit(solution)/shard_map/ppermute | solution.py:193
  39.9 3.7 copy-start.2
  39.9 3.7 copy-start.3
  43.5 0.8 copy-start.4
  44.3 35.6 %copy-start.1 = (s32[32,3072]{1,0:T(8,128)S(1)}, s32[32,3072]{1,0:T(8,128)}, u32[]{:S(2)}) copy-start(s32[32,3072]{1,0:T(8,128)} %c0.3) | copy-start | bytes 1179652
  71.7 151.0 %all-to-all-start.1 = ((f32[128,8,256]{2,1,0:T(8,128)}), f32[128,8,256]{2,1,0:T(8,128)S(1)}, u32[]{:S(2)}, u32[]{:S(2)}) async-start(f32[128,8,256]{2,1,0:T(8,128)} %code_sums.1), calls=%async_computation.1 | async-start | bytes 2097152 | tf_op jit(solution)/shard_map/all_to_all | solution.py:206
  306.7 58.4 %all-to-all-start.4 = ((f32[128,32,256]{2,1,0:T(8,128)}), f32[128,32,256]{2,1,0:T(8,128)}, u32[]{:S(2)}, u32[]{:S(2)}) async-start(f32[128,32,256]{2,1,0:T(8,128)} %broadcast_in_dim.8), calls=%async_computation.4 | async-start | bytes 8388608 | tf_op jit(solution)/shard_map/all_to_all | solution.py:40
  377.0 1.9 copy-start

commit v2 on v1

v2 whole, which is shorter than its diff:
```python
import jax
import jax.numpy as jnp
from jax import lax
from jax.experimental import pallas as pl
from jax.experimental.pallas import tpu as pltpu
from jax.sharding import Mesh, PartitionSpec as P

D = 1024
M = 128
K = 256
NS_ITERS = 6
SUB = 8
ROWS = ("x", "z", "core")
CHIPS = ("y", "x", "z")
BF16 = jnp.bfloat16
F32 = jnp.float32
NN = (((1,), (0,)), ((), ()))
NT = (((1,), (1,)), ((), ()))
VMEM = pl.BlockSpec(memory_space=pltpu.VMEM)
SMEM = pl.BlockSpec(memory_space=pltpu.SMEM)
PARAMS = pltpu.CompilerParams(vmem_limit_bytes=56 * 1024 * 1024)
PAYLOAD = K + 128


def split(value):
    high = value.astype(BF16)
    return high, (value - high.astype(F32)).astype(BF16)


def mxu(left, right, dims):
    return lax.dot_general(left, right, dims, preferred_element_type=F32)


def dot3(left_high, left_low, right_high, right_low, dims):
    return (
        mxu(left_high, right_high, dims)
        + mxu(left_high, right_low, dims)
        + mxu(left_low, right_high, dims)
    )


def spread_to(value, axes, count):
    copies = jnp.broadcast_to(value[None], (count,) + value.shape)
    return lax.all_to_all(copies, axes, 0, 0, tiled=True)


def swap_core(value):
    return lax.ppermute(value, "core", [(0, 1), (1, 0)])


def at8(index):
    return pl.ds(pl.multiple_of(index * 8, 8), 8)


def place_codes(where, y, c0, c1, c2, c3):
    for i, codes_ref in enumerate((c0, c1, c2, c3)):
        block = lax.rem(y + 4 - i, 4)
        where[pl.ds(pl.multiple_of(block * 32, 32), 32), :] = codes_ref[...]


def sums_kernel(
    place_ref, pts_ref, mine_ref, other_ref, c0, c1, c2, c3,
    keep_ref, give_ref, codes_ref, panel_ref, rotated_ref, ph_ref, pl_ref,
):
    count = pts_ref.shape[0]
    y, core = place_ref[0], place_ref[1]
    place_codes(codes_ref, y, c0, c1, c2, c3)
    ph, plo = split(pts_ref[...])
    ph_ref[...] = ph
    pl_ref[...] = plo
    for a in range(4):
        for z in range(4):
            columns = slice(a * 256, a * 256 + 256)
            first = pl.multiple_of(z * 64 + core * 32, 32)
            second = pl.multiple_of(z * 64 + (1 - core) * 32, 32)
            panel_ref[pl.ds(first, 32), columns] = mine_ref[a * 4 + z]
            panel_ref[pl.ds(second, 32), columns] = other_ref[a * 4 + z]

    def rotate(j, carry):
        panel = panel_ref[:, pl.ds(pl.multiple_of(j * 256, 256), 256)].T
        rh, rl = split(panel)
        part = dot3(rh, rl, ph_ref[...], pl_ref[...], NT)
        rotated_ref[pl.ds(j * 32, 32)] = part.reshape(32, SUB, count)
        return carry

    lax.fori_loop(0, D // 256, rotate, 0)

    step = 512
    rows16 = lax.broadcasted_iota(jnp.int32, (16, step), 0).astype(F32)
    marks = [(rows16 + 16.0 * t).astype(BF16) for t in range(4)]
    tops = [jnp.full((16, step), t, BF16) for t in range(4)]
    one = jnp.ones((16, step), BF16)
    zero = jnp.zeros((16, step), BF16)
    lane = lax.broadcasted_iota(jnp.int32, (SUB, 128), 1)

    def pick(even, odd, mm):
        if mm % 2 == 0:
            odd = pltpu.roll(odd, 64, axis=1)
        else:
            even = pltpu.roll(even, 64, axis=1)
        return jnp.where(lane < 64, even, odd)

    def group(eight, quad):
        total = jnp.zeros((288, 256), F32)
        for n in range(0, count, step):
            lefts, rights = [], []
            rows = codes_ref[at8(eight), n : n + step]
            for mm in range(4):
                row = rows[quad * 4 + mm : quad * 4 + mm + 1]
                low = jnp.broadcast_to((row & 63).astype(F32), (16, step)).astype(BF16)
                top = jnp.broadcast_to((row >> 6).astype(F32), (16, step)).astype(BF16)
                value = rotated_ref[eight * 8 + quad * 4 + mm, :, n : n + step]
                high = value.astype(BF16).astype(F32)
                both = jnp.concatenate([high, value - high], axis=0).astype(BF16)
                for t in range(4):
                    lefts.append(jnp.where(top == tops[t], both, zero))
                    rights.append(jnp.where(low == marks[t], one, zero))
            tall = (rows >> 6).astype(F32)
            tall = jnp.concatenate([tall, tall], axis=0).astype(BF16)
            for t in range(2):
                pattern = jnp.where(rows16 < 8, 2.0 * t, 2.0 * t + 1.0).astype(BF16)
                lefts.append(jnp.where(tall == pattern, one, zero))
            total += mxu(jnp.concatenate(lefts, axis=0), jnp.concatenate(rights, axis=0), NT)
        found = []
        for mm in range(4):
            columns = slice((mm // 2) * 128, (mm // 2) * 128 + 128)
            slab = total[mm * 64 : mm * 64 + 64, columns]
            parts = [slab[t * 16 : t * 16 + 8] + slab[t * 16 + 8 : t * 16 + 16] for t in range(4)]
            tally = [total[256 + t * 8 : 264 + t * 8, columns] for t in range(4)]
            halves = [pick(parts[2 * h], parts[2 * h + 1], mm) for h in range(2)]
            r = quad * 4 + mm
            ticks = [pick(tally[2 * h], tally[2 * h + 1], mm)[r : r + 1] for h in range(2)]
            ticks = jnp.concatenate(ticks + [jnp.zeros((6, 128), F32)], axis=0)
            found.append(jnp.concatenate(halves + [ticks], axis=1))
        for h in range(2):
            even, odd = found[2 * h], found[2 * h + 1]
            q = eight * 4 + quad * 2 + h
            keep_ref[q] = jnp.where(core == 0, even, odd)
            give_ref[q] = jnp.where(core == 0, odd, even)

    def eight_rows(eight, carry):
        group(eight, 0)
        group(eight, 1)
        return carry

    lax.fori_loop(0, M // 8, eight_rows, 0)


def code_sums(place, points, mine, other, codes):
    count = points.shape[0]
    half = jax.ShapeDtypeStruct((M // 2, SUB, PAYLOAD), F32)
    return pl.pallas_call(
        sums_kernel,
        out_shape=(half, half),
        in_specs=[SMEM] + [VMEM] * 7,
        out_specs=(VMEM, VMEM),
        scratch_shapes=[
            pltpu.VMEM((M, count), jnp.int32),
            pltpu.VMEM((256, D), F32),
            pltpu.VMEM((M, SUB, count), F32),
            pltpu.VMEM((count, 256), BF16),
            pltpu.VMEM((count, 256), BF16),
        ],
        compiler_params=PARAMS,
        name="code_sums",
    )(place, points, mine, other, *codes)


def cross_kernel(
    place_ref, pts_ref, mine_ref, other_ref, c0, c1, c2, c3,
    keep_ref, give_ref, codes_ref, tab_ref, ah_ref, al_ref, ph_ref, pl_ref,
):
    count = pts_ref.shape[0]
    y, core = place_ref[0], place_ref[1]
    place_codes(codes_ref, y, c0, c1, c2, c3)
    tab_ref[core] = mine_ref[...]
    tab_ref[1 - core] = other_ref[...]
    ph, plo = split(pts_ref[...])
    ph_ref[...] = ph
    pl_ref[...] = plo
    wide = 1024

    def look_up(block, eight):
        for n in range(0, count, wide):
            rows = codes_ref[at8(block * 4 + eight), n : n + wide]
            for two in range(4):
                both = []
                for mm in range(2):
                    index = jnp.broadcast_to(rows[two * 2 + mm : two * 2 + mm + 1], (SUB, wide))
                    table = tab_ref[mm, block * 16 + eight * 4 + two]
                    found = []
                    for k in range(0, wide, 128):
                        here = index[:, k : k + 128]
                        inner = here & 127
                        first = jnp.take_along_axis(
                            table[:, :128], inner, axis=1, mode="promise_in_bounds"
                        )
                        second = jnp.take_along_axis(
                            table[:, 128:], inner, axis=1, mode="promise_in_bounds"
                        )
                        found.append(jnp.where(here < 128, first, second))
                    both.append(jnp.concatenate(found, axis=1))
                high, low = split(jnp.concatenate(both, axis=0))
                place = pl.ds(pl.multiple_of(eight * 64 + two * 16, 16), 16)
                ah_ref[place, n : n + wide] = high
                al_ref[place, n : n + wide] = low

    def one_block(block, carry):
        def eight_rows(eight, inside):
            look_up(block, eight)
            return inside

        lax.fori_loop(0, 4, eight_rows, 0)
        part = dot3(ah_ref[...], al_ref[...], ph_ref[...], pl_ref[...], NN)
        for h in range(4):
            even = part[h * 64 : h * 64 + 32]
            odd = part[h * 64 + 32 : h * 64 + 64]
            keep_ref[block * 4 + h] = jnp.where(core == 0, even, odd)
            give_ref[block * 4 + h] = jnp.where(core == 0, odd, even)
        return carry

    lax.fori_loop(0, 4, one_block, 0)


def cross_part(place, points, mine, other, codes):
    count = points.shape[0]
    half = jax.ShapeDtypeStruct((16, 32, 256), F32)
    return pl.pallas_call(
        cross_kernel,
        out_shape=(half, half),
        in_specs=[SMEM] + [VMEM] * 7,
        out_specs=(VMEM, VMEM),
        scratch_shapes=[
            pltpu.VMEM((M, count), jnp.int32),
            pltpu.VMEM((2, M // 2, SUB, K), F32),
            pltpu.VMEM((256, count), BF16),
            pltpu.VMEM((256, count), BF16),
            pltpu.VMEM((count, 256), BF16),
            pltpu.VMEM((count, 256), BF16),
        ],
        compiler_params=PARAMS,
        name="cross_part",
    )(place, points, mine, other, *codes)


def iterate_kernel(place_ref, mine_ref, other_ref, out_ref, now_ref, hl_ref, gh_ref, gl_ref, tail_ref):
    y, column = place_ref[0], place_ref[2]
    total = jnp.zeros((1, 256), F32)
    for half, source in enumerate((mine_ref, other_ref)):
        for block in range(4):
            part = source[block * 16 : block * 16 + 16].reshape(512, 256)
            total += jnp.sum(part * part, axis=0, keepdims=True)
    scale = 1.7 / jnp.sqrt(jnp.sum(total, axis=1, keepdims=True) + 1e-06)
    for half, source in enumerate((mine_ref, other_ref)):
        for block in range(4):
            rows, columns = slice(half * 512, half * 512 + 512), slice(block * 256, block * 256 + 256)
            part = source[block * 16 : block * 16 + 16].reshape(512, 256) * scale
            now_ref[rows, columns] = part
            high, low = split(part)
            hl_ref[0, 0, rows, columns] = high
            hl_ref[0, 1, rows, columns] = low

    def step(k, carry):
        old, new = lax.rem(k, 2), 1 - lax.rem(k, 2)
        high_ref, low_ref = hl_ref.at[old, 0], hl_ref.at[old, 1]
        for j in range(4):
            strip, below = slice(j * 256, j * 256 + 256), slice(j * 256, D)
            gram = dot3(high_ref[below], low_ref[below], high_ref[strip], low_ref[strip], NT)
            high, low = split(gram)
            gh_ref[below, strip] = high
            gl_ref[below, strip] = low
            if j < 3:
                high, low = split(gram[256:].T)
                gh_ref[strip, j * 256 + 256 : D] = high
                gl_ref[strip, j * 256 + 256 : D] = low
        for j in range(4):
            strip = slice(j * 256, j * 256 + 256)
            moved = dot3(gh_ref[...], gl_ref[...], high_ref[:, strip], low_ref[:, strip], NN)
            value = 1.5 * now_ref[:, strip] - 0.5 * moved
            now_ref[:, strip] = value
            high, low = split(value)
            hl_ref[new, 0, :, strip] = high
            hl_ref[new, 1, :, strip] = low
        return carry

    lax.fori_loop(0, NS_ITERS - 1, step, 0)
    last = (NS_ITERS - 1) % 2
    high_ref, low_ref = hl_ref.at[last, 0], hl_ref.at[last, 1]
    columns = pl.ds(pl.multiple_of(column * 128, 128), 128)
    for half in range(2):
        rows = pl.ds(pl.multiple_of(half * 512 + y * 128, 128), 128)
        here = slice(half * 128, half * 128 + 128)
        tail_ref[0, here] = high_ref[rows]
        tail_ref[1, here] = low_ref[rows]
    gram = dot3(tail_ref[0], tail_ref[1], high_ref[...], low_ref[...], NT)
    high, low = split(gram)
    moved = dot3(high, low, high_ref[:, columns], low_ref[:, columns], NN)
    for half in range(2):
        rows = pl.ds(pl.multiple_of(half * 512 + y * 128, 128), 128)
        here = slice(half * 128, half * 128 + 128)
        out_ref[here, :] = (1.5 * now_ref[rows, columns] - 0.5 * moved[here]) * D**0.5


def newton_schulz(place, mine, other):
    return pl.pallas_call(
        iterate_kernel,
        out_shape=jax.ShapeDtypeStruct((256, 128), F32),
        in_specs=[SMEM, VMEM, VMEM],
        out_specs=VMEM,
        scratch_shapes=[
            pltpu.VMEM((D, D), F32),
            pltpu.VMEM((2, 2, D, D), BF16),
            pltpu.VMEM((D, D), BF16),
            pltpu.VMEM((D, D), BF16),
            pltpu.VMEM((2, 256, D), BF16),
        ],
        compiler_params=PARAMS,
        name="newton_schulz",
    )(place, mine, other)


def shards(points, codes, rotation):
    y, core = lax.axis_index("y"), lax.axis_index("core")
    own_row = lax.axis_index(ROWS)
    place = jnp.stack([y, core, own_row // 4]).astype(jnp.int32)
    all_codes = [codes] + [
        lax.ppermute(codes, "y", [(s, (s + i) % 4) for s in range(4)]) for i in (1, 2, 3)
    ]
    swapped = lax.ppermute(
        rotation, ("x", "y"), [(a * 4 + b, b * 4 + a) for a in range(4) for b in range(4)]
    )
    pieces = spread_to(swapped, ("x", "z"), 16)
    keep, give = code_sums(place, points, pieces, swap_core(pieces), all_codes)

    sums = keep + swap_core(give)
    sums = jnp.sum(lax.all_to_all(sums, CHIPS, 0, 0, tiled=True), axis=0)
    counts = 0.25 * sums[:2, K:].reshape(1, K)
    centers = spread_to(sums[:, :K] / counts, CHIPS, 64)
    others = swap_core(centers)

    keep, give = cross_part(place, points, centers, others, all_codes)
    block = keep + swap_core(give)
    block = jnp.sum(lax.all_to_all(block, ("x", "z"), 0, 0, tiled=True), axis=0)
    whole = spread_to(block, CHIPS, 64)
    result = newton_schulz(place, whole, swap_core(whole))

    result = lax.dynamic_slice_in_dim(result, (own_row % 4) * 32, 32, axis=1)
    result = result.reshape(2, 4, 32, 32)
    result = jnp.where(core == 0, result, result[::-1])
    rotated = result.transpose(3, 1, 0, 2).reshape(32, 256)

    ours = lax.dynamic_slice_in_dim(centers, y * 16, 16, axis=0)
    theirs = lax.dynamic_slice_in_dim(others, y * 16, 16, axis=0)
    first, second = jnp.where(core == 0, ours, theirs), jnp.where(core == 0, theirs, ours)
    centroids = jnp.stack([first, second], axis=1).transpose(0, 1, 3, 2).reshape(32, K * SUB)
    return (rotated, centroids)


def solution(mesh):
    grid = Mesh(mesh.devices.reshape(4, 4, 2, 4), ("x", "z", "core", "y"))
    in_specs = (P(ROWS, "y"), P("y", ROWS), P(ROWS, "y"))
    out_specs = (P(ROWS, "y"), P("y", None))
    return jax.shard_map(shards, mesh=grid, in_specs=in_specs, out_specs=out_specs, check_vma=False)
```

time: 486 us -> 281 us (0.58); the launches traced: 478 us -> 280 us
  matrix products: 92.9 us -> 0 us
  blocking collectives: 175 us -> 106 us
  Pallas kernels: 57.9 us -> 118 us
  waiting for transfers between devices: 68.3 us -> 24.3 us
  other arithmetic: 26.4 us -> 4.07 us
  starting transfers between devices: 35.7 us -> 15.2 us
  local copies, waits for them, and re-layouts: 20.6 us -> 11.9 us
    psum x1 -> x0, blocking collectives: 124 us -> none  [shards(): counts = lax.psum(local_counts, ROWS)]
    dot_general x12 -> x0, matrix products: 92.9 us -> none  [the longest x6 47.3 us: shards(): lax.dot_general(gram, iterate, NN, precision=lax.Precision.HIGH, preferre...]
    all_to_all x3 -> x0, waiting for transfers between devices: 64.6 us -> none  [the longest x2 64.6 us: spread_to(): return lax.all_to_all(copies, axes, 0, 0, tiled=True)]
    pallas_call x2 -> x3, Pallas kernels: 57.9 us -> 118 us  [the longest x1 62.7 us: newton_schulz(): pl.pallas_call(iterate_kernel, out_shape=jax.ShapeDtypeStruct((256, 128),...]
    all_to_all x1 -> x3, blocking collectives: 28.9 us -> 72.7 us  [spread_to(): return lax.all_to_all(copies, axes, 0, 0, tiled=True)]
    all_to_all x3 -> x0, starting transfers between devices: 31.4 us -> none  [the longest x2 23.3 us: spread_to(): return lax.all_to_all(copies, axes, 0, 0, tiled=True)]
    reduce_sum x4 -> x2, other arithmetic: 23 us -> 0.12 us  [the longest x1 0.08 us: shards(): sums = jnp.sum(lax.all_to_all(sums, CHIPS, 0, 0, tiled=True), axis=0)]
    ppermute x3, waiting for transfers between devices: 3.66 us -> 18.9 us  [shards(): lax.ppermute(codes, 'y', [(s, (s + i) % 4) for s in range(4)])]
  transfers between devices with their start and end apart: 7 -> 9, of which waited for: 3 -> 6; matrix products, arithmetic and copies ran while one was open for 5% -> 3% of each run, Pallas kernels for 0% -> 0%
where the time goes in v2:
time: 281 us; the launch traced here: 280 us
  Pallas kernels  118 us (42%)
  blocking collectives  106 us (38%)
  waiting for transfers between devices  24.3 us (9%)
  starting transfers between devices  15.2 us (5%)
  local copies, waits for them, and re-layouts  11.9 us (4%)
  other arithmetic  4.07 us (1%)
    all_to_all x3, blocking collectives, spread_to(): return lax.all_to_all(copies, axes, 0, 0, tiled=True)  72.7 us
    pallas_call x1, Pallas kernels, newton_schulz(): pl.pallas_call(iterate_kernel, out_shape=jax.ShapeDtypeStruct((256, 128),...  62.7 us
    pallas_call x1, Pallas kernels, code_sums(): pl.pallas_call(sums_kernel, out_shape=(half, half), in_specs=[SMEM] + [VM...  29.6 us
    pallas_call x1, Pallas kernels, cross_part(): pl.pallas_call(cross_kernel, out_shape=(half, half), in_specs=[SMEM] + [V...  26 us
    all_to_all x1, blocking collectives, shards(): sums = jnp.sum(lax.all_to_all(sums, CHIPS, 0, 0, tiled=True), axis=0)  19.9 us
    ppermute x3, waiting for transfers between devices, shards(): lax.ppermute(codes, 'y', [(s, (s + i) % 4) for s in range(4)])  18.9 us
    all_to_all x1, blocking collectives, shards(): block = jnp.sum(lax.all_to_all(block, ('x', 'z'), 0, 0, tiled=True), axis=0)  13.1 us
    ppermute x5, starting transfers between devices, swap_core(): return lax.ppermute(value, 'core', [(0, 1), (1, 0)])  10.9 us
  transfers between devices with their start and end apart: 9, of which 6 were waited for; matrix products, arithmetic and copies ran while one was open for 3% of the time, Pallas kernels for 0%

profile of v2, /device:TPU:1, one launch (start us, length us, event | category | flops | bytes accessed | tf_op | source)
XLA Modules:
  0.0 280.2 jit_solution(6883405423789789277)
XLA Ops:
  0.6 1.4 collective-permute-start
  2.0 0.0 collective-permute-done
  2.1 24.9 %all_to_all.25.mine_ref = f32[16,32,256]{2,1,0:T(8,128)S(1)} all-to-all(f32[16,32,256]{2,1,0:T(8,128)S(1)} %broadcast_in_dim.6), channel_id=1, replica_groups=mesh['x'=4,'z'=4,'core'=2,'y'=4] {'x','z'}, dimensions={0} | all-to-all | bytes 1048576 | tf_op jit(solution)/shard_map/all_to_all | solution.py:44
  27.0 0.0 copy-start.2
  27.0 3.2 %collective-permute-start.1 = (f32[16,32,256]{2,1,0:T(8,128)S(1)}, f32[16,32,256]{2,1,0:T(8,128)S(1)}, u32[]{:S(2)}, u32[]{:S(2)}) collective-permute-start(f32[16,32,256]{2,1,0:T(8,128)S(1)} %all_to_all.25.mine_ref), channel_id=1, source_target_pairs={{0,4},{4,0},{1,5},{5,1},{2,6},{6,2},{3,7},{7,3},{8,12},{12,8},{9,1... | collective-permute-start | bytes 1572872 | tf_op jit(solution)/shard_map/ppermute | solution.py:48
  30.2 1.1 collective-permute-start.4
  31.3 1.7 collective-permute-start.3
  33.1 0.0 collective-permute-start.2
  33.1 0.6 pad_add_fusion.place_ref
  33.6 7.5 %collective-permute-done.4.c3 = s32[32,3072]{1,0:T(8,128)S(1)} collective-permute-done((s32[32,3072]{1,0:T(8,128)}, s32[32,3072]{1,0:T(8,128)S(1)}, u32[]{:S(2)}, u32[]{:S(2)}) %collective-permute-start.4) | collective-permute-done | bytes 393248 | tf_op jit(solution)/shard_map/ppermute | solution.py:327
  41.2 0.0 copy-start.3
  41.2 2.3 collective-permute-done.3.c2
  43.5 9.0 %collective-permute-done.2.c1 = s32[32,3072]{1,0:T(8,128)S(1)} collective-permute-done((s32[32,3072]{1,0:T(8,128)}, s32[32,3072]{1,0:T(8,128)S(1)}, u32[]{:S(2)}, u32[]{:S(2)}) %collective-permute-start.2) | collective-permute-done | bytes 393248 | tf_op jit(solution)/shard_map/ppermute | solution.py:327
  52.5 0.0 collective-permute-done.1.other_ref
  52.5 0.0 copy-done.2
  52.5 0.0 copy-done.3
  52.5 0.0 copy-done.4
  52.5 0.7 copy-done.5
  53.3 0.8 copy-done.7
  54.1 29.6 %code_sums.1 = (f32[64,8,384]{2,1,0:T(8,128)}, f32[64,8,384]{2,1,0:T(8,128)}) custom-call(s32[3]{0:T(128)} %pad_add_fusion.place_ref, f32[3072,256]{1,0:T(8,128)} %pts_ref.3, f32[16,32,256]{2,1,0:T(8,128)} %copy-done.2, f32[16,32,256]{2,1,0:T(8,128)} %copy-done.7, s32[32,3072]{1,0:T(8,128)} %c0.3, s32[32,3072]{1,0:T(8,128)} %copy-done.5, ...), custom_call_target="tpu_custom_call" | custom-call | tf_op jit(solution)/shard_map/code_sums/pallas_call | solution.py:152
  83.7 0.5 collective-permute-start.5
  84.2 2.1 collective-permute-done.5
  86.4 1.2 add.26
  87.6 19.9 %all_to_all.26 = f32[64,8,384]{2,1,0:T(8,128)S(1)} all-to-all(f32[64,8,384]{2,1,0:T(8,128)S(1)} %add.26), channel_id=1, replica_groups=mesh['x'=4,'z'=4,'core'=2,'y'=4] {'y','x','z'}, dimensions={0} | all-to-all | bytes 1572864 | tf_op jit(solution)/shard_map/all_to_all | solution.py:336
  107.5 0.1 reduce_sum.18
  107.6 15.8 %all_to_all.27.mine_ref = f32[64,8,256]{2,1,0:T(8,128)S(1)} all-to-all(f32[64,8,256]{2,1,0:T(8,128)S(1)} %broadcast_in_dim.7), channel_id=1, replica_groups=mesh['x'=4,'z'=4,'core'=2,'y'=4] {'y','x','z'}, dimensions={0} | all-to-all | bytes 1048576 | tf_op jit(solution)/shard_map/all_to_all | solution.py:44
  123.4 3.1 %collective-permute-start.6 = (f32[64,8,256]{2,1,0:T(8,128)S(1)}, f32[64,8,256]{2,1,0:T(8,128)S(1)}, u32[]{:S(2)}, u32[]{:S(2)}) collective-permute-start(f32[64,8,256]{2,1,0:T(8,128)S(1)} %all_to_all.27.mine_ref), channel_id=1, source_target_pairs={{0,4},{4,0},{1,5},{5,1},{2,6},{6,2},{3,7},{7,3},{8,12},{12,8},{9,1... | collective-permute-start | bytes 1572872 | tf_op jit(solution)/shard_map/ppermute | solution.py:48
  126.5 1.5 collective-permute-done.6.other_ref
  128.1 0.0 copy-done.1
  128.1 0.8 copy-done.6
  128.9 26.0 %cross_part.1 = (f32[16,32,256]{2,1,0:T(8,128)}, f32[16,32,256]{2,1,0:T(8,128)}) custom-call(s32[3]{0:T(128)} %pad_add_fusion.place_ref, f32[3072,256]{1,0:T(8,128)} %pts_ref.3, f32[64,8,256]{2,1,0:T(8,128)} %copy-done.1, f32[64,8,256]{2,1,0:T(8,128)} %copy-done.6, s32[32,3072]{1,0:T(8,128)} %c0.3, s32[32,3072]{1,0:T(8,128)} %copy-done.5, ...), custom_call_target="tpu_custom_call" | custom-call | tf_op jit(solution)/shard_map/cross_part/pallas_call | solution.py:228
  154.9 0.4 collective-permute-start.7
  155.3 1.7 collective-permute-done.7
  157.0 1.1 add.27
  158.2 13.1 %all_to_all.28 = f32[16,32,256]{2,1,0:T(8,128)S(1)} all-to-all(f32[16,32,256]{2,1,0:T(8,128)S(1)} %add.27), channel_id=1, replica_groups=mesh['x'=4,'z'=4,'core'=2,'y'=4] {'x','z'}, dimensions={0} | all-to-all | bytes 1048576 | tf_op jit(solution)/shard_map/all_to_all | solution.py:343
  171.3 0.2 broadcast_in_dim.8
  171.5 32.0 %all_to_all.29.mine_ref = f32[64,32,256]{2,1,0:T(8,128)S(1)} all-to-all(f32[64,32,256]{2,1,0:T(8,128)S(1)} %broadcast_in_dim.8), channel_id=1, replica_groups=mesh['x'=4,'z'=4,'core'=2,'y'=4] {'y','x','z'}, dimensions={0} | all-to-all | bytes 4194304 | tf_op jit(solution)/shard_map/all_to_all | solution.py:44
  203.5 3.7 %collective-permute-start.8 = (f32[64,32,256]{2,1,0:T(8,128)S(1)}, f32[64,32,256]{2,1,0:T(8,128)}, u32[]{:S(2)}, u32[]{:S(2)}) collective-permute-start(f32[64,32,256]{2,1,0:T(8,128)S(1)} %all_to_all.29.mine_ref), channel_id=1, source_target_pairs={{0,4},{4,0},{1,5},{5,1},{2,6},{6,2},{3,7},{7,3},{8,12},{12,8},{9,1... | collective-permute-start | bytes 6291464 | tf_op jit(solution)/shard_map/ppermute | solution.py:48
  207.2 1.0 select_bitcast_fusion.1
  208.3 2.6 copy.9
  210.9 0.0 copy-done
  210.9 4.6 %reshape.28 = f32[32,2048]{1,0:T(8,128)} reshape(f32[16,2,256,8]{3,2,1,0:T(8,128)} %copy.9) | data formatting | bytes 524288 | tf_op jit(solution)/shard_map/reshape | solution.py:355
  215.5 0.0 collective-permute-done.8.other_ref
  215.5 62.7 %newton_schulz.1 = f32[256,128]{1,0:T(8,128)} custom-call(s32[3]{0:T(128)} %pad_add_fusion.place_ref, f32[64,32,256]{2,1,0:T(8,128)} %copy-done, f32[64,32,256]{2,1,0:T(8,128)} %collective-permute-done.8.other_ref), custom_call_target="tpu_custom_call" | custom-call | tf_op jit(solution)/shard_map/newton_schulz/pallas_call | solution.py:305
  278.2 1.0 constant_dynamic-slice_fusion
  279.2 0.1 copy.10
  279.3 0.1 copy.8
  279.4 0.8 reshape.27
  (13 shorter events, 0.2 us)
Async XLA Ops:
  0.6 1.4 collective-permute-start
  27.0 25.5 %copy-start.2 = (f32[16,32,256]{2,1,0:T(8,128)}, f32[16,32,256]{2,1,0:T(8,128)S(1)}, u32[]{:S(2)}) copy-start(f32[16,32,256]{2,1,0:T(8,128)S(1)} %all_to_all.25.mine_ref) | copy-start | bytes 1572868
  27.0 25.5 %collective-permute-start.1 = (f32[16,32,256]{2,1,0:T(8,128)S(1)}, f32[16,32,256]{2,1,0:T(8,128)S(1)}, u32[]{:S(2)}, u32[]{:S(2)}) collective-permute-start(f32[16,32,256]{2,1,0:T(8,128)S(1)} %all_to_all.25.mine_ref), channel_id=1, source_target_pairs={{0,4},{4,0},{1,5},{5,1},{2,6},{6,2},{3,7},{7,3},{8,12},{12,8},{9,1... | collective-permute-start | bytes 1572872 | tf_op jit(solution)/shard_map/ppermute | solution.py:48
  30.2 11.0 %collective-permute-start.4 = (s32[32,3072]{1,0:T(8,128)}, s32[32,3072]{1,0:T(8,128)S(1)}, u32[]{:S(2)}, u32[]{:S(2)}) collective-permute-start(s32[32,3072]{1,0:T(8,128)} %c0.3), channel_id=1, source_target_pairs={{0,3},{1,0},{2,1},{3,2},{4,7},{5,4},{6,5},{7,6},{8,11},{9,8},{10,9... | collective-permute-start | bytes 1179656 | tf_op jit(solution)/shard_map/ppermute | solution.py:327
  31.3 12.2 %collective-permute-start.3 = (s32[32,3072]{1,0:T(8,128)}, s32[32,3072]{1,0:T(8,128)S(1)}, u32[]{:S(2)}, u32[]{:S(2)}) collective-permute-start(s32[32,3072]{1,0:T(8,128)} %c0.3), channel_id=1, source_target_pairs={{0,2},{1,3},{2,0},{3,1},{4,6},{5,7},{6,4},{7,5},{8,10},{9,11},{10,... | collective-permute-start | bytes 1179656 | tf_op jit(solution)/shard_map/ppermute | solution.py:327
  33.1 19.5 %collective-permute-start.2 = (s32[32,3072]{1,0:T(8,128)}, s32[32,3072]{1,0:T(8,128)S(1)}, u32[]{:S(2)}, u32[]{:S(2)}) collective-permute-start(s32[32,3072]{1,0:T(8,128)} %c0.3), channel_id=1, source_target_pairs={{0,1},{1,2},{2,3},{3,0},{4,5},{5,6},{6,7},{7,4},{8,9},{9,10},{10,1... | collective-permute-start | bytes 1179656 | tf_op jit(solution)/shard_map/ppermute | solution.py:327
  41.2 11.3 %copy-start.3 = (s32[32,3072]{1,0:T(8,128)}, s32[32,3072]{1,0:T(8,128)S(1)}, u32[]{:S(2)}) copy-start(s32[32,3072]{1,0:T(8,128)S(1)} %collective-permute-done.4.c3) | copy-start | bytes 1179652
  43.5 9.0 %copy-start.4 = (s32[32,3072]{1,0:T(8,128)}, s32[32,3072]{1,0:T(8,128)S(1)}, u32[]{:S(2)}) copy-start(s32[32,3072]{1,0:T(8,128)S(1)} %collective-permute-done.3.c2) | copy-start | bytes 1179652
  52.5 0.8 copy-start.5
  53.3 0.8 copy-start.7
  83.7 2.6 collective-permute-start.5
  123.4 4.6 %copy-start.1 = (f32[64,8,256]{2,1,0:T(8,128)}, f32[64,8,256]{2,1,0:T(8,128)S(1)}, u32[]{:S(2)}) copy-start(f32[64,8,256]{2,1,0:T(8,128)S(1)} %all_to_all.27.mine_ref) | copy-start | bytes 1572868
  123.4 4.6 %collective-permute-start.6 = (f32[64,8,256]{2,1,0:T(8,128)S(1)}, f32[64,8,256]{2,1,0:T(8,128)S(1)}, u32[]{:S(2)}, u32[]{:S(2)}) collective-permute-start(f32[64,8,256]{2,1,0:T(8,128)S(1)} %all_to_all.27.mine_ref), channel_id=1, source_target_pairs={{0,4},{4,0},{1,5},{5,1},{2,6},{6,2},{3,7},{7,3},{8,12},{12,8},{9,1... | collective-permute-start | bytes 1572872 | tf_op jit(solution)/shard_map/ppermute | solution.py:48
  128.1 0.8 copy-start.6
  154.9 2.1 collective-permute-start.7
  203.5 7.3 %copy-start = (f32[64,32,256]{2,1,0:T(8,128)}, f32[64,32,256]{2,1,0:T(8,128)S(1)}, u32[]{:S(2)}) copy-start(f32[64,32,256]{2,1,0:T(8,128)S(1)} %all_to_all.29.mine_ref) | copy-start | bytes 6291460
  203.5 12.0 %collective-permute-start.8 = (f32[64,32,256]{2,1,0:T(8,128)S(1)}, f32[64,32,256]{2,1,0:T(8,128)}, u32[]{:S(2)}, u32[]{:S(2)}) collective-permute-start(f32[64,32,256]{2,1,0:T(8,128)S(1)} %all_to_all.29.mine_ref), channel_id=1, source_target_pairs={{0,4},{4,0},{1,5},{5,1},{2,6},{6,2},{3,7},{7,3},{8,12},{12,8},{9,1... | collective-permute-start | bytes 6291464 | tf_op jit(solution)/shard_map/ppermute | solution.py:48

commit v3 on v2

--- a/solution.py
+++ b/solution.py
@@ -59,7 +59,7 @@
 
 
 def sums_kernel(
-    place_ref, pts_ref, mine_ref, other_ref, c0, c1, c2, c3,
+    place_ref, pts_ref, pieces_ref, c0, c1, c2, c3,
     keep_ref, give_ref, codes_ref, panel_ref, rotated_ref, ph_ref, pl_ref,
 ):
     count = pts_ref.shape[0]
@@ -73,8 +73,8 @@
             columns = slice(a * 256, a * 256 + 256)
             first = pl.multiple_of(z * 64 + core * 32, 32)
             second = pl.multiple_of(z * 64 + (1 - core) * 32, 32)
-            panel_ref[pl.ds(first, 32), columns] = mine_ref[a * 4 + z]
-            panel_ref[pl.ds(second, 32), columns] = other_ref[a * 4 + z]
+            panel_ref[pl.ds(first, 32), columns] = pieces_ref[a * 4 + z, 0]
+            panel_ref[pl.ds(second, 32), columns] = pieces_ref[a * 4 + z, 1]
 
     def rotate(j, carry):
         panel = panel_ref[:, pl.ds(pl.multiple_of(j * 256, 256), 256)].T
@@ -146,13 +146,13 @@
     lax.fori_loop(0, M // 8, eight_rows, 0)
 
 
-def code_sums(place, points, mine, other, codes):
+def code_sums(place, points, pieces, codes):
     count = points.shape[0]
     half = jax.ShapeDtypeStruct((M // 2, SUB, PAYLOAD), F32)
     return pl.pallas_call(
         sums_kernel,
         out_shape=(half, half),
-        in_specs=[SMEM] + [VMEM] * 7,
+        in_specs=[SMEM] + [VMEM] * 6,
         out_specs=(VMEM, VMEM),
         scratch_shapes=[
             pltpu.VMEM((M, count), jnp.int32),
@@ -163,12 +163,12 @@
         ],
         compiler_params=PARAMS,
         name="code_sums",
-    )(place, points, mine, other, *codes)
+    )(place, points, pieces, *codes)
 
 
 def cross_kernel(
     place_ref, pts_ref, mine_ref, other_ref, c0, c1, c2, c3,
-    keep_ref, give_ref, codes_ref, tab_ref, ah_ref, al_ref, ph_ref, pl_ref,
+    keep_ref, give_ref, codes_ref, tab_ref, ah0_ref, al0_ref, ah1_ref, al1_ref, ph_ref, pl_ref, acc_ref,
 ):
     count = pts_ref.shape[0]
     y, core = place_ref[0], place_ref[1]
@@ -179,8 +179,9 @@
     ph_ref[...] = ph
     pl_ref[...] = plo
     wide = 1024
-
-    def look_up(block, eight):
+    quarter = count // 4
+
+    def look_up(block, eight, ah_ref, al_ref):
         for n in range(0, count, wide):
             rows = codes_ref[at8(block * 4 + eight), n : n + wide]
             for two in range(4):
@@ -205,21 +206,29 @@
                 ah_ref[place, n : n + wide] = high
                 al_ref[place, n : n + wide] = low
 
-    def one_block(block, carry):
-        def eight_rows(eight, inside):
-            look_up(block, eight)
-            return inside
-
-        lax.fori_loop(0, 4, eight_rows, 0)
-        part = dot3(ah_ref[...], al_ref[...], ph_ref[...], pl_ref[...], NN)
-        for h in range(4):
-            even = part[h * 64 : h * 64 + 32]
-            odd = part[h * 64 + 32 : h * 64 + 64]
-            keep_ref[block * 4 + h] = jnp.where(core == 0, even, odd)
-            give_ref[block * 4 + h] = jnp.where(core == 0, odd, even)
-        return carry
-
-    lax.fori_loop(0, 4, one_block, 0)
+    slots = ((ah0_ref, al0_ref), (ah1_ref, al1_ref))
+    for stage in range(5):
+
+        def part(e, carry, stage=stage):
+            if stage > 0:
+                high_ref, low_ref = slots[(stage - 1) % 2]
+                here = pl.ds(pl.multiple_of(e * quarter, 128), quarter)
+                more = dot3(high_ref[:, here], low_ref[:, here], ph_ref[here], pl_ref[here], NN)
+            if stage < 4:
+                look_up(stage, e, *slots[stage % 2])
+            if stage > 0:
+                acc_ref[...] = more + jnp.where(e == 0, jnp.zeros_like(more), acc_ref[...])
+            return carry
+
+        if stage == 1:
+            acc_ref[...] = jnp.zeros_like(acc_ref)
+        lax.fori_loop(0, 4, part, 0)
+        if stage > 0:
+            for h in range(4):
+                even = acc_ref[h * 64 : h * 64 + 32]
+                odd = acc_ref[h * 64 + 32 : h * 64 + 64]
+                keep_ref[(stage - 1) * 4 + h] = jnp.where(core == 0, even, odd)
+                give_ref[(stage - 1) * 4 + h] = jnp.where(core == 0, odd, even)
 
 
 def cross_part(place, points, mine, other, codes):
@@ -235,16 +244,19 @@
             pltpu.VMEM((2, M // 2, SUB, K), F32),
             pltpu.VMEM((256, count), BF16),
             pltpu.VMEM((256, count), BF16),
+            pltpu.VMEM((256, count), BF16),
+            pltpu.VMEM((256, count), BF16),
             pltpu.VMEM((count, 256), BF16),
             pltpu.VMEM((count, 256), BF16),
+            pltpu.VMEM((256, 256), F32),
         ],
         compiler_params=PARAMS,
         name="cross_part",
     )(place, points, mine, other, *codes)
 
 
-def iterate_kernel(place_ref, mine_ref, other_ref, out_ref, now_ref, hl_ref, gh_ref, gl_ref, tail_ref):
-    y, column = place_ref[0], place_ref[2]
+def iterate_kernel(place_ref, mine_ref, other_ref, out_ref, now_ref, hl_ref, gh_ref, gl_ref, tail_ref, turned_ref):
+    y, core, column = place_ref[0], place_ref[1], place_ref[2]
     total = jnp.zeros((1, 256), F32)
     for half, source in enumerate((mine_ref, other_ref)):
         for block in range(4):
@@ -286,25 +298,27 @@
     lax.fori_loop(0, NS_ITERS - 1, step, 0)
     last = (NS_ITERS - 1) % 2
     high_ref, low_ref = hl_ref.at[last, 0], hl_ref.at[last, 1]
-    columns = pl.ds(pl.multiple_of(column * 128, 128), 128)
-    for half in range(2):
-        rows = pl.ds(pl.multiple_of(half * 512 + y * 128, 128), 128)
-        here = slice(half * 128, half * 128 + 128)
-        tail_ref[0, here] = high_ref[rows]
-        tail_ref[1, here] = low_ref[rows]
+    columns = pl.ds(pl.multiple_of(column // 4 * 128, 128), 128)
+    now = []
+    for z in range(4):
+        for c in range(2):
+            half = lax.rem(c + core, 2)
+            rows = pl.ds(pl.multiple_of(half * 512 + y * 128 + z * 32, 32), 32)
+            here = slice(z * 64 + c * 32, z * 64 + c * 32 + 32)
+            tail_ref[0, here] = high_ref[rows]
+            tail_ref[1, here] = low_ref[rows]
+            now.append(now_ref[rows, columns])
     gram = dot3(tail_ref[0], tail_ref[1], high_ref[...], low_ref[...], NT)
     high, low = split(gram)
     moved = dot3(high, low, high_ref[:, columns], low_ref[:, columns], NN)
-    for half in range(2):
-        rows = pl.ds(pl.multiple_of(half * 512 + y * 128, 128), 128)
-        here = slice(half * 128, half * 128 + 128)
-        out_ref[here, :] = (1.5 * now_ref[rows, columns] - 0.5 * moved[here]) * D**0.5
+    turned_ref[...] = ((1.5 * jnp.concatenate(now, axis=0) - 0.5 * moved) * D**0.5).T
+    out_ref[...] = turned_ref[pl.ds(pl.multiple_of(lax.rem(column, 4) * 32, 32), 32), :]
 
 
 def newton_schulz(place, mine, other):
     return pl.pallas_call(
         iterate_kernel,
-        out_shape=jax.ShapeDtypeStruct((256, 128), F32),
+        out_shape=jax.ShapeDtypeStruct((32, 256), F32),
         in_specs=[SMEM, VMEM, VMEM],
         out_specs=VMEM,
         scratch_shapes=[
@@ -313,6 +327,7 @@
             pltpu.VMEM((D, D), BF16),
             pltpu.VMEM((D, D), BF16),
             pltpu.VMEM((2, 256, D), BF16),
+            pltpu.VMEM((128, 256), F32),
         ],
         compiler_params=PARAMS,
         name="newton_schulz",
@@ -322,15 +337,15 @@
 def shards(points, codes, rotation):
     y, core = lax.axis_index("y"), lax.axis_index("core")
     own_row = lax.axis_index(ROWS)
-    place = jnp.stack([y, core, own_row // 4]).astype(jnp.int32)
+    place = jnp.stack([y, core, own_row]).astype(jnp.int32)
     all_codes = [codes] + [
         lax.ppermute(codes, "y", [(s, (s + i) % 4) for s in range(4)]) for i in (1, 2, 3)
     ]
     swapped = lax.ppermute(
         rotation, ("x", "y"), [(a * 4 + b, b * 4 + a) for a in range(4) for b in range(4)]
     )
-    pieces = spread_to(swapped, ("x", "z"), 16)
-    keep, give = code_sums(place, points, pieces, swap_core(pieces), all_codes)
+    pieces = spread_to(jnp.stack([swapped, swap_core(swapped)]), ("x", "z"), 16)
+    keep, give = code_sums(place, points, pieces, all_codes)
 
     sums = keep + swap_core(give)
     sums = jnp.sum(lax.all_to_all(sums, CHIPS, 0, 0, tiled=True), axis=0)
@@ -342,17 +357,12 @@
     block = keep + swap_core(give)
     block = jnp.sum(lax.all_to_all(block, ("x", "z"), 0, 0, tiled=True), axis=0)
     whole = spread_to(block, CHIPS, 64)
-    result = newton_schulz(place, whole, swap_core(whole))
-
-    result = lax.dynamic_slice_in_dim(result, (own_row % 4) * 32, 32, axis=1)
-    result = result.reshape(2, 4, 32, 32)
-    result = jnp.where(core == 0, result, result[::-1])
-    rotated = result.transpose(3, 1, 0, 2).reshape(32, 256)
-
     ours = lax.dynamic_slice_in_dim(centers, y * 16, 16, axis=0)
     theirs = lax.dynamic_slice_in_dim(others, y * 16, 16, axis=0)
     first, second = jnp.where(core == 0, ours, theirs), jnp.where(core == 0, theirs, ours)
     centroids = jnp.stack([first, second], axis=1).transpose(0, 1, 3, 2).reshape(32, K * SUB)
+    whole, centroids = lax.optimization_barrier((whole, centroids))
+    rotated = newton_schulz(place, whole, swap_core(whole))
     return (rotated, centroids)
 
 

time: 281 us -> 269 us (0.957)
  blocking collectives: 106 us -> 52.3 us
  waiting for transfers between devices: 24.3 us -> 47.4 us
  starting transfers between devices: 15.2 us -> 35.1 us
  Pallas kernels: 118 us -> 115 us
    all_to_all x3 -> x1, blocking collectives: 72.7 us -> 15.8 us  [spread_to(): return lax.all_to_all(copies, axes, 0, 0, tiled=True)]
    all_to_all x0 -> x2, starting transfers between devices: none -> 21.6 us  [spread_to(): return lax.all_to_all(copies, axes, 0, 0, tiled=True)]
    all_to_all x0 -> x2, waiting for transfers between devices: none -> 18.6 us  [spread_to(): return lax.all_to_all(copies, axes, 0, 0, tiled=True)]
    ppermute x5, waiting for transfers between devices: 5.41 us -> 10.1 us  [swap_core(): return lax.ppermute(value, 'core', [(0, 1), (1, 0)])]
    all_to_all x1, blocking collectives: 19.9 us -> 23.4 us  [shards(): sums = jnp.sum(lax.all_to_all(sums, CHIPS, 0, 0, tiled=True), axis=0)]
    pallas_call x1, Pallas kernels: 26 us -> 23.1 us  [cross_part(): pl.pallas_call(cross_kernel, out_shape=(half, half), in_specs=[SMEM] + [V...]
  transfers between devices with their start and end apart: 9 -> 11, of which waited for: 6 -> 9; matrix products, arithmetic and copies ran while one was open for 3% -> 3% of each run, Pallas kernels for 0% -> 0%
where the time goes in v3:
time: 269 us
  Pallas kernels  115 us (43%)
  blocking collectives  52.3 us (19%)
  waiting for transfers between devices  47.4 us (18%)
  starting transfers between devices  35.1 us (13%)
  local copies, waits for them, and re-layouts  13.8 us (5%)
  other arithmetic  4.07 us (2%)
    pallas_call x1, Pallas kernels, newton_schulz(): pl.pallas_call(iterate_kernel, out_shape=jax.ShapeDtypeStruct((32, 256),...  62.7 us
    pallas_call x1, Pallas kernels, code_sums(): pl.pallas_call(sums_kernel, out_shape=(half, half), in_specs=[SMEM] + [VM...  29.6 us
    all_to_all x1, blocking collectives, shards(): sums = jnp.sum(lax.all_to_all(sums, CHIPS, 0, 0, tiled=True), axis=0)  23.4 us
    pallas_call x1, Pallas kernels, cross_part(): pl.pallas_call(cross_kernel, out_shape=(half, half), in_specs=[SMEM] + [V...  23.1 us
    all_to_all x2, starting transfers between devices, spread_to(): return lax.all_to_all(copies, axes, 0, 0, tiled=True)  21.6 us
    ppermute x3, waiting for transfers between devices, shards(): lax.ppermute(codes, 'y', [(s, (s + i) % 4) for s in range(4)])  18.7 us
    all_to_all x2, waiting for transfers between devices, spread_to(): return lax.all_to_all(copies, axes, 0, 0, tiled=True)  18.6 us
    all_to_all x1, blocking collectives, spread_to(): return lax.all_to_all(copies, axes, 0, 0, tiled=True)  15.8 us
  transfers between devices with their start and end apart: 11, of which 9 were waited for; matrix products, arithmetic and copies ran while one was open for 3% of the time, Pallas kernels for 0%

profile of v3, /device:TPU:1, one launch (start us, length us, event | category | flops | bytes accessed | tf_op | source)
XLA Modules:
  0.0 268.8 jit_solution(13030962454176323410)
XLA Ops:
  0.6 0.0 copy-start.4
  0.6 1.5 collective-permute-start
  2.2 0.0 collective-permute-done
  2.2 1.4 collective-permute-start.1
  3.6 0.9 collective-permute-done.1
  4.5 1.1 broadcast_in_dim.6
  5.6 16.2 %all-to-all-start = ((f32[16,2,32,256]{3,2,1,0:T(8,128)}), f32[16,2,32,256]{3,2,1,0:T(8,128)S(1)}, u32[]{:S(2)}, u32[]{:S(2)}) async-start(f32[16,2,32,256]{3,2,1,0:T(8,128)} %broadcast_in_dim.6), calls=%async_computation | async-start | bytes 2097152 | tf_op jit(solution)/shard_map/all_to_all | solution.py:44
  21.8 0.0 copy-done.4
  21.8 1.3 collective-permute-start.4
  23.1 1.6 collective-permute-start.3
  24.7 0.0 collective-permute-start.2
  24.7 0.6 pad_add_fusion.place_ref
  25.3 6.6 %collective-permute-done.4.c3 = s32[32,3072]{1,0:T(8,128)S(1)} collective-permute-done((s32[32,3072]{1,0:T(8,128)S(1)}, s32[32,3072]{1,0:T(8,128)S(1)}, u32[]{:S(2)}, u32[]{:S(2)}) %collective-permute-start.4) | collective-permute-done | bytes 393248 | tf_op jit(solution)/shard_map/ppermute | solution.py:342
  31.9 2.4 collective-permute-done.3.c2
  34.3 0.0 copy-start.6
  34.3 9.7 %collective-permute-done.2.c1 = s32[32,3072]{1,0:T(8,128)S(1)} collective-permute-done((s32[32,3072]{1,0:T(8,128)S(1)}, s32[32,3072]{1,0:T(8,128)S(1)}, u32[]{:S(2)}, u32[]{:S(2)}) %collective-permute-start.2) | collective-permute-done | bytes 393248 | tf_op jit(solution)/shard_map/ppermute | solution.py:342
  44.0 0.0 all-to-all-done.pieces_ref
  44.0 0.0 copy-done.5
  44.0 0.0 copy-done.6
  44.0 0.7 copy-done.7
  44.8 1.0 copy-done.1
  45.8 29.6 %code_sums.1 = (f32[64,8,384]{2,1,0:T(8,128)}, f32[64,8,384]{2,1,0:T(8,128)}) custom-call(s32[3]{0:T(128)} %pad_add_fusion.place_ref, f32[3072,256]{1,0:T(8,128)} %pts_ref.3, f32[16,2,32,256]{3,2,1,0:T(8,128)} %copy-done.1, s32[32,3072]{1,0:T(8,128)} %c0.3, s32[32,3072]{1,0:T(8,128)} %copy-done.7, s32[32,3072]{1,0:T(8,128)} %copy-done.6, s32[32,3072]{1,0:T(8,128)} %copy-done.5), custom_call_target="tpu_custom_call" | custom-call | tf_op jit(solution)/shard_map/code_sums/pallas_call | solution.py:152
  75.4 0.5 collective-permute-start.5
  75.9 2.1 collective-permute-done.5
  78.0 1.2 add.18
  79.2 23.4 %all_to_all.25 = f32[64,8,384]{2,1,0:T(8,128)S(1)} all-to-all(f32[64,8,384]{2,1,0:T(8,128)S(1)} %add.18), channel_id=1, replica_groups=mesh['x'=4,'z'=4,'core'=2,'y'=4] {'y','x','z'}, dimensions={0} | all-to-all | bytes 1572864 | tf_op jit(solution)/shard_map/all_to_all | solution.py:351
  102.6 0.1 reduce_sum.18
  102.8 15.8 %all_to_all.26.mine_ref = f32[64,8,256]{2,1,0:T(8,128)S(1)} all-to-all(f32[64,8,256]{2,1,0:T(8,128)S(1)} %broadcast_in_dim.7), channel_id=1, replica_groups=mesh['x'=4,'z'=4,'core'=2,'y'=4] {'y','x','z'}, dimensions={0} | all-to-all | bytes 1048576 | tf_op jit(solution)/shard_map/all_to_all | solution.py:44
  118.6 3.1 %collective-permute-start.6 = (f32[64,8,256]{2,1,0:T(8,128)S(1)}, f32[64,8,256]{2,1,0:T(8,128)S(1)}, u32[]{:S(2)}, u32[]{:S(2)}) collective-permute-start(f32[64,8,256]{2,1,0:T(8,128)S(1)} %all_to_all.26.mine_ref), channel_id=1, source_target_pairs={{0,4},{4,0},{1,5},{5,1},{2,6},{6,2},{3,7},{7,3},{8,12},{12,8},{9,1... | collective-permute-start | bytes 1572872 | tf_op jit(solution)/shard_map/ppermute | solution.py:48
  121.7 1.5 collective-permute-done.6.other_ref
  123.2 0.0 copy-done.2
  123.2 0.8 copy-done.8
  124.0 23.1 %cross_part.1 = (f32[16,32,256]{2,1,0:T(8,128)}, f32[16,32,256]{2,1,0:T(8,128)}) custom-call(s32[3]{0:T(128)} %pad_add_fusion.place_ref, f32[3072,256]{1,0:T(8,128)} %pts_ref.3, f32[64,8,256]{2,1,0:T(8,128)} %copy-done.2, f32[64,8,256]{2,1,0:T(8,128)} %copy-done.8, s32[32,3072]{1,0:T(8,128)} %c0.3, s32[32,3072]{1,0:T(8,128)} %copy-done.7, ...), custom_call_target="tpu_custom_call" | custom-call | tf_op jit(solution)/shard_map/cross_part/pallas_call | solution.py:237
  147.1 0.4 collective-permute-start.7
  147.5 1.7 collective-permute-done.7
  149.2 1.1 add.19
  150.3 13.1 %all_to_all.27 = f32[16,32,256]{2,1,0:T(8,128)S(1)} all-to-all(f32[16,32,256]{2,1,0:T(8,128)S(1)} %add.19), channel_id=1, replica_groups=mesh['x'=4,'z'=4,'core'=2,'y'=4] {'x','z'}, dimensions={0} | all-to-all | bytes 1048576 | tf_op jit(solution)/shard_map/all_to_all | solution.py:358
  163.4 1.6 broadcast_in_dim.8
  165.1 5.4 %all-to-all-start.4 = ((f32[64,32,256]{2,1,0:T(8,128)}), f32[64,32,256]{2,1,0:T(8,128)S(1)}, u32[]{:S(2)}, u32[]{:S(2)}) async-start(f32[64,32,256]{2,1,0:T(8,128)} %broadcast_in_dim.8), calls=%async_computation.4 | async-start | bytes 4194304 | tf_op jit(solution)/shard_map/all_to_all | solution.py:44
  170.5 1.0 select_bitcast_fusion.1
  171.5 2.6 copy.5
  174.1 4.6 %reshape.20 = f32[32,2048]{1,0:T(8,128)} reshape(f32[16,2,256,8]{3,2,1,0:T(8,128)} %copy.5) | data formatting | bytes 524288 | tf_op jit(solution)/shard_map/reshape | solution.py:363
  178.8 18.6 %all-to-all-done.4.mine_ref = f32[64,32,256]{2,1,0:T(8,128)S(1)} async-done(((f32[64,32,256]{2,1,0:T(8,128)}), f32[64,32,256]{2,1,0:T(8,128)S(1)}, u32[]{:S(2)}, u32[]{:S(2)}) %all-to-all-start.4) | async-done | bytes 2097184 | tf_op jit(solution)/shard_map/all_to_all | solution.py:44
  197.3 3.7 %collective-permute-start.8 = (f32[64,32,256]{2,1,0:T(8,128)S(1)}, f32[64,32,256]{2,1,0:T(8,128)S(1)}, u32[]{:S(2)}, u32[]{:S(2)}) collective-permute-start(f32[64,32,256]{2,1,0:T(8,128)S(1)} %all-to-all-done.4.mine_ref), channel_id=1, source_target_pairs={{0,4},{4,0},{1,5},{5,1},{2,6},{6,2},{3,7},{7,3},{8,12},{12,8},{9,1... | collective-permute-start | bytes 6291464 | tf_op jit(solution)/shard_map/ppermute | solution.py:48
  201.0 3.8 %collective-permute-done.8.other_ref = f32[64,32,256]{2,1,0:T(8,128)S(1)} collective-permute-done((f32[64,32,256]{2,1,0:T(8,128)S(1)}, f32[64,32,256]{2,1,0:T(8,128)S(1)}, u32[]{:S(2)}, u32[]{:S(2)}) %collective-permute-start.8) | collective-permute-done | bytes 2097184 | tf_op jit(solution)/shard_map/ppermute | solution.py:48
  204.8 0.0 copy-done
  204.8 1.3 copy-done.3
  206.1 62.7 %newton_schulz.1 = f32[32,256]{1,0:T(8,128)} custom-call(s32[3]{0:T(128)} %pad_add_fusion.place_ref, f32[64,32,256]{2,1,0:T(8,128)} %copy-done, f32[64,32,256]{2,1,0:T(8,128)} %copy-done.3), custom_call_target="tpu_custom_call" | custom-call | tf_op jit(solution)/shard_map/newton_schulz/pallas_call | solution.py:319
  (13 shorter events, 0.1 us)
Async XLA Ops:
  0.6 21.1 %copy-start.4 = (s32[32,3072]{1,0:T(8,128)S(1)}, s32[32,3072]{1,0:T(8,128)}, u32[]{:S(2)}) copy-start(s32[32,3072]{1,0:T(8,128)} %c0.3) | copy-start | bytes 1179652
  0.6 1.6 collective-permute-start
  2.2 2.3 collective-permute-start.1
  5.6 38.4 %all-to-all-start = ((f32[16,2,32,256]{3,2,1,0:T(8,128)}), f32[16,2,32,256]{3,2,1,0:T(8,128)S(1)}, u32[]{:S(2)}, u32[]{:S(2)}) async-start(f32[16,2,32,256]{3,2,1,0:T(8,128)} %broadcast_in_dim.6), calls=%async_computation | async-start | bytes 2097152 | tf_op jit(solution)/shard_map/all_to_all | solution.py:44
  21.8 10.1 %collective-permute-start.4 = (s32[32,3072]{1,0:T(8,128)S(1)}, s32[32,3072]{1,0:T(8,128)S(1)}, u32[]{:S(2)}, u32[]{:S(2)}) collective-permute-start(s32[32,3072]{1,0:T(8,128)S(1)} %copy-done.4), channel_id=1, source_target_pairs={{0,3},{1,0},{2,1},{3,2},{4,7},{5,4},{6,5},{7,6},{8,11},{9,8},{10,9... | collective-permute-start | bytes 1179656 | tf_op jit(solution)/shard_map/ppermute | solution.py:342
  23.1 11.3 %collective-permute-start.3 = (s32[32,3072]{1,0:T(8,128)S(1)}, s32[32,3072]{1,0:T(8,128)S(1)}, u32[]{:S(2)}, u32[]{:S(2)}) collective-permute-start(s32[32,3072]{1,0:T(8,128)S(1)} %copy-done.4), channel_id=1, source_target_pairs={{0,2},{1,3},{2,0},{3,1},{4,6},{5,7},{6,4},{7,5},{8,10},{9,11},{10,... | collective-permute-start | bytes 1179656 | tf_op jit(solution)/shard_map/ppermute | solution.py:342
  24.7 19.4 %collective-permute-start.2 = (s32[32,3072]{1,0:T(8,128)S(1)}, s32[32,3072]{1,0:T(8,128)S(1)}, u32[]{:S(2)}, u32[]{:S(2)}) collective-permute-start(s32[32,3072]{1,0:T(8,128)S(1)} %copy-done.4), channel_id=1, source_target_pairs={{0,1},{1,2},{2,3},{3,0},{4,5},{5,6},{6,7},{7,4},{8,9},{9,10},{10,1... | collective-permute-start | bytes 1179656 | tf_op jit(solution)/shard_map/ppermute | solution.py:342
  31.9 12.1 %copy-start.5 = (s32[32,3072]{1,0:T(8,128)}, s32[32,3072]{1,0:T(8,128)S(1)}, u32[]{:S(2)}) copy-start(s32[32,3072]{1,0:T(8,128)S(1)} %collective-permute-done.4.c3) | copy-start | bytes 1179652
  34.3 9.7 %copy-start.6 = (s32[32,3072]{1,0:T(8,128)}, s32[32,3072]{1,0:T(8,128)S(1)}, u32[]{:S(2)}) copy-start(s32[32,3072]{1,0:T(8,128)S(1)} %collective-permute-done.3.c2) | copy-start | bytes 1179652
  44.0 0.8 copy-start.7
  44.8 1.0 copy-start.1
  75.4 2.6 collective-permute-start.5
  118.6 4.6 %copy-start.2 = (f32[64,8,256]{2,1,0:T(8,128)}, f32[64,8,256]{2,1,0:T(8,128)S(1)}, u32[]{:S(2)}) copy-start(f32[64,8,256]{2,1,0:T(8,128)S(1)} %all_to_all.26.mine_ref) | copy-start | bytes 1572868
  118.6 4.6 %collective-permute-start.6 = (f32[64,8,256]{2,1,0:T(8,128)S(1)}, f32[64,8,256]{2,1,0:T(8,128)S(1)}, u32[]{:S(2)}, u32[]{:S(2)}) collective-permute-start(f32[64,8,256]{2,1,0:T(8,128)S(1)} %all_to_all.26.mine_ref), channel_id=1, source_target_pairs={{0,4},{4,0},{1,5},{5,1},{2,6},{6,2},{3,7},{7,3},{8,12},{12,8},{9,1... | collective-permute-start | bytes 1572872 | tf_op jit(solution)/shard_map/ppermute | solution.py:48
  123.2 0.8 copy-start.8
  147.1 2.1 collective-permute-start.7
  165.1 32.3 %all-to-all-start.4 = ((f32[64,32,256]{2,1,0:T(8,128)}), f32[64,32,256]{2,1,0:T(8,128)S(1)}, u32[]{:S(2)}, u32[]{:S(2)}) async-start(f32[64,32,256]{2,1,0:T(8,128)} %broadcast_in_dim.8), calls=%async_computation.4 | async-start | bytes 4194304 | tf_op jit(solution)/shard_map/all_to_all | solution.py:44
  197.3 7.5 %copy-start = (f32[64,32,256]{2,1,0:T(8,128)}, f32[64,32,256]{2,1,0:T(8,128)S(1)}, u32[]{:S(2)}) copy-start(f32[64,32,256]{2,1,0:T(8,128)S(1)} %all-to-all-done.4.mine_ref) | copy-start | bytes 6291460
  197.3 7.5 %collective-permute-start.8 = (f32[64,32,256]{2,1,0:T(8,128)S(1)}, f32[64,32,256]{2,1,0:T(8,128)S(1)}, u32[]{:S(2)}, u32[]{:S(2)}) collective-permute-start(f32[64,32,256]{2,1,0:T(8,128)S(1)} %all-to-all-done.4.mine_ref), channel_id=1, source_target_pairs={{0,4},{4,0},{1,5},{5,1},{2,6},{6,2},{3,7},{7,3},{8,12},{12,8},{9,1... | collective-permute-start | bytes 6291464 | tf_op jit(solution)/shard_map/ppermute | solution.py:48
  204.8 1.3 copy-start.3

commit v4 on v3

--- a/solution.py
+++ b/solution.py
@@ -338,13 +338,16 @@
     y, core = lax.axis_index("y"), lax.axis_index("core")
     own_row = lax.axis_index(ROWS)
     place = jnp.stack([y, core, own_row]).astype(jnp.int32)
-    all_codes = [codes] + [
-        lax.ppermute(codes, "y", [(s, (s + i) % 4) for s in range(4)]) for i in (1, 2, 3)
-    ]
+    one = lax.ppermute(codes, "y", [(s, (s + 1) % 4) for s in range(4)])
+    three = lax.ppermute(codes, "y", [(s, (s + 3) % 4) for s in range(4)])
     swapped = lax.ppermute(
         rotation, ("x", "y"), [(a * 4 + b, b * 4 + a) for a in range(4) for b in range(4)]
     )
-    pieces = spread_to(jnp.stack([swapped, swap_core(swapped)]), ("x", "z"), 16)
+    pieces = jnp.stack([swapped, swap_core(swapped)])
+    pieces, one, three = lax.optimization_barrier((pieces, one, three))
+    pieces = spread_to(pieces, ("x", "z"), 16)
+    two = lax.ppermute(one, "y", [(s, (s + 1) % 4) for s in range(4)])
+    all_codes = [codes, one, two, three]
     keep, give = code_sums(place, points, pieces, all_codes)
 
     sums = keep + swap_core(give)

time: 269 us -> 264 us (0.981)
  starting transfers between devices: 35.1 us -> 30.4 us
  waiting for transfers between devices: 47.4 us -> 50.8 us
  blocking collectives: 52.3 us -> 49.2 us
    all_to_all x2, starting transfers between devices: 21.6 us -> 14 us  [spread_to(): return lax.all_to_all(copies, axes, 0, 0, tiled=True)]
    all_to_all x2, waiting for transfers between devices: 18.6 us -> 23.5 us  [spread_to(): return lax.all_to_all(copies, axes, 0, 0, tiled=True)]
    all_to_all x1, blocking collectives: 23.4 us -> 20.4 us  [shards(): sums = jnp.sum(lax.all_to_all(sums, CHIPS, 0, 0, tiled=True), axis=0)]
  transfers between devices with their start and end apart: 11 -> 11, of which waited for: 9 -> 10; matrix products, arithmetic and copies ran while one was open for 3% -> 3% of each run, Pallas kernels for 0% -> 0%
where the time goes in v4:
time: 264 us
  Pallas kernels  115 us (44%)
  waiting for transfers between devices  50.8 us (19%)
  blocking collectives  49.2 us (19%)
  starting transfers between devices  30.4 us (12%)
  local copies, waits for them, and re-layouts  13.1 us (5%)
  other arithmetic  4.08 us (2%)
    pallas_call x1, Pallas kernels, newton_schulz(): pl.pallas_call(iterate_kernel, out_shape=jax.ShapeDtypeStruct((32, 256),...  62.7 us
    pallas_call x1, Pallas kernels, code_sums(): pl.pallas_call(sums_kernel, out_shape=(half, half), in_specs=[SMEM] + [VM...  29.6 us
    all_to_all x2, waiting for transfers between devices, spread_to(): return lax.all_to_all(copies, axes, 0, 0, tiled=True)  23.5 us
    pallas_call x1, Pallas kernels, cross_part(): pl.pallas_call(cross_kernel, out_shape=(half, half), in_specs=[SMEM] + [V...  23.1 us
    all_to_all x1, blocking collectives, shards(): sums = jnp.sum(lax.all_to_all(sums, CHIPS, 0, 0, tiled=True), axis=0)  20.4 us
    all_to_all x1, blocking collectives, spread_to(): return lax.all_to_all(copies, axes, 0, 0, tiled=True)  15.8 us
    all_to_all x2, starting transfers between devices, spread_to(): return lax.all_to_all(copies, axes, 0, 0, tiled=True)  14 us
    all_to_all x1, blocking collectives, shards(): block = jnp.sum(lax.all_to_all(block, ('x', 'z'), 0, 0, tiled=True), axis=0)  13.1 us
  transfers between devices with their start and end apart: 11, of which 10 were waited for; matrix products, arithmetic and copies ran while one was open for 3% of the time, Pallas kernels for 0%

profile of v4, /device:TPU:1, one launch (start us, length us, event | category | flops | bytes accessed | tf_op | source)
XLA Modules:
  0.0 263.8 jit_solution(15790238284735710315)
XLA Ops:
  0.6 3.6 %collective-permute-start.3 = (s32[32,3072]{1,0:T(8,128)}, s32[32,3072]{1,0:T(8,128)S(1)}, u32[]{:S(2)}, u32[]{:S(2)}) collective-permute-start(s32[32,3072]{1,0:T(8,128)} %c0.3), channel_id=1, source_target_pairs={{0,3},{1,0},{2,1},{3,2},{4,7},{5,4},{6,5},{7,6},{8,11},{9,8},{10,9... | collective-permute-start | bytes 1179656 | tf_op jit(solution)/shard_map/ppermute | solution.py:342
  4.3 0.0 collective-permute-start.2
  4.3 1.4 collective-permute-start
  5.7 0.0 collective-permute-done
  5.7 1.0 collective-permute-start.1
  6.6 0.9 collective-permute-done.1
  7.5 5.1 %collective-permute-done.3.c3 = s32[32,3072]{1,0:T(8,128)S(1)} collective-permute-done((s32[32,3072]{1,0:T(8,128)}, s32[32,3072]{1,0:T(8,128)S(1)}, u32[]{:S(2)}, u32[]{:S(2)}) %collective-permute-start.3) | collective-permute-done | bytes 393248 | tf_op jit(solution)/shard_map/ppermute | solution.py:342
  12.6 0.0 copy-start.4
  12.6 2.8 %collective-permute-done.2.c1 = s32[32,3072]{1,0:T(8,128)S(1)} collective-permute-done((s32[32,3072]{1,0:T(8,128)}, s32[32,3072]{1,0:T(8,128)S(1)}, u32[]{:S(2)}, u32[]{:S(2)}) %collective-permute-start.2) | collective-permute-done | bytes 393248 | tf_op jit(solution)/shard_map/ppermute | solution.py:341
  15.3 0.0 copy-start.5
  15.4 1.1 broadcast_in_dim.6
  16.5 8.6 %all-to-all-start = ((f32[16,2,32,256]{3,2,1,0:T(8,128)}), f32[16,2,32,256]{3,2,1,0:T(8,128)S(1)}, u32[]{:S(2)}, u32[]{:S(2)}) async-start(f32[16,2,32,256]{3,2,1,0:T(8,128)} %broadcast_in_dim.6), calls=%async_computation | async-start | bytes 2097152 | tf_op jit(solution)/shard_map/all_to_all | solution.py:44
  25.1 0.1 collective-permute-start.4
  25.2 0.6 pad_add_fusion.place_ref
  25.8 9.4 %collective-permute-done.4.c2 = s32[32,3072]{1,0:T(8,128)S(1)} collective-permute-done((s32[32,3072]{1,0:T(8,128)S(1)}, s32[32,3072]{1,0:T(8,128)S(1)}, u32[]{:S(2)}, u32[]{:S(2)}) %collective-permute-start.4) | collective-permute-done | bytes 393248 | tf_op jit(solution)/shard_map/ppermute | solution.py:349
  35.2 4.9 %all-to-all-done.pieces_ref = f32[16,2,32,256]{3,2,1,0:T(8,128)S(1)} async-done(((f32[16,2,32,256]{3,2,1,0:T(8,128)}), f32[16,2,32,256]{3,2,1,0:T(8,128)S(1)}, u32[]{:S(2)}, u32[]{:S(2)}) %all-to-all-start) | async-done | bytes 1048608 | tf_op jit(solution)/shard_map/all_to_all | solution.py:44
  40.1 0.0 copy-done.4
  40.1 0.0 copy-done.5
  40.1 0.0 copy-done.6
  40.1 0.0 copy-start.1
  40.1 1.0 copy-done.1
  41.1 29.6 %code_sums.1 = (f32[64,8,384]{2,1,0:T(8,128)}, f32[64,8,384]{2,1,0:T(8,128)}) custom-call(s32[3]{0:T(128)} %pad_add_fusion.place_ref, f32[3072,256]{1,0:T(8,128)} %pts_ref.3, f32[16,2,32,256]{3,2,1,0:T(8,128)} %copy-done.1, s32[32,3072]{1,0:T(8,128)} %c0.3, s32[32,3072]{1,0:T(8,128)} %copy-done.5, s32[32,3072]{1,0:T(8,128)} %copy-done.6, s32[32,3072]{1,0:T(8,128)} %copy-done.4), custom_call_target="tpu_custom_call" | custom-call | tf_op jit(solution)/shard_map/code_sums/pallas_call | solution.py:152
  70.7 3.1 %collective-permute-start.5 = (f32[64,8,384]{2,1,0:T(8,128)}, f32[64,8,384]{2,1,0:T(8,128)S(1)}, u32[]{:S(2)}, u32[]{:S(2)}) collective-permute-start(f32[64,8,384]{2,1,0:T(8,128)} %get-tuple-element.15), channel_id=1, source_target_pairs={{0,4},{4,0},{1,5},{5,1},{2,6},{6,2},{3,7},{7,3},{8,12},{12,8},{9,1... | collective-permute-start | bytes 2359304 | tf_op jit(solution)/shard_map/ppermute | solution.py:48
  73.8 2.1 collective-permute-done.5
  76.0 1.2 add.18
  77.2 20.4 %all_to_all.25 = f32[64,8,384]{2,1,0:T(8,128)S(1)} all-to-all(f32[64,8,384]{2,1,0:T(8,128)S(1)} %add.18), channel_id=1, replica_groups=mesh['x'=4,'z'=4,'core'=2,'y'=4] {'y','x','z'}, dimensions={0} | all-to-all | bytes 1572864 | tf_op jit(solution)/shard_map/all_to_all | solution.py:354
  97.6 0.1 reduce_sum.18
  97.7 15.8 %all_to_all.26.mine_ref = f32[64,8,256]{2,1,0:T(8,128)S(1)} all-to-all(f32[64,8,256]{2,1,0:T(8,128)S(1)} %broadcast_in_dim.7), channel_id=1, replica_groups=mesh['x'=4,'z'=4,'core'=2,'y'=4] {'y','x','z'}, dimensions={0} | all-to-all | bytes 1048576 | tf_op jit(solution)/shard_map/all_to_all | solution.py:44
  113.5 3.1 %collective-permute-start.6 = (f32[64,8,256]{2,1,0:T(8,128)S(1)}, f32[64,8,256]{2,1,0:T(8,128)S(1)}, u32[]{:S(2)}, u32[]{:S(2)}) collective-permute-start(f32[64,8,256]{2,1,0:T(8,128)S(1)} %all_to_all.26.mine_ref), channel_id=1, source_target_pairs={{0,4},{4,0},{1,5},{5,1},{2,6},{6,2},{3,7},{7,3},{8,12},{12,8},{9,1... | collective-permute-start | bytes 1572872 | tf_op jit(solution)/shard_map/ppermute | solution.py:48
  116.6 1.5 collective-permute-done.6.other_ref
  118.1 0.0 copy-done.2
  118.1 0.8 copy-done.7
  118.9 23.1 %cross_part.1 = (f32[16,32,256]{2,1,0:T(8,128)}, f32[16,32,256]{2,1,0:T(8,128)}) custom-call(s32[3]{0:T(128)} %pad_add_fusion.place_ref, f32[3072,256]{1,0:T(8,128)} %pts_ref.3, f32[64,8,256]{2,1,0:T(8,128)} %copy-done.2, f32[64,8,256]{2,1,0:T(8,128)} %copy-done.7, s32[32,3072]{1,0:T(8,128)} %c0.3, s32[32,3072]{1,0:T(8,128)} %copy-done.5, ...), custom_call_target="tpu_custom_call" | custom-call | tf_op jit(solution)/shard_map/cross_part/pallas_call | solution.py:237
  142.0 0.4 collective-permute-start.7
  142.4 1.7 collective-permute-done.7
  144.2 1.1 add.19
  145.3 13.1 %all_to_all.27 = f32[16,32,256]{2,1,0:T(8,128)S(1)} all-to-all(f32[16,32,256]{2,1,0:T(8,128)S(1)} %add.19), channel_id=1, replica_groups=mesh['x'=4,'z'=4,'core'=2,'y'=4] {'x','z'}, dimensions={0} | all-to-all | bytes 1048576 | tf_op jit(solution)/shard_map/all_to_all | solution.py:361
  158.4 1.6 broadcast_in_dim.8
  160.0 5.4 %all-to-all-start.4 = ((f32[64,32,256]{2,1,0:T(8,128)}), f32[64,32,256]{2,1,0:T(8,128)S(1)}, u32[]{:S(2)}, u32[]{:S(2)}) async-start(f32[64,32,256]{2,1,0:T(8,128)} %broadcast_in_dim.8), calls=%async_computation.4 | async-start | bytes 4194304 | tf_op jit(solution)/shard_map/all_to_all | solution.py:44
  165.4 1.0 select_bitcast_fusion.1
  166.4 2.6 copy.5
  169.0 4.6 %reshape.20 = f32[32,2048]{1,0:T(8,128)} reshape(f32[16,2,256,8]{3,2,1,0:T(8,128)} %copy.5) | data formatting | bytes 524288 | tf_op jit(solution)/shard_map/reshape | solution.py:366
  173.7 18.6 %all-to-all-done.4.mine_ref = f32[64,32,256]{2,1,0:T(8,128)S(1)} async-done(((f32[64,32,256]{2,1,0:T(8,128)}), f32[64,32,256]{2,1,0:T(8,128)S(1)}, u32[]{:S(2)}, u32[]{:S(2)}) %all-to-all-start.4) | async-done | bytes 2097184 | tf_op jit(solution)/shard_map/all_to_all | solution.py:44
  192.2 3.7 %collective-permute-start.8 = (f32[64,32,256]{2,1,0:T(8,128)S(1)}, f32[64,32,256]{2,1,0:T(8,128)S(1)}, u32[]{:S(2)}, u32[]{:S(2)}) collective-permute-start(f32[64,32,256]{2,1,0:T(8,128)S(1)} %all-to-all-done.4.mine_ref), channel_id=1, source_target_pairs={{0,4},{4,0},{1,5},{5,1},{2,6},{6,2},{3,7},{7,3},{8,12},{12,8},{9,1... | collective-permute-start | bytes 6291464 | tf_op jit(solution)/shard_map/ppermute | solution.py:48
  195.9 3.8 %collective-permute-done.8.other_ref = f32[64,32,256]{2,1,0:T(8,128)S(1)} collective-permute-done((f32[64,32,256]{2,1,0:T(8,128)S(1)}, f32[64,32,256]{2,1,0:T(8,128)S(1)}, u32[]{:S(2)}, u32[]{:S(2)}) %collective-permute-start.8) | collective-permute-done | bytes 2097184 | tf_op jit(solution)/shard_map/ppermute | solution.py:48
  199.7 0.0 copy-done
  199.7 1.3 copy-done.3
  201.0 62.7 %newton_schulz.1 = f32[32,256]{1,0:T(8,128)} custom-call(s32[3]{0:T(128)} %pad_add_fusion.place_ref, f32[64,32,256]{2,1,0:T(8,128)} %copy-done, f32[64,32,256]{2,1,0:T(8,128)} %copy-done.3), custom_call_target="tpu_custom_call" | custom-call | tf_op jit(solution)/shard_map/newton_schulz/pallas_call | solution.py:319
  (11 shorter events, 0.1 us)
Async XLA Ops:
  0.6 11.9 %collective-permute-start.3 = (s32[32,3072]{1,0:T(8,128)}, s32[32,3072]{1,0:T(8,128)S(1)}, u32[]{:S(2)}, u32[]{:S(2)}) collective-permute-start(s32[32,3072]{1,0:T(8,128)} %c0.3), channel_id=1, source_target_pairs={{0,3},{1,0},{2,1},{3,2},{4,7},{5,4},{6,5},{7,6},{8,11},{9,8},{10,9... | collective-permute-start | bytes 1179656 | tf_op jit(solution)/shard_map/ppermute | solution.py:342
  4.3 11.1 %collective-permute-start.2 = (s32[32,3072]{1,0:T(8,128)}, s32[32,3072]{1,0:T(8,128)S(1)}, u32[]{:S(2)}, u32[]{:S(2)}) collective-permute-start(s32[32,3072]{1,0:T(8,128)} %c0.3), channel_id=1, source_target_pairs={{0,1},{1,2},{2,3},{3,0},{4,5},{5,6},{6,7},{7,4},{8,9},{9,10},{10,1... | collective-permute-start | bytes 1179656 | tf_op jit(solution)/shard_map/ppermute | solution.py:341
  4.3 1.4 collective-permute-start
  5.7 1.8 collective-permute-start.1
  12.6 27.5 %copy-start.4 = (s32[32,3072]{1,0:T(8,128)}, s32[32,3072]{1,0:T(8,128)S(1)}, u32[]{:S(2)}) copy-start(s32[32,3072]{1,0:T(8,128)S(1)} %collective-permute-done.3.c3) | copy-start | bytes 1179652
  15.3 24.8 %copy-start.5 = (s32[32,3072]{1,0:T(8,128)}, s32[32,3072]{1,0:T(8,128)S(1)}, u32[]{:S(2)}) copy-start(s32[32,3072]{1,0:T(8,128)S(1)} %collective-permute-done.2.c1) | copy-start | bytes 1179652
  16.5 23.6 %all-to-all-start = ((f32[16,2,32,256]{3,2,1,0:T(8,128)}), f32[16,2,32,256]{3,2,1,0:T(8,128)S(1)}, u32[]{:S(2)}, u32[]{:S(2)}) async-start(f32[16,2,32,256]{3,2,1,0:T(8,128)} %broadcast_in_dim.6), calls=%async_computation | async-start | bytes 2097152 | tf_op jit(solution)/shard_map/all_to_all | solution.py:44
  25.1 10.1 %collective-permute-start.4 = (s32[32,3072]{1,0:T(8,128)S(1)}, s32[32,3072]{1,0:T(8,128)S(1)}, u32[]{:S(2)}, u32[]{:S(2)}) collective-permute-start(s32[32,3072]{1,0:T(8,128)S(1)} %collective-permute-done.2.c1), channel_id=1, source_target_pairs={{0,1},{1,2},{2,3},{3,0},{4,5},{5,6},{6,7},{7,4},{8,9},{9,10},{10,1... | collective-permute-start | bytes 1179656 | tf_op jit(solution)/shard_map/ppermute | solution.py:349
  35.2 4.9 %copy-start.6 = (s32[32,3072]{1,0:T(8,128)}, s32[32,3072]{1,0:T(8,128)S(1)}, u32[]{:S(2)}) copy-start(s32[32,3072]{1,0:T(8,128)S(1)} %collective-permute-done.4.c2) | copy-start | bytes 1179652
  40.1 1.0 copy-start.1
  70.7 5.2 %collective-permute-start.5 = (f32[64,8,384]{2,1,0:T(8,128)}, f32[64,8,384]{2,1,0:T(8,128)S(1)}, u32[]{:S(2)}, u32[]{:S(2)}) collective-permute-start(f32[64,8,384]{2,1,0:T(8,128)} %get-tuple-element.15), channel_id=1, source_target_pairs={{0,4},{4,0},{1,5},{5,1},{2,6},{6,2},{3,7},{7,3},{8,12},{12,8},{9,1... | collective-permute-start | bytes 2359304 | tf_op jit(solution)/shard_map/ppermute | solution.py:48
  113.5 4.6 %copy-start.2 = (f32[64,8,256]{2,1,0:T(8,128)}, f32[64,8,256]{2,1,0:T(8,128)S(1)}, u32[]{:S(2)}) copy-start(f32[64,8,256]{2,1,0:T(8,128)S(1)} %all_to_all.26.mine_ref) | copy-start | bytes 1572868
  113.5 4.6 %collective-permute-start.6 = (f32[64,8,256]{2,1,0:T(8,128)S(1)}, f32[64,8,256]{2,1,0:T(8,128)S(1)}, u32[]{:S(2)}, u32[]{:S(2)}) collective-permute-start(f32[64,8,256]{2,1,0:T(8,128)S(1)} %all_to_all.26.mine_ref), channel_id=1, source_target_pairs={{0,4},{4,0},{1,5},{5,1},{2,6},{6,2},{3,7},{7,3},{8,12},{12,8},{9,1... | collective-permute-start | bytes 1572872 | tf_op jit(solution)/shard_map/ppermute | solution.py:48
  118.1 0.8 copy-start.7
  142.0 2.1 collective-permute-start.7
  160.0 32.2 %all-to-all-start.4 = ((f32[64,32,256]{2,1,0:T(8,128)}), f32[64,32,256]{2,1,0:T(8,128)S(1)}, u32[]{:S(2)}, u32[]{:S(2)}) async-start(f32[64,32,256]{2,1,0:T(8,128)} %broadcast_in_dim.8), calls=%async_computation.4 | async-start | bytes 4194304 | tf_op jit(solution)/shard_map/all_to_all | solution.py:44
  192.2 7.5 %copy-start = (f32[64,32,256]{2,1,0:T(8,128)}, f32[64,32,256]{2,1,0:T(8,128)S(1)}, u32[]{:S(2)}) copy-start(f32[64,32,256]{2,1,0:T(8,128)S(1)} %all-to-all-done.4.mine_ref) | copy-start | bytes 6291460
  192.2 7.5 %collective-permute-start.8 = (f32[64,32,256]{2,1,0:T(8,128)S(1)}, f32[64,32,256]{2,1,0:T(8,128)S(1)}, u32[]{:S(2)}, u32[]{:S(2)}) collective-permute-start(f32[64,32,256]{2,1,0:T(8,128)S(1)} %all-to-all-done.4.mine_ref), channel_id=1, source_target_pairs={{0,4},{4,0},{1,5},{5,1},{2,6},{6,2},{3,7},{7,3},{8,12},{12,8},{9,1... | collective-permute-start | bytes 6291464 | tf_op jit(solution)/shard_map/ppermute | solution.py:48
  199.7 1.3 copy-start.3

commit v5 on v4

--- a/solution.py
+++ b/solution.py
@@ -18,7 +18,12 @@
 NT = (((1,), (1,)), ((), ()))
 VMEM = pl.BlockSpec(memory_space=pltpu.VMEM)
 SMEM = pl.BlockSpec(memory_space=pltpu.SMEM)
-PARAMS = pltpu.CompilerParams(vmem_limit_bytes=56 * 1024 * 1024)
+
+
+def grant(mebibytes):
+    return pltpu.CompilerParams(vmem_limit_bytes=mebibytes * 1024 * 1024)
+
+
 PAYLOAD = K + 128
 
 
@@ -161,7 +166,7 @@
             pltpu.VMEM((count, 256), BF16),
             pltpu.VMEM((count, 256), BF16),
         ],
-        compiler_params=PARAMS,
+        compiler_params=grant(36),
         name="code_sums",
     )(place, points, pieces, *codes)
 
@@ -250,7 +255,7 @@
             pltpu.VMEM((count, 256), BF16),
             pltpu.VMEM((256, 256), F32),
         ],
-        compiler_params=PARAMS,
+        compiler_params=grant(28),
         name="cross_part",
     )(place, points, mine, other, *codes)
 
@@ -329,7 +334,7 @@
             pltpu.VMEM((2, 256, D), BF16),
             pltpu.VMEM((128, 256), F32),
         ],
-        compiler_params=PARAMS,
+        compiler_params=grant(34),
         name="newton_schulz",
     )(place, mine, other)
 
@@ -344,8 +349,9 @@
         rotation, ("x", "y"), [(a * 4 + b, b * 4 + a) for a in range(4) for b in range(4)]
     )
     pieces = jnp.stack([swapped, swap_core(swapped)])
+    pieces = jnp.broadcast_to(pieces[None], (16,) + pieces.shape)
     pieces, one, three = lax.optimization_barrier((pieces, one, three))
-    pieces = spread_to(pieces, ("x", "z"), 16)
+    pieces = lax.all_to_all(pieces, ("x", "z"), 0, 0, tiled=True)
     two = lax.ppermute(one, "y", [(s, (s + 1) % 4) for s in range(4)])
     all_codes = [codes, one, two, three]
     keep, give = code_sums(place, points, pieces, all_codes)

time: 264 us -> 256 us (0.970)
  Pallas kernels: 115 us -> 109 us
    all_to_all x2 -> x1, starting transfers between devices: 14 us -> 5.37 us  [spread_to(): return lax.all_to_all(copies, axes, 0, 0, tiled=True)]
    all_to_all x0 -> x1, starting transfers between devices: none -> 8.45 us  [shards(): pieces = lax.all_to_all(pieces, ('x', 'z'), 0, 0, tiled=True)]
    all_to_all x2 -> x1, waiting for transfers between devices: 23.5 us -> 18.5 us  [spread_to(): return lax.all_to_all(copies, axes, 0, 0, tiled=True)]
    all_to_all x0 -> x1, waiting for transfers between devices: none -> 4.79 us  [shards(): pieces = lax.all_to_all(pieces, ('x', 'z'), 0, 0, tiled=True)]
where the time goes in v5:
time: 256 us; the launch traced here: 255 us
  Pallas kernels  109 us (43%)
  waiting for transfers between devices  50.9 us (20%)
  blocking collectives  49.3 us (19%)
  starting transfers between devices  30.4 us (12%)
  local copies, waits for them, and re-layouts  12 us (5%)
    pallas_call x1, Pallas kernels, newton_schulz(): pl.pallas_call(iterate_kernel, out_shape=jax.ShapeDtypeStruct((32, 256),...  61 us
    pallas_call x1, Pallas kernels, code_sums(): pl.pallas_call(sums_kernel, out_shape=(half, half), in_specs=[SMEM] + [VM...  27.3 us
    pallas_call x1, Pallas kernels, cross_part(): pl.pallas_call(cross_kernel, out_shape=(half, half), in_specs=[SMEM] + [V...  20.8 us
    all_to_all x1, blocking collectives, shards(): sums = jnp.sum(lax.all_to_all(sums, CHIPS, 0, 0, tiled=True), axis=0)  20.4 us
    all_to_all x1, waiting for transfers between devices, spread_to(): return lax.all_to_all(copies, axes, 0, 0, tiled=True)  18.5 us
    all_to_all x1, blocking collectives, spread_to(): return lax.all_to_all(copies, axes, 0, 0, tiled=True)  15.8 us
    all_to_all x1, blocking collectives, shards(): block = jnp.sum(lax.all_to_all(block, ('x', 'z'), 0, 0, tiled=True), axis=0)  13.1 us
    ppermute x5, starting transfers between devices, swap_core(): return lax.ppermute(value, 'core', [(0, 1), (1, 0)])  11.5 us
  transfers between devices with their start and end apart: 11, of which 10 were waited for; matrix products, arithmetic and copies ran while one was open for 3% of the time, Pallas kernels for 0%

profile of v5, /device:TPU:1, one launch (start us, length us, event | category | flops | bytes accessed | tf_op | source)
XLA Modules:
  0.0 255.0 jit_solution(10379208452276669565)
XLA Ops:
  0.6 0.0 copy-start
  0.6 3.6 %collective-permute-start.3 = (s32[32,3072]{1,0:T(8,128)}, s32[32,3072]{1,0:T(8,128)S(1)}, u32[]{:S(2)}, u32[]{:S(2)}) collective-permute-start(s32[32,3072]{1,0:T(8,128)} %c0.3), channel_id=1, source_target_pairs={{0,3},{1,0},{2,1},{3,2},{4,7},{5,4},{6,5},{7,6},{8,11},{9,8},{10,9... | collective-permute-start | bytes 1179656 | tf_op jit(solution)/shard_map/ppermute | solution.py:347
  4.3 0.0 collective-permute-start.2
  4.3 1.4 collective-permute-start
  5.7 0.0 collective-permute-done
  5.7 1.0 collective-permute-start.1
  6.6 0.9 collective-permute-done.1
  7.5 5.1 %collective-permute-done.3.c3 = s32[32,3072]{1,0:T(8,128)S(1)} collective-permute-done((s32[32,3072]{1,0:T(8,128)}, s32[32,3072]{1,0:T(8,128)S(1)}, u32[]{:S(2)}, u32[]{:S(2)}) %collective-permute-start.3) | collective-permute-done | bytes 393248 | tf_op jit(solution)/shard_map/ppermute | solution.py:347
  12.6 0.0 copy-start.4
  12.6 2.9 %collective-permute-done.2.c1 = s32[32,3072]{1,0:T(8,128)} collective-permute-done((s32[32,3072]{1,0:T(8,128)}, s32[32,3072]{1,0:T(8,128)}, u32[]{:S(2)}, u32[]{:S(2)}) %collective-permute-start.2) | collective-permute-done | bytes 393248 | tf_op jit(solution)/shard_map/ppermute | solution.py:346
  15.5 1.1 broadcast_in_dim.6
  16.6 8.4 %all-to-all-start = ((f32[16,2,32,256]{3,2,1,0:T(8,128)}), f32[16,2,32,256]{3,2,1,0:T(8,128)}, u32[]{:S(2)}, u32[]{:S(2)}) async-start(f32[16,2,32,256]{3,2,1,0:T(8,128)} %broadcast_in_dim.6), calls=%async_computation | async-start | bytes 2097152 | tf_op jit(solution)/shard_map/all_to_all | solution.py:354
  25.0 0.1 collective-permute-start.4
  25.1 0.1 pad_add_fusion.place_ref
  25.2 10.0 %collective-permute-done.4.c2 = s32[32,3072]{1,0:T(8,128)} collective-permute-done((s32[32,3072]{1,0:T(8,128)}, s32[32,3072]{1,0:T(8,128)}, u32[]{:S(2)}, u32[]{:S(2)}) %collective-permute-start.4) | collective-permute-done | bytes 393248 | tf_op jit(solution)/shard_map/ppermute | solution.py:355
  35.2 4.8 %all-to-all-done.pieces_ref = f32[16,2,32,256]{3,2,1,0:T(8,128)} async-done(((f32[16,2,32,256]{3,2,1,0:T(8,128)}), f32[16,2,32,256]{3,2,1,0:T(8,128)}, u32[]{:S(2)}, u32[]{:S(2)}) %all-to-all-start) | async-done | bytes 1048608 | tf_op jit(solution)/shard_map/all_to_all | solution.py:354
  40.0 0.0 copy-done
  40.0 0.0 copy-start.2
  40.0 1.0 copy-done.2
  41.0 27.3 %code_sums.1 = (f32[64,8,384]{2,1,0:T(8,128)S(1)}, f32[64,8,384]{2,1,0:T(8,128)S(1)}) custom-call(s32[3]{0:T(128)S(1)} %pad_add_fusion.place_ref, f32[3072,256]{1,0:T(8,128)S(1)} %copy-done, f32[16,2,32,256]{3,2,1,0:T(8,128)} %all-to-all-done.pieces_ref, s32[32,3072]{1,0:T(8,128)S(1)} %copy-done.2, s32[32,3072]{1,0:T(8,128)} %collective-permute-done.2.c1, ...), custom_call_target="tpu_custom_call" | custom-call | tf_op jit(solution)/shard_map/code_sums/pallas_call | solution.py:157
  68.3 0.0 copy-done.4
  68.3 3.3 %collective-permute-start.5 = (f32[64,8,384]{2,1,0:T(8,128)S(1)}, f32[64,8,384]{2,1,0:T(8,128)S(1)}, u32[]{:S(2)}, u32[]{:S(2)}) collective-permute-start(f32[64,8,384]{2,1,0:T(8,128)S(1)} %get-tuple-element.15), channel_id=1, source_target_pairs={{0,4},{4,0},{1,5},{5,1},{2,6},{6,2},{3,7},{7,3},{8,12},{12,8},{9,1... | collective-permute-start | bytes 2359304 | tf_op jit(solution)/shard_map/ppermute | solution.py:53
  71.6 1.9 collective-permute-done.5
  73.5 0.1 add.18
  73.6 0.0 copy-start.3
  73.6 20.4 %all_to_all.25 = f32[64,8,384]{2,1,0:T(8,128)} all-to-all(f32[64,8,384]{2,1,0:T(8,128)S(1)} %add.18), channel_id=1, replica_groups=mesh['x'=4,'z'=4,'core'=2,'y'=4] {'y','x','z'}, dimensions={0} | all-to-all | bytes 1572864 | tf_op jit(solution)/shard_map/all_to_all | solution.py:360
  94.0 1.2 reduce_sum.18
  95.3 15.8 %all_to_all.26.mine_ref = f32[64,8,256]{2,1,0:T(8,128)S(1)} all-to-all(f32[64,8,256]{2,1,0:T(8,128)S(1)} %broadcast_in_dim.7), channel_id=1, replica_groups=mesh['x'=4,'z'=4,'core'=2,'y'=4] {'y','x','z'}, dimensions={0} | all-to-all | bytes 1048576 | tf_op jit(solution)/shard_map/all_to_all | solution.py:49
  111.1 3.1 %collective-permute-start.6 = (f32[64,8,256]{2,1,0:T(8,128)S(1)}, f32[64,8,256]{2,1,0:T(8,128)S(1)}, u32[]{:S(2)}, u32[]{:S(2)}) collective-permute-start(f32[64,8,256]{2,1,0:T(8,128)S(1)} %all_to_all.26.mine_ref), channel_id=1, source_target_pairs={{0,4},{4,0},{1,5},{5,1},{2,6},{6,2},{3,7},{7,3},{8,12},{12,8},{9,1... | collective-permute-start | bytes 1572872 | tf_op jit(solution)/shard_map/ppermute | solution.py:53
  114.2 1.5 collective-permute-done.6.other_ref
  115.7 0.0 copy-done.3
  115.7 1.0 copy-done.5
  116.7 20.8 %cross_part.1 = (f32[16,32,256]{2,1,0:T(8,128)S(1)}, f32[16,32,256]{2,1,0:T(8,128)S(1)}) custom-call(s32[3]{0:T(128)S(1)} %pad_add_fusion.place_ref, f32[3072,256]{1,0:T(8,128)S(1)} %copy-done, f32[64,8,256]{2,1,0:T(8,128)S(1)} %all_to_all.26.mine_ref, f32[64,8,256]{2,1,0:T(8,128)S(1)} %collective-permute-done.6.other_ref, s32[32,3072]{1,0:T(8,128)S(1)} %copy-done.3, ...), custom_call_target="tpu_custom_call" | custom-call | tf_op jit(solution)/shard_map/cross_part/pallas_call | solution.py:242
  137.5 0.0 copy-done.1
  137.5 0.0 copy-done.6
  137.5 0.5 collective-permute-start.7
  138.0 1.5 collective-permute-done.7
  139.5 0.1 add.19
  139.6 13.1 %all_to_all.27 = f32[16,32,256]{2,1,0:T(8,128)S(1)} all-to-all(f32[16,32,256]{2,1,0:T(8,128)S(1)} %add.19), channel_id=1, replica_groups=mesh['x'=4,'z'=4,'core'=2,'y'=4] {'x','z'}, dimensions={0} | all-to-all | bytes 1048576 | tf_op jit(solution)/shard_map/all_to_all | solution.py:367
  152.7 1.6 broadcast_in_dim.8
  154.3 5.4 %all-to-all-start.4 = ((f32[64,32,256]{2,1,0:T(8,128)}), f32[64,32,256]{2,1,0:T(8,128)S(1)}, u32[]{:S(2)}, u32[]{:S(2)}) async-start(f32[64,32,256]{2,1,0:T(8,128)} %broadcast_in_dim.8), calls=%async_computation.4 | async-start | bytes 4194304 | tf_op jit(solution)/shard_map/all_to_all | solution.py:49
  159.7 1.0 select_bitcast_fusion.1
  160.7 2.6 %copy.5 = f32[16,2,256,8]{3,2,1,0:T(8,128)} copy(f32[16,2,256,8]{2,3,0,1:T(8,128)S(1)} %maximum_bitcast_fusion) | data formatting | bytes 524288 | tf_op jit(solution)/shard_map/transpose | solution.py:372
  163.3 4.6 %reshape.20 = f32[32,2048]{1,0:T(8,128)} reshape(f32[16,2,256,8]{3,2,1,0:T(8,128)} %copy.5) | data formatting | bytes 524288 | tf_op jit(solution)/shard_map/reshape | solution.py:372
  168.0 18.5 %all-to-all-done.4.mine_ref = f32[64,32,256]{2,1,0:T(8,128)S(1)} async-done(((f32[64,32,256]{2,1,0:T(8,128)}), f32[64,32,256]{2,1,0:T(8,128)S(1)}, u32[]{:S(2)}, u32[]{:S(2)}) %all-to-all-start.4) | async-done | bytes 2097184 | tf_op jit(solution)/shard_map/all_to_all | solution.py:49
  186.5 3.7 %collective-permute-start.8 = (f32[64,32,256]{2,1,0:T(8,128)S(1)}, f32[64,32,256]{2,1,0:T(8,128)S(1)}, u32[]{:S(2)}, u32[]{:S(2)}) collective-permute-start(f32[64,32,256]{2,1,0:T(8,128)S(1)} %all-to-all-done.4.mine_ref), channel_id=1, source_target_pairs={{0,4},{4,0},{1,5},{5,1},{2,6},{6,2},{3,7},{7,3},{8,12},{12,8},{9,1... | collective-permute-start | bytes 6291464 | tf_op jit(solution)/shard_map/ppermute | solution.py:53
  190.2 3.8 %collective-permute-done.8.other_ref = f32[64,32,256]{2,1,0:T(8,128)S(1)} collective-permute-done((f32[64,32,256]{2,1,0:T(8,128)S(1)}, f32[64,32,256]{2,1,0:T(8,128)S(1)}, u32[]{:S(2)}, u32[]{:S(2)}) %collective-permute-start.8) | collective-permute-done | bytes 2097184 | tf_op jit(solution)/shard_map/ppermute | solution.py:53
  194.0 61.0 %newton_schulz.1 = f32[32,256]{1,0:T(8,128)} custom-call(s32[3]{0:T(128)S(1)} %pad_add_fusion.place_ref, f32[64,32,256]{2,1,0:T(8,128)S(1)} %all-to-all-done.4.mine_ref, f32[64,32,256]{2,1,0:T(8,128)S(1)} %collective-permute-done.8.other_ref), custom_call_target="tpu_custom_call" | custom-call | tf_op jit(solution)/shard_map/newton_schulz/pallas_call | solution.py:324
  (9 shorter events, 0.1 us)
Async XLA Ops:
  0.6 39.4 %copy-start = (f32[3072,256]{1,0:T(8,128)S(1)}, f32[3072,256]{1,0:T(8,128)}, u32[]{:S(2)}) copy-start(f32[3072,256]{1,0:T(8,128)} %pts_ref.3) | copy-start | bytes 9437188
  0.6 11.9 %collective-permute-start.3 = (s32[32,3072]{1,0:T(8,128)}, s32[32,3072]{1,0:T(8,128)S(1)}, u32[]{:S(2)}, u32[]{:S(2)}) collective-permute-start(s32[32,3072]{1,0:T(8,128)} %c0.3), channel_id=1, source_target_pairs={{0,3},{1,0},{2,1},{3,2},{4,7},{5,4},{6,5},{7,6},{8,11},{9,8},{10,9... | collective-permute-start | bytes 1179656 | tf_op jit(solution)/shard_map/ppermute | solution.py:347
  4.3 11.2 %collective-permute-start.2 = (s32[32,3072]{1,0:T(8,128)}, s32[32,3072]{1,0:T(8,128)}, u32[]{:S(2)}, u32[]{:S(2)}) collective-permute-start(s32[32,3072]{1,0:T(8,128)} %c0.3), channel_id=1, source_target_pairs={{0,1},{1,2},{2,3},{3,0},{4,5},{5,6},{6,7},{7,4},{8,9},{9,10},{10,1... | collective-permute-start | bytes 1179656 | tf_op jit(solution)/shard_map/ppermute | solution.py:346
  4.3 1.4 collective-permute-start
  5.7 1.8 collective-permute-start.1
  12.6 55.7 %copy-start.4 = (s32[32,3072]{1,0:T(8,128)}, s32[32,3072]{1,0:T(8,128)S(1)}, u32[]{:S(2)}) copy-start(s32[32,3072]{1,0:T(8,128)S(1)} %collective-permute-done.3.c3) | copy-start | bytes 1179652
  16.6 23.4 %all-to-all-start = ((f32[16,2,32,256]{3,2,1,0:T(8,128)}), f32[16,2,32,256]{3,2,1,0:T(8,128)}, u32[]{:S(2)}, u32[]{:S(2)}) async-start(f32[16,2,32,256]{3,2,1,0:T(8,128)} %broadcast_in_dim.6), calls=%async_computation | async-start | bytes 2097152 | tf_op jit(solution)/shard_map/all_to_all | solution.py:354
  25.0 10.2 %collective-permute-start.4 = (s32[32,3072]{1,0:T(8,128)}, s32[32,3072]{1,0:T(8,128)}, u32[]{:S(2)}, u32[]{:S(2)}) collective-permute-start(s32[32,3072]{1,0:T(8,128)} %collective-permute-done.2.c1), channel_id=1, source_target_pairs={{0,1},{1,2},{2,3},{3,0},{4,5},{5,6},{6,7},{7,4},{8,9},{9,10},{10,1... | collective-permute-start | bytes 1179656 | tf_op jit(solution)/shard_map/ppermute | solution.py:355
  40.0 1.0 copy-start.2
  68.3 5.2 %collective-permute-start.5 = (f32[64,8,384]{2,1,0:T(8,128)S(1)}, f32[64,8,384]{2,1,0:T(8,128)S(1)}, u32[]{:S(2)}, u32[]{:S(2)}) collective-permute-start(f32[64,8,384]{2,1,0:T(8,128)S(1)} %get-tuple-element.15), channel_id=1, source_target_pairs={{0,4},{4,0},{1,5},{5,1},{2,6},{6,2},{3,7},{7,3},{8,12},{12,8},{9,1... | collective-permute-start | bytes 2359304 | tf_op jit(solution)/shard_map/ppermute | solution.py:53
  73.6 42.2 %copy-start.3 = (s32[32,3072]{1,0:T(8,128)S(1)}, s32[32,3072]{1,0:T(8,128)}, u32[]{:S(2)}) copy-start(s32[32,3072]{1,0:T(8,128)} %c0.3) | copy-start | bytes 1179652
  111.1 26.4 %copy-start.1 = (f32[64,8,256]{2,1,0:T(8,128)}, f32[64,8,256]{2,1,0:T(8,128)S(1)}, u32[]{:S(2)}) copy-start(f32[64,8,256]{2,1,0:T(8,128)S(1)} %all_to_all.26.mine_ref) | copy-start | bytes 1572868
  111.1 4.6 %collective-permute-start.6 = (f32[64,8,256]{2,1,0:T(8,128)S(1)}, f32[64,8,256]{2,1,0:T(8,128)S(1)}, u32[]{:S(2)}, u32[]{:S(2)}) collective-permute-start(f32[64,8,256]{2,1,0:T(8,128)S(1)} %all_to_all.26.mine_ref), channel_id=1, source_target_pairs={{0,4},{4,0},{1,5},{5,1},{2,6},{6,2},{3,7},{7,3},{8,12},{12,8},{9,1... | collective-permute-start | bytes 1572872 | tf_op jit(solution)/shard_map/ppermute | solution.py:53
  115.7 1.0 copy-start.5
  116.7 20.8 %copy-start.6 = (f32[64,8,256]{2,1,0:T(8,128)}, f32[64,8,256]{2,1,0:T(8,128)S(1)}, u32[]{:S(2)}) copy-start(f32[64,8,256]{2,1,0:T(8,128)S(1)} %collective-permute-done.6.other_ref) | copy-start | bytes 1572868
  137.5 2.0 collective-permute-start.7
  154.3 32.2 %all-to-all-start.4 = ((f32[64,32,256]{2,1,0:T(8,128)}), f32[64,32,256]{2,1,0:T(8,128)S(1)}, u32[]{:S(2)}, u32[]{:S(2)}) async-start(f32[64,32,256]{2,1,0:T(8,128)} %broadcast_in_dim.8), calls=%async_computation.4 | async-start | bytes 4194304 | tf_op jit(solution)/shard_map/all_to_all | solution.py:49
  186.5 7.5 %collective-permute-start.8 = (f32[64,32,256]{2,1,0:T(8,128)S(1)}, f32[64,32,256]{2,1,0:T(8,128)S(1)}, u32[]{:S(2)}, u32[]{:S(2)}) collective-permute-start(f32[64,32,256]{2,1,0:T(8,128)S(1)} %all-to-all-done.4.mine_ref), channel_id=1, source_target_pairs={{0,4},{4,0},{1,5},{5,1},{2,6},{6,2},{3,7},{7,3},{8,12},{12,8},{9,1... | collective-permute-start | bytes 6291464 | tf_op jit(solution)/shard_map/ppermute | solution.py:53

commit v6 on v5

--- a/solution.py
+++ b/solution.py
@@ -1,3 +1,5 @@
+import functools
+
 import jax
 import jax.numpy as jnp
 from jax import lax
@@ -18,6 +20,7 @@
 NT = (((1,), (1,)), ((), ()))
 VMEM = pl.BlockSpec(memory_space=pltpu.VMEM)
 SMEM = pl.BlockSpec(memory_space=pltpu.SMEM)
+ANY = pl.BlockSpec(memory_space=pl.ANY)
 
 
 def grant(mebibytes):
@@ -53,33 +56,39 @@
     return lax.ppermute(value, "core", [(0, 1), (1, 0)])
 
 
+def shift(value, by):
+    return lax.ppermute(value, "y", [(s, (s + by) % 4) for s in range(4)])
+
+
 def at8(index):
     return pl.ds(pl.multiple_of(index * 8, 8), 8)
 
 
-def place_codes(where, y, c0, c1, c2, c3):
-    for i, codes_ref in enumerate((c0, c1, c2, c3)):
-        block = lax.rem(y + 4 - i, 4)
-        where[pl.ds(pl.multiple_of(block * 32, 32), 32), :] = codes_ref[...]
+def fetch_codes(y, codes_ref, sources, arrived):
+    places = ((0, 0), (1, 0), (1, 1), (2, 0), (2, 1), (3, 0), (3, 1))
+    copies = []
+    for number, (source, (back, half)) in enumerate(zip(sources, places, strict=True)):
+        first = pl.multiple_of(lax.rem(y + 4 - back, 4) * 32 + half * 16, 16)
+        target = codes_ref.at[pl.ds(first, source.shape[0]), :]
+        copies.append(pltpu.make_async_copy(source, target, arrived.at[number]))
+    for copy in copies:
+        copy.start()
+    return copies
 
 
 def sums_kernel(
-    place_ref, pts_ref, pieces_ref, c0, c1, c2, c3,
-    keep_ref, give_ref, codes_ref, panel_ref, rotated_ref, ph_ref, pl_ref,
+    place_ref, pts_ref, pieces_ref, c0, c1a, c1b, c2a, c2b, c3a, c3b,
+    keep_ref, give_ref, codes_ref, ph_ref, pl_ref, panel_ref, rotated_ref, arrived,
 ):
     count = pts_ref.shape[0]
     y, core = place_ref[0], place_ref[1]
-    place_codes(codes_ref, y, c0, c1, c2, c3)
+    copies = fetch_codes(y, codes_ref, (c0, c1a, c1b, c2a, c2b, c3a, c3b), arrived)
     ph, plo = split(pts_ref[...])
     ph_ref[...] = ph
     pl_ref[...] = plo
     for a in range(4):
-        for z in range(4):
-            columns = slice(a * 256, a * 256 + 256)
-            first = pl.multiple_of(z * 64 + core * 32, 32)
-            second = pl.multiple_of(z * 64 + (1 - core) * 32, 32)
-            panel_ref[pl.ds(first, 32), columns] = pieces_ref[a * 4 + z, 0]
-            panel_ref[pl.ds(second, 32), columns] = pieces_ref[a * 4 + z, 1]
+        for part in range(8):
+            panel_ref[part * 32 : part * 32 + 32, a * 256 : a * 256 + 256] = pieces_ref[a * 8 + part]
 
     def rotate(j, carry):
         panel = panel_ref[:, pl.ds(pl.multiple_of(j * 256, 256), 256)].T
@@ -89,6 +98,8 @@
         return carry
 
     lax.fori_loop(0, D // 256, rotate, 0)
+    for copy in copies:
+        copy.wait()
 
     step = 512
     rows16 = lax.broadcasted_iota(jnp.int32, (16, step), 0).astype(F32)
@@ -105,8 +116,8 @@
             even = pltpu.roll(even, 64, axis=1)
         return jnp.where(lane < 64, even, odd)
 
-    def group(eight, quad):
-        total = jnp.zeros((288, 256), F32)
+    def group(eight, quad, counted):
+        total = jnp.zeros((288 if counted else 256, 256), F32)
         for n in range(0, count, step):
             lefts, rights = [], []
             rows = codes_ref[at8(eight), n : n + step]
@@ -120,22 +131,25 @@
                 for t in range(4):
                     lefts.append(jnp.where(top == tops[t], both, zero))
                     rights.append(jnp.where(low == marks[t], one, zero))
-            tall = (rows >> 6).astype(F32)
-            tall = jnp.concatenate([tall, tall], axis=0).astype(BF16)
-            for t in range(2):
-                pattern = jnp.where(rows16 < 8, 2.0 * t, 2.0 * t + 1.0).astype(BF16)
-                lefts.append(jnp.where(tall == pattern, one, zero))
+            if counted:
+                tall = (rows >> 6).astype(F32)
+                tall = jnp.concatenate([tall, tall], axis=0).astype(BF16)
+                for t in range(2):
+                    pattern = jnp.where(rows16 < 8, 2.0 * t, 2.0 * t + 1.0).astype(BF16)
+                    lefts.append(jnp.where(tall == pattern, one, zero))
             total += mxu(jnp.concatenate(lefts, axis=0), jnp.concatenate(rights, axis=0), NT)
         found = []
         for mm in range(4):
             columns = slice((mm // 2) * 128, (mm // 2) * 128 + 128)
             slab = total[mm * 64 : mm * 64 + 64, columns]
             parts = [slab[t * 16 : t * 16 + 8] + slab[t * 16 + 8 : t * 16 + 16] for t in range(4)]
-            tally = [total[256 + t * 8 : 264 + t * 8, columns] for t in range(4)]
             halves = [pick(parts[2 * h], parts[2 * h + 1], mm) for h in range(2)]
-            r = quad * 4 + mm
-            ticks = [pick(tally[2 * h], tally[2 * h + 1], mm)[r : r + 1] for h in range(2)]
-            ticks = jnp.concatenate(ticks + [jnp.zeros((6, 128), F32)], axis=0)
+            ticks = jnp.zeros((SUB, 128), F32)
+            if counted:
+                r = quad * 4 + mm
+                tally = [total[256 + t * 8 : 264 + t * 8, columns] for t in range(4)]
+                ticks = [pick(tally[2 * h], tally[2 * h + 1], mm)[r : r + 1] for h in range(2)]
+                ticks = jnp.concatenate(ticks + [jnp.zeros((6, 128), F32)], axis=0)
             found.append(jnp.concatenate(halves + [ticks], axis=1))
         for h in range(2):
             even, odd = found[2 * h], found[2 * h + 1]
@@ -143,12 +157,14 @@
             keep_ref[q] = jnp.where(core == 0, even, odd)
             give_ref[q] = jnp.where(core == 0, odd, even)
 
-    def eight_rows(eight, carry):
-        group(eight, 0)
-        group(eight, 1)
+    def eight_rows(i, carry, counted):
+        eight = lax.rem(y * 4 + i, M // 8)
+        group(eight, 0, counted)
+        group(eight, 1, counted)
         return carry
 
-    lax.fori_loop(0, M // 8, eight_rows, 0)
+    lax.fori_loop(0, 4, functools.partial(eight_rows, counted=True), 0)
+    lax.fori_loop(4, M // 8, functools.partial(eight_rows, counted=False), 0)
 
 
 def code_sums(place, points, pieces, codes):
@@ -157,32 +173,36 @@
     return pl.pallas_call(
         sums_kernel,
         out_shape=(half, half),
-        in_specs=[SMEM] + [VMEM] * 6,
+        in_specs=[SMEM, VMEM, VMEM] + [ANY] * len(codes),
         out_specs=(VMEM, VMEM),
         scratch_shapes=[
             pltpu.VMEM((M, count), jnp.int32),
+            pltpu.VMEM((count, 256), BF16),
+            pltpu.VMEM((count, 256), BF16),
             pltpu.VMEM((256, D), F32),
             pltpu.VMEM((M, SUB, count), F32),
-            pltpu.VMEM((count, 256), BF16),
-            pltpu.VMEM((count, 256), BF16),
+            pltpu.SemaphoreType.DMA((len(codes),)),
         ],
-        compiler_params=grant(36),
+        compiler_params=grant(34),
         name="code_sums",
     )(place, points, pieces, *codes)
 
 
 def cross_kernel(
-    place_ref, pts_ref, mine_ref, other_ref, c0, c1, c2, c3,
-    keep_ref, give_ref, codes_ref, tab_ref, ah0_ref, al0_ref, ah1_ref, al1_ref, ph_ref, pl_ref, acc_ref,
+    place_ref, pts_ref, mine_ref, other_ref, c0, c1a, c1b, c2a, c2b, c3a, c3b,
+    keep_ref, give_ref,
+    codes_ref, ph_ref, pl_ref, tab_ref, ah0_ref, al0_ref, ah1_ref, al1_ref, acc_ref, arrived,
 ):
     count = pts_ref.shape[0]
     y, core = place_ref[0], place_ref[1]
-    place_codes(codes_ref, y, c0, c1, c2, c3)
+    copies = fetch_codes(y, codes_ref, (c0, c1a, c1b, c2a, c2b, c3a, c3b), arrived)
     tab_ref[core] = mine_ref[...]
     tab_ref[1 - core] = other_ref[...]
     ph, plo = split(pts_ref[...])
     ph_ref[...] = ph
     pl_ref[...] = plo
+    for copy in copies:
+        copy.wait()
     wide = 1024
     quarter = count // 4
 
@@ -242,18 +262,19 @@
     return pl.pallas_call(
         cross_kernel,
         out_shape=(half, half),
-        in_specs=[SMEM] + [VMEM] * 7,
+        in_specs=[SMEM] + [VMEM] * 3 + [ANY] * len(codes),
         out_specs=(VMEM, VMEM),
         scratch_shapes=[
             pltpu.VMEM((M, count), jnp.int32),
+            pltpu.VMEM((count, 256), BF16),
+            pltpu.VMEM((count, 256), BF16),
             pltpu.VMEM((2, M // 2, SUB, K), F32),
             pltpu.VMEM((256, count), BF16),
             pltpu.VMEM((256, count), BF16),
             pltpu.VMEM((256, count), BF16),
             pltpu.VMEM((256, count), BF16),
-            pltpu.VMEM((count, 256), BF16),
-            pltpu.VMEM((count, 256), BF16),
             pltpu.VMEM((256, 256), F32),
+            pltpu.SemaphoreType.DMA((len(codes),)),
         ],
         compiler_params=grant(28),
         name="cross_part",
@@ -343,22 +364,21 @@
     y, core = lax.axis_index("y"), lax.axis_index("core")
     own_row = lax.axis_index(ROWS)
     place = jnp.stack([y, core, own_row]).astype(jnp.int32)
-    one = lax.ppermute(codes, "y", [(s, (s + 1) % 4) for s in range(4)])
-    three = lax.ppermute(codes, "y", [(s, (s + 3) % 4) for s in range(4)])
+    upper, lower = codes[:16], codes[16:]
+    one_a, three_a = shift(upper, 1), shift(upper, 3)
     swapped = lax.ppermute(
         rotation, ("x", "y"), [(a * 4 + b, b * 4 + a) for a in range(4) for b in range(4)]
     )
-    pieces = jnp.stack([swapped, swap_core(swapped)])
-    pieces = jnp.broadcast_to(pieces[None], (16,) + pieces.shape)
-    pieces, one, three = lax.optimization_barrier((pieces, one, three))
-    pieces = lax.all_to_all(pieces, ("x", "z"), 0, 0, tiled=True)
-    two = lax.ppermute(one, "y", [(s, (s + 1) % 4) for s in range(4)])
-    all_codes = [codes, one, two, three]
+    swapped, one_a, three_a = lax.optimization_barrier((swapped, one_a, three_a))
+    pieces = spread_to(swapped, ROWS, 32)
+    one_b, three_b = shift(lower, 1), shift(lower, 3)
+    two_a, two_b = shift(one_a, 1), shift(three_b, 3)
+    all_codes = [codes, one_a, one_b, two_a, two_b, three_a, three_b]
     keep, give = code_sums(place, points, pieces, all_codes)
 
     sums = keep + swap_core(give)
     sums = jnp.sum(lax.all_to_all(sums, CHIPS, 0, 0, tiled=True), axis=0)
-    counts = 0.25 * sums[:2, K:].reshape(1, K)
+    counts = sums[:2, K:].reshape(1, K)
     centers = spread_to(sums[:, :K] / counts, CHIPS, 64)
     others = swap_core(centers)
 

time: 256 us -> 258 us (level)
  waiting for transfers between devices: 50.9 us -> 44.7 us
  starting transfers between devices: 30.4 us -> 35.7 us
    all_to_all x1 -> x2, starting transfers between devices: 5.37 us -> 18.2 us  [spread_to(): return lax.all_to_all(copies, axes, 0, 0, tiled=True)]
    all_to_all x1 -> x0, starting transfers between devices: 8.45 us -> none  [shards(): pieces = lax.all_to_all(pieces, ('x', 'z'), 0, 0, tiled=True)]
    all_to_all x1 -> x0, waiting for transfers between devices: 4.79 us -> none  [shards(): pieces = lax.all_to_all(pieces, ('x', 'z'), 0, 0, tiled=True)]
    ppermute x3 -> x6, starting transfers between devices: 3.71 us -> 7.72 us  [shift(): return lax.ppermute(value, 'y', [(s, (s + by) % 4) for s in range(4)])]
    ppermute x5 -> x4, starting transfers between devices: 11.5 us -> 8.44 us  [swap_core(): return lax.ppermute(value, 'core', [(0, 1), (1, 0)])]
    ppermute x3 -> x6, waiting for transfers between devices: 17.9 us -> 16.1 us  [shift(): return lax.ppermute(value, 'y', [(s, (s + by) % 4) for s in range(4)])]
    all_to_all x1 -> x2, waiting for transfers between devices: 18.5 us -> 19.8 us  [spread_to(): return lax.all_to_all(copies, axes, 0, 0, tiled=True)]
    ppermute x5 -> x4, waiting for transfers between devices: 9.63 us -> 8.77 us  [swap_core(): return lax.ppermute(value, 'core', [(0, 1), (1, 0)])]
  transfers between devices with their start and end apart: 11 -> 13, of which waited for: 10 -> 11; matrix products, arithmetic and copies ran while one was open for 3% -> 3% of each run, Pallas kernels for 0% -> 0%
where the time goes in v6:
time: 258 us; the launch traced here: 257 us
  Pallas kernels  108 us (42%)
  blocking collectives  51.2 us (20%)
  waiting for transfers between devices  44.7 us (17%)
  starting transfers between devices  35.7 us (14%)
  local copies, waits for them, and re-layouts  14.4 us (6%)
    pallas_call x1, Pallas kernels, newton_schulz(): pl.pallas_call(iterate_kernel, out_shape=jax.ShapeDtypeStruct((32, 256),...  61 us
    pallas_call x1, Pallas kernels, code_sums(): pl.pallas_call(sums_kernel, out_shape=(half, half), in_specs=[SMEM, VMEM,...  26.1 us
    all_to_all x1, blocking collectives, shards(): sums = jnp.sum(lax.all_to_all(sums, CHIPS, 0, 0, tiled=True), axis=0)  22.4 us
    pallas_call x1, Pallas kernels, cross_part(): pl.pallas_call(cross_kernel, out_shape=(half, half), in_specs=[SMEM] + [V...  20.9 us
    all_to_all x2, waiting for transfers between devices, spread_to(): return lax.all_to_all(copies, axes, 0, 0, tiled=True)  19.8 us
    all_to_all x2, starting transfers between devices, spread_to(): return lax.all_to_all(copies, axes, 0, 0, tiled=True)  18.2 us
    ppermute x6, waiting for transfers between devices, shift(): return lax.ppermute(value, 'y', [(s, (s + by) % 4) for s in range(4)])  16.1 us
    all_to_all x1, blocking collectives, spread_to(): return lax.all_to_all(copies, axes, 0, 0, tiled=True)  15.8 us
  transfers between devices with their start and end apart: 13, of which 11 were waited for; matrix products, arithmetic and copies ran while one was open for 3% of the time, Pallas kernels for 0%

profile of v6, /device:TPU:1, one launch (start us, length us, event | category | flops | bytes accessed | tf_op | source)
XLA Modules:
  0.0 257.4 jit_solution(14545905081913436694)
XLA Ops:
  0.6 0.0 copy-start.1
  0.6 1.9 fusion
  2.5 3.6 %collective-permute-start.2 = (s32[16,3072]{1,0:T(8,128)S(1)}, s32[16,3072]{1,0:T(8,128)S(1)}, u32[]{:S(2)}, u32[]{:S(2)}) collective-permute-start(s32[16,3072]{1,0:T(8,128)S(1)} %get-tuple-element.23), channel_id=1, source_target_pairs={{0,3},{1,0},{2,1},{3,2},{4,7},{5,4},{6,5},{7,6},{8,11},{9,8},{10,9... | collective-permute-start | bytes 589832 | tf_op jit(solution)/shard_map/ppermute | solution.py:60
  6.1 0.0 collective-permute-start.1
  6.1 1.4 collective-permute-start
  7.5 0.0 collective-permute-done
  7.5 2.2 collective-permute-done.2.c3a
  9.7 0.7 copy-done.4
  10.3 2.5 collective-permute-done.1.c1a
  12.9 1.1 broadcast_in_dim.6
  14.0 12.8 %all-to-all-start = ((f32[32,32,256]{2,1,0:T(8,128)}), f32[32,32,256]{2,1,0:T(8,128)}, u32[]{:S(2)}, u32[]{:S(2)}) async-start(f32[32,32,256]{2,1,0:T(8,128)} %broadcast_in_dim.6), calls=%async_computation | async-start | bytes 2097152 | tf_op jit(solution)/shard_map/all_to_all | solution.py:52
  26.8 1.5 collective-permute-start.5
  28.2 0.1 collective-permute-start.3
  28.3 5.0 %collective-permute-done.5.c3b = s32[16,3072]{1,0:T(8,128)} collective-permute-done((s32[16,3072]{1,0:T(8,128)}, s32[16,3072]{1,0:T(8,128)}, u32[]{:S(2)}, u32[]{:S(2)}) %collective-permute-start.5) | collective-permute-done | bytes 196640 | tf_op jit(solution)/shard_map/ppermute | solution.py:60
  33.3 2.6 %collective-permute-start.6 = (s32[16,3072]{1,0:T(8,128)}, s32[16,3072]{1,0:T(8,128)}, u32[]{:S(2)}, u32[]{:S(2)}) collective-permute-start(s32[16,3072]{1,0:T(8,128)} %collective-permute-done.5.c3b), channel_id=1, source_target_pairs={{0,3},{1,0},{2,1},{3,2},{4,7},{5,4},{6,5},{7,6},{8,11},{9,8},{10,9... | collective-permute-start | bytes 589832 | tf_op jit(solution)/shard_map/ppermute | solution.py:60
  36.0 0.0 collective-permute-start.4
  36.0 0.1 pad_add_fusion.place_ref
  36.0 0.0 collective-permute-done.3.c1b
  36.0 3.3 %collective-permute-done.6.c2b = s32[16,3072]{1,0:T(8,128)} collective-permute-done((s32[16,3072]{1,0:T(8,128)}, s32[16,3072]{1,0:T(8,128)}, u32[]{:S(2)}, u32[]{:S(2)}) %collective-permute-start.6) | collective-permute-done | bytes 196640 | tf_op jit(solution)/shard_map/ppermute | solution.py:60
  39.3 3.1 %collective-permute-done.4.c2a = s32[16,3072]{1,0:T(8,128)} collective-permute-done((s32[16,3072]{1,0:T(8,128)}, s32[16,3072]{1,0:T(8,128)}, u32[]{:S(2)}, u32[]{:S(2)}) %collective-permute-start.4) | collective-permute-done | bytes 196640 | tf_op jit(solution)/shard_map/ppermute | solution.py:60
  42.5 1.3 all-to-all-done.pieces_ref
  43.7 0.9 copy-done.5
  44.7 26.1 %code_sums.1 = (f32[64,8,384]{2,1,0:T(8,128)S(1)}, f32[64,8,384]{2,1,0:T(8,128)S(1)}) custom-call(s32[3]{0:T(128)S(1)} %pad_add_fusion.place_ref, f32[3072,256]{1,0:T(8,128)S(1)} %copy-done, f32[32,32,256]{2,1,0:T(8,128)} %all-to-all-done.pieces_ref, s32[32,3072]{1,0:T(8,128)S(1)} %copy-done.1, s32[16,3072]{1,0:T(8,128)} %collective-permute-done.1.c1a, ...), custom_call_target="tpu_custom_call" | custom-call | tf_op jit(solution)/shard_map/code_sums/pallas_call | solution.py:173
  70.7 1.2 collective-permute-start.7
  71.9 1.9 collective-permute-done.7
  73.8 0.1 add.18
  73.9 22.4 %all_to_all.25 = f32[64,8,384]{2,1,0:T(8,128)} all-to-all(f32[64,8,384]{2,1,0:T(8,128)S(1)} %add.18), channel_id=1, replica_groups=mesh['x'=4,'z'=4,'core'=2,'y'=4] {'y','x','z'}, dimensions={0} | all-to-all | bytes 1572864 | tf_op jit(solution)/shard_map/all_to_all | solution.py:380
  96.2 1.2 reduce_sum.18
  97.5 15.8 %all_to_all.26.mine_ref = f32[64,8,256]{2,1,0:T(8,128)S(1)} all-to-all(f32[64,8,256]{2,1,0:T(8,128)S(1)} %broadcast_in_dim.7), channel_id=1, replica_groups=mesh['x'=4,'z'=4,'core'=2,'y'=4] {'y','x','z'}, dimensions={0} | all-to-all | bytes 1048576 | tf_op jit(solution)/shard_map/all_to_all | solution.py:52
  113.3 3.1 %collective-permute-start.8 = (f32[64,8,256]{2,1,0:T(8,128)S(1)}, f32[64,8,256]{2,1,0:T(8,128)S(1)}, u32[]{:S(2)}, u32[]{:S(2)}) collective-permute-start(f32[64,8,256]{2,1,0:T(8,128)S(1)} %all_to_all.26.mine_ref), channel_id=1, source_target_pairs={{0,4},{4,0},{1,5},{5,1},{2,6},{6,2},{3,7},{7,3},{8,12},{12,8},{9,1... | collective-permute-start | bytes 1572872 | tf_op jit(solution)/shard_map/ppermute | solution.py:56
  116.4 1.5 collective-permute-done.8.other_ref
  118.0 0.9 copy-done.6
  118.9 20.9 %cross_part.1 = (f32[16,32,256]{2,1,0:T(8,128)S(1)}, f32[16,32,256]{2,1,0:T(8,128)S(1)}) custom-call(s32[3]{0:T(128)S(1)} %pad_add_fusion.place_ref, f32[3072,256]{1,0:T(8,128)S(1)} %copy-done, f32[64,8,256]{2,1,0:T(8,128)S(1)} %all_to_all.26.mine_ref, f32[64,8,256]{2,1,0:T(8,128)S(1)} %collective-permute-done.8.other_ref, s32[32,3072]{1,0:T(8,128)S(1)} %copy-done.1, ...), custom_call_target="tpu_custom_call" | custom-call | tf_op jit(solution)/shard_map/cross_part/pallas_call | solution.py:262
  139.8 0.0 copy-done.2
  139.8 0.0 copy-done.3
  139.9 0.5 collective-permute-start.9
  140.3 1.5 collective-permute-done.9
  141.8 0.1 add.19
  141.9 13.1 %all_to_all.27 = f32[16,32,256]{2,1,0:T(8,128)S(1)} all-to-all(f32[16,32,256]{2,1,0:T(8,128)S(1)} %add.19), channel_id=1, replica_groups=mesh['x'=4,'z'=4,'core'=2,'y'=4] {'x','z'}, dimensions={0} | all-to-all | bytes 1048576 | tf_op jit(solution)/shard_map/all_to_all | solution.py:387
  155.0 1.6 broadcast_in_dim.8
  156.6 5.4 %all-to-all-start.4 = ((f32[64,32,256]{2,1,0:T(8,128)}), f32[64,32,256]{2,1,0:T(8,128)S(1)}, u32[]{:S(2)}, u32[]{:S(2)}) async-start(f32[64,32,256]{2,1,0:T(8,128)} %broadcast_in_dim.8), calls=%async_computation.4 | async-start | bytes 4194304 | tf_op jit(solution)/shard_map/all_to_all | solution.py:52
  162.0 1.0 select_bitcast_fusion.1
  163.0 2.6 %copy.5 = f32[16,2,256,8]{3,2,1,0:T(8,128)} copy(f32[16,2,256,8]{2,3,0,1:T(8,128)S(1)} %maximum_bitcast_fusion) | data formatting | bytes 524288 | tf_op jit(solution)/shard_map/transpose | solution.py:392
  165.6 4.6 %reshape.12 = f32[32,2048]{1,0:T(8,128)} reshape(f32[16,2,256,8]{3,2,1,0:T(8,128)} %copy.5) | data formatting | bytes 524288 | tf_op jit(solution)/shard_map/reshape | solution.py:392
  170.3 18.6 %all-to-all-done.4.mine_ref = f32[64,32,256]{2,1,0:T(8,128)S(1)} async-done(((f32[64,32,256]{2,1,0:T(8,128)}), f32[64,32,256]{2,1,0:T(8,128)S(1)}, u32[]{:S(2)}, u32[]{:S(2)}) %all-to-all-start.4) | async-done | bytes 2097184 | tf_op jit(solution)/shard_map/all_to_all | solution.py:52
  188.8 3.7 %collective-permute-start.10 = (f32[64,32,256]{2,1,0:T(8,128)S(1)}, f32[64,32,256]{2,1,0:T(8,128)S(1)}, u32[]{:S(2)}, u32[]{:S(2)}) collective-permute-start(f32[64,32,256]{2,1,0:T(8,128)S(1)} %all-to-all-done.4.mine_ref), channel_id=1, source_target_pairs={{0,4},{4,0},{1,5},{5,1},{2,6},{6,2},{3,7},{7,3},{8,12},{12,8},{9,1... | collective-permute-start | bytes 6291464 | tf_op jit(solution)/shard_map/ppermute | solution.py:56
  192.6 3.8 %collective-permute-done.10.other_ref = f32[64,32,256]{2,1,0:T(8,128)S(1)} collective-permute-done((f32[64,32,256]{2,1,0:T(8,128)S(1)}, f32[64,32,256]{2,1,0:T(8,128)S(1)}, u32[]{:S(2)}, u32[]{:S(2)}) %collective-permute-start.10) | collective-permute-done | bytes 2097184 | tf_op jit(solution)/shard_map/ppermute | solution.py:56
  196.4 61.0 %newton_schulz.1 = f32[32,256]{1,0:T(8,128)} custom-call(s32[3]{0:T(128)S(1)} %pad_add_fusion.place_ref, f32[64,32,256]{2,1,0:T(8,128)S(1)} %all-to-all-done.4.mine_ref, f32[64,32,256]{2,1,0:T(8,128)S(1)} %collective-permute-done.10.other_ref), custom_call_target="tpu_custom_call" | custom-call | tf_op jit(solution)/shard_map/newton_schulz/pallas_call | solution.py:345
  (13 shorter events, 0.1 us)
Async XLA Ops:
  0.6 43.1 %copy-start.1 = (s32[32,3072]{1,0:T(8,128)S(1)}, s32[32,3072]{1,0:T(8,128)}, u32[]{:S(2)}) copy-start(s32[32,3072]{1,0:T(8,128)} %c0.3) | copy-start | bytes 1179652
  0.6 43.1 %copy-start = (f32[3072,256]{1,0:T(8,128)S(1)}, f32[3072,256]{1,0:T(8,128)}, u32[]{:S(2)}) copy-start(f32[3072,256]{1,0:T(8,128)} %pts_ref.3) | copy-start | bytes 9437188
  2.5 7.1 %collective-permute-start.2 = (s32[16,3072]{1,0:T(8,128)S(1)}, s32[16,3072]{1,0:T(8,128)S(1)}, u32[]{:S(2)}, u32[]{:S(2)}) collective-permute-start(s32[16,3072]{1,0:T(8,128)S(1)} %get-tuple-element.23), channel_id=1, source_target_pairs={{0,3},{1,0},{2,1},{3,2},{4,7},{5,4},{6,5},{7,6},{8,11},{9,8},{10,9... | collective-permute-start | bytes 589832 | tf_op jit(solution)/shard_map/ppermute | solution.py:60
  6.1 6.8 %collective-permute-start.1 = (s32[16,3072]{1,0:T(8,128)S(1)}, s32[16,3072]{1,0:T(8,128)}, u32[]{:S(2)}, u32[]{:S(2)}) collective-permute-start(s32[16,3072]{1,0:T(8,128)S(1)} %get-tuple-element.23), channel_id=1, source_target_pairs={{0,1},{1,2},{2,3},{3,0},{4,5},{5,6},{6,7},{7,4},{8,9},{9,10},{10,1... | collective-permute-start | bytes 589832 | tf_op jit(solution)/shard_map/ppermute | solution.py:60
  6.1 1.4 collective-permute-start
  9.7 0.7 copy-start.4
  14.0 29.8 %all-to-all-start = ((f32[32,32,256]{2,1,0:T(8,128)}), f32[32,32,256]{2,1,0:T(8,128)}, u32[]{:S(2)}, u32[]{:S(2)}) async-start(f32[32,32,256]{2,1,0:T(8,128)} %broadcast_in_dim.6), calls=%async_computation | async-start | bytes 2097152 | tf_op jit(solution)/shard_map/all_to_all | solution.py:52
  26.8 6.6 %collective-permute-start.5 = (s32[16,3072]{1,0:T(8,128)}, s32[16,3072]{1,0:T(8,128)}, u32[]{:S(2)}, u32[]{:S(2)}) collective-permute-start(s32[16,3072]{1,0:T(8,128)} %get-tuple-element.22), channel_id=1, source_target_pairs={{0,3},{1,0},{2,1},{3,2},{4,7},{5,4},{6,5},{7,6},{8,11},{9,8},{10,9... | collective-permute-start | bytes 589832 | tf_op jit(solution)/shard_map/ppermute | solution.py:60
  28.2 7.8 %collective-permute-start.3 = (s32[16,3072]{1,0:T(8,128)}, s32[16,3072]{1,0:T(8,128)}, u32[]{:S(2)}, u32[]{:S(2)}) collective-permute-start(s32[16,3072]{1,0:T(8,128)} %get-tuple-element.22), channel_id=1, source_target_pairs={{0,1},{1,2},{2,3},{3,0},{4,5},{5,6},{6,7},{7,4},{8,9},{9,10},{10,1... | collective-permute-start | bytes 589832 | tf_op jit(solution)/shard_map/ppermute | solution.py:60
  33.3 6.0 %collective-permute-start.6 = (s32[16,3072]{1,0:T(8,128)}, s32[16,3072]{1,0:T(8,128)}, u32[]{:S(2)}, u32[]{:S(2)}) collective-permute-start(s32[16,3072]{1,0:T(8,128)} %collective-permute-done.5.c3b), channel_id=1, source_target_pairs={{0,3},{1,0},{2,1},{3,2},{4,7},{5,4},{6,5},{7,6},{8,11},{9,8},{10,9... | collective-permute-start | bytes 589832 | tf_op jit(solution)/shard_map/ppermute | solution.py:60
  36.0 6.5 %collective-permute-start.4 = (s32[16,3072]{1,0:T(8,128)}, s32[16,3072]{1,0:T(8,128)}, u32[]{:S(2)}, u32[]{:S(2)}) collective-permute-start(s32[16,3072]{1,0:T(8,128)} %collective-permute-done.1.c1a), channel_id=1, source_target_pairs={{0,1},{1,2},{2,3},{3,0},{4,5},{5,6},{6,7},{7,4},{8,9},{9,10},{10,1... | collective-permute-start | bytes 589832 | tf_op jit(solution)/shard_map/ppermute | solution.py:60
  43.7 0.9 copy-start.5
  70.7 3.1 %collective-permute-start.7 = (f32[64,8,384]{2,1,0:T(8,128)S(1)}, f32[64,8,384]{2,1,0:T(8,128)S(1)}, u32[]{:S(2)}, u32[]{:S(2)}) collective-permute-start(f32[64,8,384]{2,1,0:T(8,128)S(1)} %get-tuple-element.15), channel_id=1, source_target_pairs={{0,4},{4,0},{1,5},{5,1},{2,6},{6,2},{3,7},{7,3},{8,12},{12,8},{9,1... | collective-permute-start | bytes 2359304 | tf_op jit(solution)/shard_map/ppermute | solution.py:56
  113.3 26.5 %copy-start.2 = (f32[64,8,256]{2,1,0:T(8,128)}, f32[64,8,256]{2,1,0:T(8,128)S(1)}, u32[]{:S(2)}) copy-start(f32[64,8,256]{2,1,0:T(8,128)S(1)} %all_to_all.26.mine_ref) | copy-start | bytes 1572868
  113.3 4.6 %collective-permute-start.8 = (f32[64,8,256]{2,1,0:T(8,128)S(1)}, f32[64,8,256]{2,1,0:T(8,128)S(1)}, u32[]{:S(2)}, u32[]{:S(2)}) collective-permute-start(f32[64,8,256]{2,1,0:T(8,128)S(1)} %all_to_all.26.mine_ref), channel_id=1, source_target_pairs={{0,4},{4,0},{1,5},{5,1},{2,6},{6,2},{3,7},{7,3},{8,12},{12,8},{9,1... | collective-permute-start | bytes 1572872 | tf_op jit(solution)/shard_map/ppermute | solution.py:56
  118.0 0.9 copy-start.6
  118.9 21.0 %copy-start.3 = (f32[64,8,256]{2,1,0:T(8,128)}, f32[64,8,256]{2,1,0:T(8,128)S(1)}, u32[]{:S(2)}) copy-start(f32[64,8,256]{2,1,0:T(8,128)S(1)} %collective-permute-done.8.other_ref) | copy-start | bytes 1572868
  139.9 2.0 collective-permute-start.9
  156.6 32.2 %all-to-all-start.4 = ((f32[64,32,256]{2,1,0:T(8,128)}), f32[64,32,256]{2,1,0:T(8,128)S(1)}, u32[]{:S(2)}, u32[]{:S(2)}) async-start(f32[64,32,256]{2,1,0:T(8,128)} %broadcast_in_dim.8), calls=%async_computation.4 | async-start | bytes 4194304 | tf_op jit(solution)/shard_map/all_to_all | solution.py:52
  188.8 7.5 %collective-permute-start.10 = (f32[64,32,256]{2,1,0:T(8,128)S(1)}, f32[64,32,256]{2,1,0:T(8,128)S(1)}, u32[]{:S(2)}, u32[]{:S(2)}) collective-permute-start(f32[64,32,256]{2,1,0:T(8,128)S(1)} %all-to-all-done.4.mine_ref), channel_id=1, source_target_pairs={{0,4},{4,0},{1,5},{5,1},{2,6},{6,2},{3,7},{7,3},{8,12},{12,8},{9,1... | collective-permute-start | bytes 6291464 | tf_op jit(solution)/shard_map/ppermute | solution.py:56

commit v7 on v6

--- a/solution.py
+++ b/solution.py
@@ -27,6 +27,7 @@
     return pltpu.CompilerParams(vmem_limit_bytes=mebibytes * 1024 * 1024)
 
 
+QUARTER = 98304 // 32 // 4
 PAYLOAD = K + 128
 
 
@@ -56,6 +57,10 @@
     return lax.ppermute(value, "core", [(0, 1), (1, 0)])
 
 
+def in_hbm(value):
+    return pltpu.with_memory_space_constraint(value, pltpu.HBM)
+
+
 def shift(value, by):
     return lax.ppermute(value, "y", [(s, (s + by) % 4) for s in range(4)])
 
@@ -65,30 +70,48 @@
 
 
 def fetch_codes(y, codes_ref, sources, arrived):
-    places = ((0, 0), (1, 0), (1, 1), (2, 0), (2, 1), (3, 0), (3, 1))
     copies = []
-    for number, (source, (back, half)) in enumerate(zip(sources, places, strict=True)):
-        first = pl.multiple_of(lax.rem(y + 4 - back, 4) * 32 + half * 16, 16)
-        target = codes_ref.at[pl.ds(first, source.shape[0]), :]
+    for number, source in enumerate(sources):
+        first = pl.multiple_of(lax.rem(y + 4 - number, 4) * 32, 32)
+        target = codes_ref.at[pl.ds(first, 32), :]
         copies.append(pltpu.make_async_copy(source, target, arrived.at[number]))
     for copy in copies:
         copy.start()
     return copies
 
 
+def load_points(i, pts_ref, points_ref, arrived):
+    chunk = pl.ds(pl.multiple_of(i * QUARTER, QUARTER), QUARTER)
+    return pltpu.make_async_copy(pts_ref.at[chunk], points_ref.at[chunk], arrived.at[4 + i])
+
+
+def split_points(i, points_ref, ph_ref, pl_ref):
+    chunk = pl.ds(pl.multiple_of(i * QUARTER, QUARTER), QUARTER)
+    high, low = split(points_ref[chunk])
+    ph_ref[chunk] = high
+    pl_ref[chunk] = low
+
+
 def sums_kernel(
-    place_ref, pts_ref, pieces_ref, c0, c1a, c1b, c2a, c2b, c3a, c3b,
-    keep_ref, give_ref, codes_ref, ph_ref, pl_ref, panel_ref, rotated_ref, arrived,
+    place_ref, pts_ref, first_ref, second_ref, c0, c1, c2, c3,
+    keep_ref, give_ref, codes_ref, points_ref, ph_ref, pl_ref, panel_ref, rotated_ref, arrived,
 ):
     count = pts_ref.shape[0]
     y, core = place_ref[0], place_ref[1]
-    copies = fetch_codes(y, codes_ref, (c0, c1a, c1b, c2a, c2b, c3a, c3b), arrived)
-    ph, plo = split(pts_ref[...])
-    ph_ref[...] = ph
-    pl_ref[...] = plo
+    for i in range(4):
+        load_points(i, pts_ref, points_ref, arrived).start()
+    copies = fetch_codes(y, codes_ref, (c0, c1, c2, c3), arrived)
     for a in range(4):
-        for part in range(8):
-            panel_ref[part * 32 : part * 32 + 32, a * 256 : a * 256 + 256] = pieces_ref[a * 8 + part]
+        for z in range(4):
+            columns = slice(a * 256, a * 256 + 256)
+            ours = pl.multiple_of(z * 64 + core * 32, 32)
+            theirs = pl.multiple_of(z * 64 + (1 - core) * 32, 32)
+            panel_ref[pl.ds(ours, 32), columns] = first_ref[a * 4 + z]
+            panel_ref[pl.ds(theirs, 32), columns] = second_ref[a * 4 + z]
+
+    for i in range(4):
+        load_points(i, pts_ref, points_ref, arrived).wait()
+        split_points(i, points_ref, ph_ref, pl_ref)
 
     def rotate(j, carry):
         panel = panel_ref[:, pl.ds(pl.multiple_of(j * 256, 256), 256)].T
@@ -167,40 +190,40 @@
     lax.fori_loop(4, M // 8, functools.partial(eight_rows, counted=False), 0)
 
 
-def code_sums(place, points, pieces, codes):
+def code_sums(place, points, first, second, codes):
     count = points.shape[0]
     half = jax.ShapeDtypeStruct((M // 2, SUB, PAYLOAD), F32)
     return pl.pallas_call(
         sums_kernel,
         out_shape=(half, half),
-        in_specs=[SMEM, VMEM, VMEM] + [ANY] * len(codes),
+        in_specs=[SMEM, ANY, VMEM, VMEM] + [ANY] * len(codes),
         out_specs=(VMEM, VMEM),
         scratch_shapes=[
             pltpu.VMEM((M, count), jnp.int32),
+            pltpu.VMEM((count, 256), F32),
             pltpu.VMEM((count, 256), BF16),
             pltpu.VMEM((count, 256), BF16),
             pltpu.VMEM((256, D), F32),
             pltpu.VMEM((M, SUB, count), F32),
-            pltpu.SemaphoreType.DMA((len(codes),)),
+            pltpu.SemaphoreType.DMA((8,)),
         ],
         compiler_params=grant(34),
         name="code_sums",
-    )(place, points, pieces, *codes)
+    )(place, points, first, second, *codes)
 
 
 def cross_kernel(
-    place_ref, pts_ref, mine_ref, other_ref, c0, c1a, c1b, c2a, c2b, c3a, c3b,
+    place_ref, pts_ref, mine_ref, other_ref, c0, c1, c2, c3,
     keep_ref, give_ref,
-    codes_ref, ph_ref, pl_ref, tab_ref, ah0_ref, al0_ref, ah1_ref, al1_ref, acc_ref, arrived,
+    codes_ref, points_ref, ph_ref, pl_ref, tab_ref, ah0_ref, al0_ref, ah1_ref, al1_ref, acc_ref, arrived,
 ):
     count = pts_ref.shape[0]
     y, core = place_ref[0], place_ref[1]
-    copies = fetch_codes(y, codes_ref, (c0, c1a, c1b, c2a, c2b, c3a, c3b), arrived)
+    copies = fetch_codes(y, codes_ref, (c0, c1, c2, c3), arrived)
+    for i in range(4):
+        load_points(i, pts_ref, points_ref, arrived).start()
     tab_ref[core] = mine_ref[...]
     tab_ref[1 - core] = other_ref[...]
-    ph, plo = split(pts_ref[...])
-    ph_ref[...] = ph
-    pl_ref[...] = plo
     for copy in copies:
         copy.wait()
     wide = 1024
@@ -239,6 +262,9 @@
                 high_ref, low_ref = slots[(stage - 1) % 2]
                 here = pl.ds(pl.multiple_of(e * quarter, 128), quarter)
                 more = dot3(high_ref[:, here], low_ref[:, here], ph_ref[here], pl_ref[here], NN)
+            if stage == 0:
+                load_points(e, pts_ref, points_ref, arrived).wait()
+                split_points(e, points_ref, ph_ref, pl_ref)
             if stage < 4:
                 look_up(stage, e, *slots[stage % 2])
             if stage > 0:
@@ -262,10 +288,11 @@
     return pl.pallas_call(
         cross_kernel,
         out_shape=(half, half),
-        in_specs=[SMEM] + [VMEM] * 3 + [ANY] * len(codes),
+        in_specs=[SMEM, ANY, VMEM, VMEM] + [ANY] * len(codes),
         out_specs=(VMEM, VMEM),
         scratch_shapes=[
             pltpu.VMEM((M, count), jnp.int32),
+            pltpu.VMEM((count, 256), F32),
             pltpu.VMEM((count, 256), BF16),
             pltpu.VMEM((count, 256), BF16),
             pltpu.VMEM((2, M // 2, SUB, K), F32),
@@ -274,7 +301,7 @@
             pltpu.VMEM((256, count), BF16),
             pltpu.VMEM((256, count), BF16),
             pltpu.VMEM((256, 256), F32),
-            pltpu.SemaphoreType.DMA((len(codes),)),
+            pltpu.SemaphoreType.DMA((8,)),
         ],
         compiler_params=grant(28),
         name="cross_part",
@@ -364,17 +391,16 @@
     y, core = lax.axis_index("y"), lax.axis_index("core")
     own_row = lax.axis_index(ROWS)
     place = jnp.stack([y, core, own_row]).astype(jnp.int32)
-    upper, lower = codes[:16], codes[16:]
-    one_a, three_a = shift(upper, 1), shift(upper, 3)
+    one, three = shift(codes, 1), shift(codes, 3)
     swapped = lax.ppermute(
         rotation, ("x", "y"), [(a * 4 + b, b * 4 + a) for a in range(4) for b in range(4)]
     )
-    swapped, one_a, three_a = lax.optimization_barrier((swapped, one_a, three_a))
-    pieces = spread_to(swapped, ROWS, 32)
-    one_b, three_b = shift(lower, 1), shift(lower, 3)
-    two_a, two_b = shift(one_a, 1), shift(three_b, 3)
-    all_codes = [codes, one_a, one_b, two_a, two_b, three_a, three_b]
-    keep, give = code_sums(place, points, pieces, all_codes)
+    swapped, one, three = lax.optimization_barrier((swapped, one, three))
+    pieces, two = spread_to(swapped, ("x", "z"), 16), shift(one, 1)
+    pieces, two = lax.optimization_barrier((pieces, two))
+    all_codes = [in_hbm(c) for c in (codes, one, two, three)]
+    points = in_hbm(points)
+    keep, give = code_sums(place, points, pieces, swap_core(pieces), all_codes)
 
     sums = keep + swap_core(give)
     sums = jnp.sum(lax.all_to_all(sums, CHIPS, 0, 0, tiled=True), axis=0)

time: 258 us -> 250 us (0.969)
  starting transfers between devices: 35.7 us -> 29.6 us
  local copies, waits for them, and re-layouts: 14.4 us -> 9.78 us
  waiting for transfers between devices: 44.7 us -> 49.1 us
    all_to_all x2, starting transfers between devices: 18.2 us -> 13.7 us  [spread_to(): return lax.all_to_all(copies, axes, 0, 0, tiled=True)]
    ppermute x6 -> x3, starting transfers between devices: 7.72 us -> 3.71 us  [shift(): return lax.ppermute(value, 'y', [(s, (s + by) % 4) for s in range(4)])]
    ppermute x6 -> x3, waiting for transfers between devices: 16.1 us -> 19.3 us  [shift(): return lax.ppermute(value, 'y', [(s, (s + by) % 4) for s in range(4)])]
    ppermute x4 -> x5, starting transfers between devices: 8.44 us -> 10.8 us  [swap_core(): return lax.ppermute(value, 'core', [(0, 1), (1, 0)])]
    ppermute x4 -> x5, waiting for transfers between devices: 8.77 us -> 10.3 us  [swap_core(): return lax.ppermute(value, 'core', [(0, 1), (1, 0)])]
  transfers between devices with their start and end apart: 13 -> 11, of which waited for: 11 -> 9; matrix products, arithmetic and copies ran while one was open for 3% -> 3% of each run, Pallas kernels for 0% -> 0%
where the time goes in v7:
time: 250 us
  Pallas kernels  109 us (44%)
  blocking collectives  51.1 us (20%)
  waiting for transfers between devices  49.1 us (20%)
  starting transfers between devices  29.6 us (12%)
  local copies, waits for them, and re-layouts  9.78 us (4%)
    pallas_call x1, Pallas kernels, newton_schulz(): pl.pallas_call(iterate_kernel, out_shape=jax.ShapeDtypeStruct((32, 256),...  61 us
    pallas_call x1, Pallas kernels, code_sums(): pl.pallas_call(sums_kernel, out_shape=(half, half), in_specs=[SMEM, ANY,...  26.3 us
    all_to_all x1, blocking collectives, shards(): sums = jnp.sum(lax.all_to_all(sums, CHIPS, 0, 0, tiled=True), axis=0)  22.3 us
    pallas_call x1, Pallas kernels, cross_part(): pl.pallas_call(cross_kernel, out_shape=(half, half), in_specs=[SMEM, ANY,...  21.7 us
    all_to_all x2, waiting for transfers between devices, spread_to(): return lax.all_to_all(copies, axes, 0, 0, tiled=True)  19.5 us
    ppermute x3, waiting for transfers between devices, shift(): return lax.ppermute(value, 'y', [(s, (s + by) % 4) for s in range(4)])  19.3 us
    all_to_all x1, blocking collectives, spread_to(): return lax.all_to_all(copies, axes, 0, 0, tiled=True)  15.8 us
    all_to_all x2, starting transfers between devices, spread_to(): return lax.all_to_all(copies, axes, 0, 0, tiled=True)  13.7 us
  transfers between devices with their start and end apart: 11, of which 9 were waited for; matrix products, arithmetic and copies ran while one was open for 3% of the time, Pallas kernels for 0%

profile of v7, /device:TPU:1, one launch (start us, length us, event | category | flops | bytes accessed | tf_op | source)
XLA Modules:
  0.0 249.8 jit_solution(224880531890789485)
XLA Ops:
  0.6 3.6 %collective-permute-start.2 = (s32[32,3072]{1,0:T(8,128)}, s32[32,3072]{1,0:T(8,128)S(1)}, u32[]{:S(2)}, u32[]{:S(2)}) collective-permute-start(s32[32,3072]{1,0:T(8,128)} %c0.3), channel_id=1, source_target_pairs={{0,3},{1,0},{2,1},{3,2},{4,7},{5,4},{6,5},{7,6},{8,11},{9,8},{10,9... | collective-permute-start | bytes 1179656 | tf_op jit(solution)/shard_map/ppermute | solution.py:65
  4.3 0.0 collective-permute-start.1
  4.3 1.4 collective-permute-start
  5.7 0.0 collective-permute-done
  5.7 6.9 %collective-permute-done.2.c3 = s32[32,3072]{1,0:T(8,128)S(1)} collective-permute-done((s32[32,3072]{1,0:T(8,128)}, s32[32,3072]{1,0:T(8,128)S(1)}, u32[]{:S(2)}, u32[]{:S(2)}) %collective-permute-start.2) | collective-permute-done | bytes 393248 | tf_op jit(solution)/shard_map/ppermute | solution.py:65
  12.6 0.0 copy-start
  12.6 2.8 %collective-permute-done.1.c1 = s32[32,3072]{1,0:T(8,128)S(1)} collective-permute-done((s32[32,3072]{1,0:T(8,128)}, s32[32,3072]{1,0:T(8,128)S(1)}, u32[]{:S(2)}, u32[]{:S(2)}) %collective-permute-start.1) | collective-permute-done | bytes 393248 | tf_op jit(solution)/shard_map/ppermute | solution.py:65
  15.3 0.0 copy-start.1
  15.4 0.9 broadcast_in_dim.6
  16.3 8.3 %all-to-all-start = ((f32[16,32,256]{2,1,0:T(8,128)}), f32[16,32,256]{2,1,0:T(8,128)S(1)}, u32[]{:S(2)}, u32[]{:S(2)}) async-start(f32[16,32,256]{2,1,0:T(8,128)} %broadcast_in_dim.6), calls=%async_computation | async-start | bytes 1048576 | tf_op jit(solution)/shard_map/all_to_all | solution.py:53
  24.6 0.1 collective-permute-start.3
  24.6 9.7 %collective-permute-done.3.c2 = s32[32,3072]{1,0:T(8,128)S(1)} collective-permute-done((s32[32,3072]{1,0:T(8,128)S(1)}, s32[32,3072]{1,0:T(8,128)S(1)}, u32[]{:S(2)}, u32[]{:S(2)}) %collective-permute-start.3) | collective-permute-done | bytes 393248 | tf_op jit(solution)/shard_map/ppermute | solution.py:65
  34.3 0.0 copy-start.2
  34.3 0.0 all-to-all-done.first_ref
  34.3 3.1 %collective-permute-start.4 = (f32[16,32,256]{2,1,0:T(8,128)S(1)}, f32[16,32,256]{2,1,0:T(8,128)S(1)}, u32[]{:S(2)}, u32[]{:S(2)}) collective-permute-start(f32[16,32,256]{2,1,0:T(8,128)S(1)} %all-to-all-done.first_ref), channel_id=1, source_target_pairs={{0,4},{4,0},{1,5},{5,1},{2,6},{6,2},{3,7},{7,3},{8,12},{12,8},{9,1... | collective-permute-start | bytes 1572872 | tf_op jit(solution)/shard_map/ppermute | solution.py:57
  37.4 0.1 pad_add_fusion.place_ref
  37.5 1.5 collective-permute-done.4.second_ref
  38.9 0.0 copy-done
  38.9 0.0 copy-done.1
  38.9 0.0 copy-done.2
  38.9 26.3 %code_sums.1 = (f32[64,8,384]{2,1,0:T(8,128)S(1)}, f32[64,8,384]{2,1,0:T(8,128)S(1)}) custom-call(s32[3]{0:T(128)S(1)} %pad_add_fusion.place_ref, f32[3072,256]{1,0:T(8,128)} %pts_ref.3, f32[16,32,256]{2,1,0:T(8,128)S(1)} %all-to-all-done.first_ref, f32[16,32,256]{2,1,0:T(8,128)S(1)} %collective-permute-done.4.second_ref, s32[32,3072]{1,0:T(8,128)} %c0.3, ...), custom_call_target="tpu_custom_call" | custom-call | tf_op jit(solution)/shard_map/code_sums/pallas_call | solution.py:196
  65.2 0.5 collective-permute-start.5
  65.7 1.9 collective-permute-done.5
  67.6 0.1 add.18
  67.7 22.3 %all_to_all.25 = f32[64,8,384]{2,1,0:T(8,128)S(1)} all-to-all(f32[64,8,384]{2,1,0:T(8,128)S(1)} %add.18), channel_id=1, replica_groups=mesh['x'=4,'z'=4,'core'=2,'y'=4] {'y','x','z'}, dimensions={0} | all-to-all | bytes 1572864 | tf_op jit(solution)/shard_map/all_to_all | solution.py:406
  89.9 0.1 reduce_sum.18
  90.1 15.8 %all_to_all.26.mine_ref = f32[64,8,256]{2,1,0:T(8,128)S(1)} all-to-all(f32[64,8,256]{2,1,0:T(8,128)S(1)} %broadcast_in_dim.7), channel_id=1, replica_groups=mesh['x'=4,'z'=4,'core'=2,'y'=4] {'y','x','z'}, dimensions={0} | all-to-all | bytes 1048576 | tf_op jit(solution)/shard_map/all_to_all | solution.py:53
  105.9 3.1 %collective-permute-start.6 = (f32[64,8,256]{2,1,0:T(8,128)S(1)}, f32[64,8,256]{2,1,0:T(8,128)S(1)}, u32[]{:S(2)}, u32[]{:S(2)}) collective-permute-start(f32[64,8,256]{2,1,0:T(8,128)S(1)} %all_to_all.26.mine_ref), channel_id=1, source_target_pairs={{0,4},{4,0},{1,5},{5,1},{2,6},{6,2},{3,7},{7,3},{8,12},{12,8},{9,1... | collective-permute-start | bytes 1572872 | tf_op jit(solution)/shard_map/ppermute | solution.py:57
  109.0 1.5 collective-permute-done.6.other_ref
  110.5 21.7 %cross_part.1 = (f32[16,32,256]{2,1,0:T(8,128)S(1)}, f32[16,32,256]{2,1,0:T(8,128)S(1)}) custom-call(s32[3]{0:T(128)S(1)} %pad_add_fusion.place_ref, f32[3072,256]{1,0:T(8,128)} %pts_ref.3, f32[64,8,256]{2,1,0:T(8,128)S(1)} %all_to_all.26.mine_ref, f32[64,8,256]{2,1,0:T(8,128)S(1)} %collective-permute-done.6.other_ref, s32[32,3072]{1,0:T(8,128)} %c0.3, ...), custom_call_target="tpu_custom_call" | custom-call | tf_op jit(solution)/shard_map/cross_part/pallas_call | solution.py:288
  132.3 0.4 collective-permute-start.7
  132.7 1.6 collective-permute-done.7
  134.3 0.1 add.19
  134.3 13.1 %all_to_all.27 = f32[16,32,256]{2,1,0:T(8,128)S(1)} all-to-all(f32[16,32,256]{2,1,0:T(8,128)S(1)} %add.19), channel_id=1, replica_groups=mesh['x'=4,'z'=4,'core'=2,'y'=4] {'x','z'}, dimensions={0} | all-to-all | bytes 1048576 | tf_op jit(solution)/shard_map/all_to_all | solution.py:413
  147.4 1.6 broadcast_in_dim.8
  149.0 5.4 %all-to-all-start.4 = ((f32[64,32,256]{2,1,0:T(8,128)}), f32[64,32,256]{2,1,0:T(8,128)S(1)}, u32[]{:S(2)}, u32[]{:S(2)}) async-start(f32[64,32,256]{2,1,0:T(8,128)} %broadcast_in_dim.8), calls=%async_computation.4 | async-start | bytes 4194304 | tf_op jit(solution)/shard_map/all_to_all | solution.py:53
  154.5 2.6 %copy.5 = f32[16,2,256,8]{3,2,1,0:T(8,128)} copy(f32[16,2,256,8]{2,3,0,1:T(8,128)S(1)} %maximum_bitcast_fusion) | data formatting | bytes 524288 | tf_op jit(solution)/shard_map/transpose | solution.py:418
  157.1 4.6 %reshape.12 = f32[32,2048]{1,0:T(8,128)} reshape(f32[16,2,256,8]{3,2,1,0:T(8,128)} %copy.5) | data formatting | bytes 524288 | tf_op jit(solution)/shard_map/reshape | solution.py:418
  161.7 19.5 %all-to-all-done.4.mine_ref = f32[64,32,256]{2,1,0:T(8,128)S(1)} async-done(((f32[64,32,256]{2,1,0:T(8,128)}), f32[64,32,256]{2,1,0:T(8,128)S(1)}, u32[]{:S(2)}, u32[]{:S(2)}) %all-to-all-start.4) | async-done | bytes 2097184 | tf_op jit(solution)/shard_map/all_to_all | solution.py:53
  181.2 3.7 %collective-permute-start.8 = (f32[64,32,256]{2,1,0:T(8,128)S(1)}, f32[64,32,256]{2,1,0:T(8,128)S(1)}, u32[]{:S(2)}, u32[]{:S(2)}) collective-permute-start(f32[64,32,256]{2,1,0:T(8,128)S(1)} %all-to-all-done.4.mine_ref), channel_id=1, source_target_pairs={{0,4},{4,0},{1,5},{5,1},{2,6},{6,2},{3,7},{7,3},{8,12},{12,8},{9,1... | collective-permute-start | bytes 6291464 | tf_op jit(solution)/shard_map/ppermute | solution.py:57
  185.0 3.8 %collective-permute-done.8.other_ref = f32[64,32,256]{2,1,0:T(8,128)S(1)} collective-permute-done((f32[64,32,256]{2,1,0:T(8,128)S(1)}, f32[64,32,256]{2,1,0:T(8,128)S(1)}, u32[]{:S(2)}, u32[]{:S(2)}) %collective-permute-start.8) | collective-permute-done | bytes 2097184 | tf_op jit(solution)/shard_map/ppermute | solution.py:57
  188.7 61.0 %newton_schulz.1 = f32[32,256]{1,0:T(8,128)} custom-call(s32[3]{0:T(128)S(1)} %pad_add_fusion.place_ref, f32[64,32,256]{2,1,0:T(8,128)S(1)} %all-to-all-done.4.mine_ref, f32[64,32,256]{2,1,0:T(8,128)S(1)} %collective-permute-done.8.other_ref), custom_call_target="tpu_custom_call" | custom-call | tf_op jit(solution)/shard_map/newton_schulz/pallas_call | solution.py:372
  (6 shorter events, 0.1 us)
Async XLA Ops:
  0.6 11.9 %collective-permute-start.2 = (s32[32,3072]{1,0:T(8,128)}, s32[32,3072]{1,0:T(8,128)S(1)}, u32[]{:S(2)}, u32[]{:S(2)}) collective-permute-start(s32[32,3072]{1,0:T(8,128)} %c0.3), channel_id=1, source_target_pairs={{0,3},{1,0},{2,1},{3,2},{4,7},{5,4},{6,5},{7,6},{8,11},{9,8},{10,9... | collective-permute-start | bytes 1179656 | tf_op jit(solution)/shard_map/ppermute | solution.py:65
  4.3 11.1 %collective-permute-start.1 = (s32[32,3072]{1,0:T(8,128)}, s32[32,3072]{1,0:T(8,128)S(1)}, u32[]{:S(2)}, u32[]{:S(2)}) collective-permute-start(s32[32,3072]{1,0:T(8,128)} %c0.3), channel_id=1, source_target_pairs={{0,1},{1,2},{2,3},{3,0},{4,5},{5,6},{6,7},{7,4},{8,9},{9,10},{10,1... | collective-permute-start | bytes 1179656 | tf_op jit(solution)/shard_map/ppermute | solution.py:65
  4.3 1.4 collective-permute-start
  12.6 26.3 %copy-start = (s32[32,3072]{1,0:T(8,128)}, s32[32,3072]{1,0:T(8,128)S(1)}, u32[]{:S(2)}) copy-start(s32[32,3072]{1,0:T(8,128)S(1)} %collective-permute-done.2.c3) | copy-start | bytes 1179652
  15.3 23.6 %copy-start.1 = (s32[32,3072]{1,0:T(8,128)}, s32[32,3072]{1,0:T(8,128)S(1)}, u32[]{:S(2)}) copy-start(s32[32,3072]{1,0:T(8,128)S(1)} %collective-permute-done.1.c1) | copy-start | bytes 1179652
  16.3 18.1 %all-to-all-start = ((f32[16,32,256]{2,1,0:T(8,128)}), f32[16,32,256]{2,1,0:T(8,128)S(1)}, u32[]{:S(2)}, u32[]{:S(2)}) async-start(f32[16,32,256]{2,1,0:T(8,128)} %broadcast_in_dim.6), calls=%async_computation | async-start | bytes 1048576 | tf_op jit(solution)/shard_map/all_to_all | solution.py:53
  24.6 9.7 %collective-permute-start.3 = (s32[32,3072]{1,0:T(8,128)S(1)}, s32[32,3072]{1,0:T(8,128)S(1)}, u32[]{:S(2)}, u32[]{:S(2)}) collective-permute-start(s32[32,3072]{1,0:T(8,128)S(1)} %collective-permute-done.1.c1), channel_id=1, source_target_pairs={{0,1},{1,2},{2,3},{3,0},{4,5},{5,6},{6,7},{7,4},{8,9},{9,10},{10,1... | collective-permute-start | bytes 1179656 | tf_op jit(solution)/shard_map/ppermute | solution.py:65
  34.3 4.6 %copy-start.2 = (s32[32,3072]{1,0:T(8,128)}, s32[32,3072]{1,0:T(8,128)S(1)}, u32[]{:S(2)}) copy-start(s32[32,3072]{1,0:T(8,128)S(1)} %collective-permute-done.3.c2) | copy-start | bytes 1179652
  34.3 4.6 %collective-permute-start.4 = (f32[16,32,256]{2,1,0:T(8,128)S(1)}, f32[16,32,256]{2,1,0:T(8,128)S(1)}, u32[]{:S(2)}, u32[]{:S(2)}) collective-permute-start(f32[16,32,256]{2,1,0:T(8,128)S(1)} %all-to-all-done.first_ref), channel_id=1, source_target_pairs={{0,4},{4,0},{1,5},{5,1},{2,6},{6,2},{3,7},{7,3},{8,12},{12,8},{9,1... | collective-permute-start | bytes 1572872 | tf_op jit(solution)/shard_map/ppermute | solution.py:57
  65.2 2.4 collective-permute-start.5
  105.9 4.6 %collective-permute-start.6 = (f32[64,8,256]{2,1,0:T(8,128)S(1)}, f32[64,8,256]{2,1,0:T(8,128)S(1)}, u32[]{:S(2)}, u32[]{:S(2)}) collective-permute-start(f32[64,8,256]{2,1,0:T(8,128)S(1)} %all_to_all.26.mine_ref), channel_id=1, source_target_pairs={{0,4},{4,0},{1,5},{5,1},{2,6},{6,2},{3,7},{7,3},{8,12},{12,8},{9,1... | collective-permute-start | bytes 1572872 | tf_op jit(solution)/shard_map/ppermute | solution.py:57
  132.3 2.0 collective-permute-start.7
  149.0 32.2 %all-to-all-start.4 = ((f32[64,32,256]{2,1,0:T(8,128)}), f32[64,32,256]{2,1,0:T(8,128)S(1)}, u32[]{:S(2)}, u32[]{:S(2)}) async-start(f32[64,32,256]{2,1,0:T(8,128)} %broadcast_in_dim.8), calls=%async_computation.4 | async-start | bytes 4194304 | tf_op jit(solution)/shard_map/all_to_all | solution.py:53
  181.2 7.5 %collective-permute-start.8 = (f32[64,32,256]{2,1,0:T(8,128)S(1)}, f32[64,32,256]{2,1,0:T(8,128)S(1)}, u32[]{:S(2)}, u32[]{:S(2)}) collective-permute-start(f32[64,32,256]{2,1,0:T(8,128)S(1)} %all-to-all-done.4.mine_ref), channel_id=1, source_target_pairs={{0,4},{4,0},{1,5},{5,1},{2,6},{6,2},{3,7},{7,3},{8,12},{12,8},{9,1... | collective-permute-start | bytes 6291464 | tf_op jit(solution)/shard_map/ppermute | solution.py:57

commit v8 on v7

--- a/solution.py
+++ b/solution.py
@@ -28,7 +28,7 @@
 
 
 QUARTER = 98304 // 32 // 4
-PAYLOAD = K + 128
+PAYLOAD = K * SUB // 2 + 128
 
 
 def split(value):
@@ -167,18 +167,23 @@
             slab = total[mm * 64 : mm * 64 + 64, columns]
             parts = [slab[t * 16 : t * 16 + 8] + slab[t * 16 + 8 : t * 16 + 16] for t in range(4)]
             halves = [pick(parts[2 * h], parts[2 * h + 1], mm) for h in range(2)]
-            ticks = jnp.zeros((SUB, 128), F32)
+            ticks = jnp.zeros((2, 128), F32)
             if counted:
                 r = quad * 4 + mm
                 tally = [total[256 + t * 8 : 264 + t * 8, columns] for t in range(4)]
                 ticks = [pick(tally[2 * h], tally[2 * h + 1], mm)[r : r + 1] for h in range(2)]
-                ticks = jnp.concatenate(ticks + [jnp.zeros((6, 128), F32)], axis=0)
-            found.append(jnp.concatenate(halves + [ticks], axis=1))
+                ticks = jnp.concatenate(ticks, axis=0)
+            found.append(halves + [ticks])
         for h in range(2):
-            even, odd = found[2 * h], found[2 * h + 1]
             q = eight * 4 + quad * 2 + h
-            keep_ref[q] = jnp.where(core == 0, even, odd)
-            give_ref[q] = jnp.where(core == 0, odd, even)
+            for number, (even, odd) in enumerate(zip(found[2 * h], found[2 * h + 1], strict=True)):
+                for ref, value in (
+                    (keep_ref, jnp.where(core == 0, even, odd)),
+                    (give_ref, jnp.where(core == 0, odd, even)),
+                ):
+                    for i in range(value.shape[0] // 2):
+                        lanes = slice((number * 4 + i) * 128, (number * 4 + i) * 128 + 128)
+                        ref[q, :, lanes] = value[2 * i : 2 * i + 2]
 
     def eight_rows(i, carry, counted):
         eight = lax.rem(y * 4 + i, M // 8)
@@ -192,7 +197,7 @@
 
 def code_sums(place, points, first, second, codes):
     count = points.shape[0]
-    half = jax.ShapeDtypeStruct((M // 2, SUB, PAYLOAD), F32)
+    half = jax.ShapeDtypeStruct((M // 2, 2, PAYLOAD), F32)
     return pl.pallas_call(
         sums_kernel,
         out_shape=(half, half),
@@ -308,7 +313,7 @@
     )(place, points, mine, other, *codes)
 
 
-def iterate_kernel(place_ref, mine_ref, other_ref, out_ref, now_ref, hl_ref, gh_ref, gl_ref, tail_ref, turned_ref):
+def iterate_kernel(place_ref, mine_ref, other_ref, out_ref, now_ref, hl_ref, gh_ref, gl_ref, tail_ref, turned_ref, mixed_ref):
     y, core, column = place_ref[0], place_ref[1], place_ref[2]
     total = jnp.zeros((1, 256), F32)
     for half, source in enumerate((mine_ref, other_ref)):
@@ -329,8 +334,12 @@
         old, new = lax.rem(k, 2), 1 - lax.rem(k, 2)
         high_ref, low_ref = hl_ref.at[old, 0], hl_ref.at[old, 1]
         for j in range(4):
+            strip = slice(j * 256, j * 256 + 256)
+            mixed_ref[:, strip] = mxu(high_ref[...], low_ref[strip], NT)
+        for j in range(4):
             strip, below = slice(j * 256, j * 256 + 256), slice(j * 256, D)
-            gram = dot3(high_ref[below], low_ref[below], high_ref[strip], low_ref[strip], NT)
+            gram = mxu(high_ref[below], high_ref[strip], NT)
+            gram += mixed_ref[below, strip] + mixed_ref[strip, below].T
             high, low = split(gram)
             gh_ref[below, strip] = high
             gl_ref[below, strip] = low
@@ -381,6 +390,7 @@
             pltpu.VMEM((D, D), BF16),
             pltpu.VMEM((2, 256, D), BF16),
             pltpu.VMEM((128, 256), F32),
+            pltpu.VMEM((D, D), F32),
         ],
         compiler_params=grant(34),
         name="newton_schulz",
@@ -404,8 +414,9 @@
 
     sums = keep + swap_core(give)
     sums = jnp.sum(lax.all_to_all(sums, CHIPS, 0, 0, tiled=True), axis=0)
-    counts = sums[:2, K:].reshape(1, K)
-    centers = spread_to(sums[:, :K] / counts, CHIPS, 64)
+    counts = sums[:, PAYLOAD - 128 :].reshape(1, K)
+    sums = sums[:, : PAYLOAD - 128].reshape(2, 2, 4, 128).transpose(2, 0, 1, 3).reshape(SUB, K)
+    centers = spread_to(sums / counts, CHIPS, 64)
     others = swap_core(centers)
 
     keep, give = cross_part(place, points, centers, others, all_codes)

time: 250 us -> 246 us (0.984)
  no operation moved by 1% of the time
where the time goes in v8:
time: 246 us
  Pallas kernels  107 us (43%)
  waiting for transfers between devices  48.8 us (20%)
  blocking collectives  48.8 us (20%)
  starting transfers between devices  29.7 us (12%)
  local copies, waits for them, and re-layouts  9.81 us (4%)
    pallas_call x1, Pallas kernels, newton_schulz(): pl.pallas_call(iterate_kernel, out_shape=jax.ShapeDtypeStruct((32, 256),...  58.8 us
    pallas_call x1, Pallas kernels, code_sums(): pl.pallas_call(sums_kernel, out_shape=(half, half), in_specs=[SMEM, ANY,...  26.4 us
    pallas_call x1, Pallas kernels, cross_part(): pl.pallas_call(cross_kernel, out_shape=(half, half), in_specs=[SMEM, ANY,...  21.8 us
    all_to_all x1, blocking collectives, shards(): sums = jnp.sum(lax.all_to_all(sums, CHIPS, 0, 0, tiled=True), axis=0)  20.2 us
    all_to_all x2, waiting for transfers between devices, spread_to(): return lax.all_to_all(copies, axes, 0, 0, tiled=True)  19.5 us
    ppermute x3, waiting for transfers between devices, shift(): return lax.ppermute(value, 'y', [(s, (s + by) % 4) for s in range(4)])  19.3 us
    all_to_all x1, blocking collectives, spread_to(): return lax.all_to_all(copies, axes, 0, 0, tiled=True)  15.6 us
    all_to_all x2, starting transfers between devices, spread_to(): return lax.all_to_all(copies, axes, 0, 0, tiled=True)  13.7 us
  transfers between devices with their start and end apart: 11, of which 9 were waited for; matrix products, arithmetic and copies ran while one was open for 3% of the time, Pallas kernels for 0%

profile of v8, /device:TPU:1, one launch (start us, length us, event | category | flops | bytes accessed | tf_op | source)
XLA Modules:
  0.0 245.6 jit_solution(4290183030604746383)
XLA Ops:
  0.6 3.6 %collective-permute-start.2 = (s32[32,3072]{1,0:T(8,128)}, s32[32,3072]{1,0:T(8,128)S(1)}, u32[]{:S(2)}, u32[]{:S(2)}) collective-permute-start(s32[32,3072]{1,0:T(8,128)} %c0.3), channel_id=1, source_target_pairs={{0,3},{1,0},{2,1},{3,2},{4,7},{5,4},{6,5},{7,6},{8,11},{9,8},{10,9... | collective-permute-start | bytes 1179656 | tf_op jit(solution)/shard_map/ppermute | solution.py:65
  4.3 0.0 collective-permute-start.1
  4.3 1.4 collective-permute-start
  5.7 0.0 collective-permute-done
  5.7 6.9 %collective-permute-done.2.c3 = s32[32,3072]{1,0:T(8,128)S(1)} collective-permute-done((s32[32,3072]{1,0:T(8,128)}, s32[32,3072]{1,0:T(8,128)S(1)}, u32[]{:S(2)}, u32[]{:S(2)}) %collective-permute-start.2) | collective-permute-done | bytes 393248 | tf_op jit(solution)/shard_map/ppermute | solution.py:65
  12.6 0.0 copy-start
  12.6 2.8 %collective-permute-done.1.c1 = s32[32,3072]{1,0:T(8,128)S(1)} collective-permute-done((s32[32,3072]{1,0:T(8,128)}, s32[32,3072]{1,0:T(8,128)S(1)}, u32[]{:S(2)}, u32[]{:S(2)}) %collective-permute-start.1) | collective-permute-done | bytes 393248 | tf_op jit(solution)/shard_map/ppermute | solution.py:65
  15.3 0.0 copy-start.1
  15.4 0.9 broadcast_in_dim.6
  16.3 8.3 %all-to-all-start = ((f32[16,32,256]{2,1,0:T(8,128)}), f32[16,32,256]{2,1,0:T(8,128)S(1)}, u32[]{:S(2)}, u32[]{:S(2)}) async-start(f32[16,32,256]{2,1,0:T(8,128)} %broadcast_in_dim.6), calls=%async_computation | async-start | bytes 1048576 | tf_op jit(solution)/shard_map/all_to_all | solution.py:53
  24.6 0.1 collective-permute-start.3
  24.6 9.7 %collective-permute-done.3.c2 = s32[32,3072]{1,0:T(8,128)S(1)} collective-permute-done((s32[32,3072]{1,0:T(8,128)S(1)}, s32[32,3072]{1,0:T(8,128)S(1)}, u32[]{:S(2)}, u32[]{:S(2)}) %collective-permute-start.3) | collective-permute-done | bytes 393248 | tf_op jit(solution)/shard_map/ppermute | solution.py:65
  34.3 0.0 copy-start.2
  34.3 0.0 all-to-all-done.first_ref
  34.3 3.1 %collective-permute-start.4 = (f32[16,32,256]{2,1,0:T(8,128)S(1)}, f32[16,32,256]{2,1,0:T(8,128)S(1)}, u32[]{:S(2)}, u32[]{:S(2)}) collective-permute-start(f32[16,32,256]{2,1,0:T(8,128)S(1)} %all-to-all-done.first_ref), channel_id=1, source_target_pairs={{0,4},{4,0},{1,5},{5,1},{2,6},{6,2},{3,7},{7,3},{8,12},{12,8},{9,1... | collective-permute-start | bytes 1572872 | tf_op jit(solution)/shard_map/ppermute | solution.py:57
  37.4 0.1 pad_add_fusion.place_ref
  37.5 1.5 collective-permute-done.4.second_ref
  38.9 0.0 copy-done
  38.9 0.0 copy-done.1
  38.9 0.0 copy-done.2
  38.9 26.4 %code_sums.1 = (f32[64,2,1152]{2,1,0:T(2,128)S(1)}, f32[64,2,1152]{2,1,0:T(2,128)S(1)}) custom-call(s32[3]{0:T(128)S(1)} %pad_add_fusion.place_ref, f32[3072,256]{1,0:T(8,128)} %pts_ref.3, f32[16,32,256]{2,1,0:T(8,128)S(1)} %all-to-all-done.first_ref, f32[16,32,256]{2,1,0:T(8,128)S(1)} %collective-permute-done.4.second_ref, s32[32,3072]{1,0:T(8,128)} %c0.3, ...), custom_call_target="tpu_custom_call" | custom-call | tf_op jit(solution)/shard_map/code_sums/pallas_call | solution.py:201
  65.3 0.5 collective-permute-start.5
  65.8 1.6 collective-permute-done.5
  67.4 0.3 add.18
  67.7 20.2 %all_to_all.25 = f32[64,2,1152]{2,1,0:T(2,128)S(1)} all-to-all(f32[64,2,1152]{2,1,0:T(2,128)S(1)} %add.18), channel_id=1, replica_groups=mesh['x'=4,'z'=4,'core'=2,'y'=4] {'y','x','z'}, dimensions={0} | all-to-all | bytes 1179648 | tf_op jit(solution)/shard_map/all_to_all | solution.py:416
  87.9 0.2 reduce_sum.18
  88.2 15.6 %all_to_all.26.mine_ref = f32[64,8,256]{2,1,0:T(8,128)S(1)} all-to-all(f32[64,8,256]{2,1,0:T(8,128)S(1)} %broadcast_in_dim.7), channel_id=1, replica_groups=mesh['x'=4,'z'=4,'core'=2,'y'=4] {'y','x','z'}, dimensions={0} | all-to-all | bytes 1048576 | tf_op jit(solution)/shard_map/all_to_all | solution.py:53
  103.8 3.2 %collective-permute-start.6 = (f32[64,8,256]{2,1,0:T(8,128)S(1)}, f32[64,8,256]{2,1,0:T(8,128)S(1)}, u32[]{:S(2)}, u32[]{:S(2)}) collective-permute-start(f32[64,8,256]{2,1,0:T(8,128)S(1)} %all_to_all.26.mine_ref), channel_id=1, source_target_pairs={{0,4},{4,0},{1,5},{5,1},{2,6},{6,2},{3,7},{7,3},{8,12},{12,8},{9,1... | collective-permute-start | bytes 1572872 | tf_op jit(solution)/shard_map/ppermute | solution.py:57
  107.0 1.5 collective-permute-done.6.other_ref
  108.5 21.8 %cross_part.1 = (f32[16,32,256]{2,1,0:T(8,128)S(1)}, f32[16,32,256]{2,1,0:T(8,128)S(1)}) custom-call(s32[3]{0:T(128)S(1)} %pad_add_fusion.place_ref, f32[3072,256]{1,0:T(8,128)} %pts_ref.3, f32[64,8,256]{2,1,0:T(8,128)S(1)} %all_to_all.26.mine_ref, f32[64,8,256]{2,1,0:T(8,128)S(1)} %collective-permute-done.6.other_ref, s32[32,3072]{1,0:T(8,128)} %c0.3, ...), custom_call_target="tpu_custom_call" | custom-call | tf_op jit(solution)/shard_map/cross_part/pallas_call | solution.py:293
  130.3 0.5 collective-permute-start.7
  130.8 1.5 collective-permute-done.7
  132.3 0.1 add.19
  132.4 13.0 %all_to_all.27 = f32[16,32,256]{2,1,0:T(8,128)S(1)} all-to-all(f32[16,32,256]{2,1,0:T(8,128)S(1)} %add.19), channel_id=1, replica_groups=mesh['x'=4,'z'=4,'core'=2,'y'=4] {'x','z'}, dimensions={0} | all-to-all | bytes 1048576 | tf_op jit(solution)/shard_map/all_to_all | solution.py:424
  145.4 1.6 broadcast_in_dim.8
  147.0 5.4 %all-to-all-start.4 = ((f32[64,32,256]{2,1,0:T(8,128)}), f32[64,32,256]{2,1,0:T(8,128)S(1)}, u32[]{:S(2)}, u32[]{:S(2)}) async-start(f32[64,32,256]{2,1,0:T(8,128)} %broadcast_in_dim.8), calls=%async_computation.4 | async-start | bytes 4194304 | tf_op jit(solution)/shard_map/all_to_all | solution.py:53
  152.5 2.6 %copy.7 = f32[16,2,256,8]{3,2,1,0:T(8,128)} copy(f32[16,2,256,8]{2,3,0,1:T(8,128)S(1)} %maximum_bitcast_fusion) | data formatting | bytes 524288 | tf_op jit(solution)/shard_map/transpose | solution.py:429
  155.1 4.6 %reshape.41 = f32[32,2048]{1,0:T(8,128)} reshape(f32[16,2,256,8]{3,2,1,0:T(8,128)} %copy.7) | data formatting | bytes 524288 | tf_op jit(solution)/shard_map/reshape | solution.py:429
  159.7 19.5 %all-to-all-done.4.mine_ref = f32[64,32,256]{2,1,0:T(8,128)S(1)} async-done(((f32[64,32,256]{2,1,0:T(8,128)}), f32[64,32,256]{2,1,0:T(8,128)S(1)}, u32[]{:S(2)}, u32[]{:S(2)}) %all-to-all-start.4) | async-done | bytes 2097184 | tf_op jit(solution)/shard_map/all_to_all | solution.py:53
  179.3 3.7 %collective-permute-start.8 = (f32[64,32,256]{2,1,0:T(8,128)S(1)}, f32[64,32,256]{2,1,0:T(8,128)S(1)}, u32[]{:S(2)}, u32[]{:S(2)}) collective-permute-start(f32[64,32,256]{2,1,0:T(8,128)S(1)} %all-to-all-done.4.mine_ref), channel_id=1, source_target_pairs={{0,4},{4,0},{1,5},{5,1},{2,6},{6,2},{3,7},{7,3},{8,12},{12,8},{9,1... | collective-permute-start | bytes 6291464 | tf_op jit(solution)/shard_map/ppermute | solution.py:57
  183.0 3.8 %collective-permute-done.8.other_ref = f32[64,32,256]{2,1,0:T(8,128)S(1)} collective-permute-done((f32[64,32,256]{2,1,0:T(8,128)S(1)}, f32[64,32,256]{2,1,0:T(8,128)S(1)}, u32[]{:S(2)}, u32[]{:S(2)}) %collective-permute-start.8) | collective-permute-done | bytes 2097184 | tf_op jit(solution)/shard_map/ppermute | solution.py:57
  186.8 58.8 %newton_schulz.1 = f32[32,256]{1,0:T(8,128)} custom-call(s32[3]{0:T(128)S(1)} %pad_add_fusion.place_ref, f32[64,32,256]{2,1,0:T(8,128)S(1)} %all-to-all-done.4.mine_ref, f32[64,32,256]{2,1,0:T(8,128)S(1)} %collective-permute-done.8.other_ref), custom_call_target="tpu_custom_call" | custom-call | tf_op jit(solution)/shard_map/newton_schulz/pallas_call | solution.py:381
  (9 shorter events, 0.2 us)
Async XLA Ops:
  0.6 11.9 %collective-permute-start.2 = (s32[32,3072]{1,0:T(8,128)}, s32[32,3072]{1,0:T(8,128)S(1)}, u32[]{:S(2)}, u32[]{:S(2)}) collective-permute-start(s32[32,3072]{1,0:T(8,128)} %c0.3), channel_id=1, source_target_pairs={{0,3},{1,0},{2,1},{3,2},{4,7},{5,4},{6,5},{7,6},{8,11},{9,8},{10,9... | collective-permute-start | bytes 1179656 | tf_op jit(solution)/shard_map/ppermute | solution.py:65
  4.3 11.1 %collective-permute-start.1 = (s32[32,3072]{1,0:T(8,128)}, s32[32,3072]{1,0:T(8,128)S(1)}, u32[]{:S(2)}, u32[]{:S(2)}) collective-permute-start(s32[32,3072]{1,0:T(8,128)} %c0.3), channel_id=1, source_target_pairs={{0,1},{1,2},{2,3},{3,0},{4,5},{5,6},{6,7},{7,4},{8,9},{9,10},{10,1... | collective-permute-start | bytes 1179656 | tf_op jit(solution)/shard_map/ppermute | solution.py:65
  4.3 1.4 collective-permute-start
  12.6 26.3 %copy-start = (s32[32,3072]{1,0:T(8,128)}, s32[32,3072]{1,0:T(8,128)S(1)}, u32[]{:S(2)}) copy-start(s32[32,3072]{1,0:T(8,128)S(1)} %collective-permute-done.2.c3) | copy-start | bytes 1179652
  15.3 23.6 %copy-start.1 = (s32[32,3072]{1,0:T(8,128)}, s32[32,3072]{1,0:T(8,128)S(1)}, u32[]{:S(2)}) copy-start(s32[32,3072]{1,0:T(8,128)S(1)} %collective-permute-done.1.c1) | copy-start | bytes 1179652
  16.3 18.1 %all-to-all-start = ((f32[16,32,256]{2,1,0:T(8,128)}), f32[16,32,256]{2,1,0:T(8,128)S(1)}, u32[]{:S(2)}, u32[]{:S(2)}) async-start(f32[16,32,256]{2,1,0:T(8,128)} %broadcast_in_dim.6), calls=%async_computation | async-start | bytes 1048576 | tf_op jit(solution)/shard_map/all_to_all | solution.py:53
  24.6 9.7 %collective-permute-start.3 = (s32[32,3072]{1,0:T(8,128)S(1)}, s32[32,3072]{1,0:T(8,128)S(1)}, u32[]{:S(2)}, u32[]{:S(2)}) collective-permute-start(s32[32,3072]{1,0:T(8,128)S(1)} %collective-permute-done.1.c1), channel_id=1, source_target_pairs={{0,1},{1,2},{2,3},{3,0},{4,5},{5,6},{6,7},{7,4},{8,9},{9,10},{10,1... | collective-permute-start | bytes 1179656 | tf_op jit(solution)/shard_map/ppermute | solution.py:65
  34.3 4.6 %copy-start.2 = (s32[32,3072]{1,0:T(8,128)}, s32[32,3072]{1,0:T(8,128)S(1)}, u32[]{:S(2)}) copy-start(s32[32,3072]{1,0:T(8,128)S(1)} %collective-permute-done.3.c2) | copy-start | bytes 1179652
  34.3 4.6 %collective-permute-start.4 = (f32[16,32,256]{2,1,0:T(8,128)S(1)}, f32[16,32,256]{2,1,0:T(8,128)S(1)}, u32[]{:S(2)}, u32[]{:S(2)}) collective-permute-start(f32[16,32,256]{2,1,0:T(8,128)S(1)} %all-to-all-done.first_ref), channel_id=1, source_target_pairs={{0,4},{4,0},{1,5},{5,1},{2,6},{6,2},{3,7},{7,3},{8,12},{12,8},{9,1... | collective-permute-start | bytes 1572872 | tf_op jit(solution)/shard_map/ppermute | solution.py:57
  65.3 2.1 collective-permute-start.5
  103.8 4.7 %collective-permute-start.6 = (f32[64,8,256]{2,1,0:T(8,128)S(1)}, f32[64,8,256]{2,1,0:T(8,128)S(1)}, u32[]{:S(2)}, u32[]{:S(2)}) collective-permute-start(f32[64,8,256]{2,1,0:T(8,128)S(1)} %all_to_all.26.mine_ref), channel_id=1, source_target_pairs={{0,4},{4,0},{1,5},{5,1},{2,6},{6,2},{3,7},{7,3},{8,12},{12,8},{9,1... | collective-permute-start | bytes 1572872 | tf_op jit(solution)/shard_map/ppermute | solution.py:57
  130.3 2.0 collective-permute-start.7
  147.0 32.2 %all-to-all-start.4 = ((f32[64,32,256]{2,1,0:T(8,128)}), f32[64,32,256]{2,1,0:T(8,128)S(1)}, u32[]{:S(2)}, u32[]{:S(2)}) async-start(f32[64,32,256]{2,1,0:T(8,128)} %broadcast_in_dim.8), calls=%async_computation.4 | async-start | bytes 4194304 | tf_op jit(solution)/shard_map/all_to_all | solution.py:53
  179.3 7.5 %collective-permute-start.8 = (f32[64,32,256]{2,1,0:T(8,128)S(1)}, f32[64,32,256]{2,1,0:T(8,128)S(1)}, u32[]{:S(2)}, u32[]{:S(2)}) collective-permute-start(f32[64,32,256]{2,1,0:T(8,128)S(1)} %all-to-all-done.4.mine_ref), channel_id=1, source_target_pairs={{0,4},{4,0},{1,5},{5,1},{2,6},{6,2},{3,7},{7,3},{8,12},{12,8},{9,1... | collective-permute-start | bytes 6291464 | tf_op jit(solution)/shard_map/ppermute | solution.py:57

commit v9 on v8

--- a/solution.py
+++ b/solution.py
@@ -120,7 +120,7 @@
         rotated_ref[pl.ds(j * 32, 32)] = part.reshape(32, SUB, count)
         return carry
 
-    lax.fori_loop(0, D // 256, rotate, 0)
+    lax.fori_loop(0, D // 256, rotate, 0, unroll=2)
     for copy in copies:
         copy.wait()
 
@@ -191,8 +191,8 @@
         group(eight, 1, counted)
         return carry
 
-    lax.fori_loop(0, 4, functools.partial(eight_rows, counted=True), 0)
-    lax.fori_loop(4, M // 8, functools.partial(eight_rows, counted=False), 0)
+    lax.fori_loop(0, 4, functools.partial(eight_rows, counted=True), 0, unroll=2)
+    lax.fori_loop(4, M // 8, functools.partial(eight_rows, counted=False), 0, unroll=2)
 
 
 def code_sums(place, points, first, second, codes):
@@ -278,7 +278,7 @@
 
         if stage == 1:
             acc_ref[...] = jnp.zeros_like(acc_ref)
-        lax.fori_loop(0, 4, part, 0)
+        lax.fori_loop(0, 4, part, 0, unroll=4)
         if stage > 0:
             for h in range(4):
                 even = acc_ref[h * 64 : h * 64 + 32]

time: 246 us -> 254 us (1.033)
  Pallas kernels: 107 us -> 112 us
    pallas_call x1, Pallas kernels: 21.8 us -> 30 us  [cross_part(): pl.pallas_call(cross_kernel, out_shape=(half, half), in_specs=[SMEM, ANY,...]
    pallas_call x1, Pallas kernels: 26.4 us -> 23.7 us  [code_sums(): pl.pallas_call(sums_kernel, out_shape=(half, half), in_specs=[SMEM, ANY,...]
where the time goes in v9:
time: 254 us; the launch traced here: 252 us
  Pallas kernels  112 us (44%)
  waiting for transfers between devices  48.8 us (19%)
  blocking collectives  48.8 us (19%)
  starting transfers between devices  29.9 us (12%)
  local copies, waits for them, and re-layouts  9.81 us (4%)
    pallas_call x1, Pallas kernels, newton_schulz(): pl.pallas_call(iterate_kernel, out_shape=jax.ShapeDtypeStruct((32, 256),...  58.8 us
    pallas_call x1, Pallas kernels, cross_part(): pl.pallas_call(cross_kernel, out_shape=(half, half), in_specs=[SMEM, ANY,...  30 us
    pallas_call x1, Pallas kernels, code_sums(): pl.pallas_call(sums_kernel, out_shape=(half, half), in_specs=[SMEM, ANY,...  23.7 us
    all_to_all x1, blocking collectives, shards(): sums = jnp.sum(lax.all_to_all(sums, CHIPS, 0, 0, tiled=True), axis=0)  20.2 us
    all_to_all x2, waiting for transfers between devices, spread_to(): return lax.all_to_all(copies, axes, 0, 0, tiled=True)  19.5 us
    ppermute x3, waiting for transfers between devices, shift(): return lax.ppermute(value, 'y', [(s, (s + by) % 4) for s in range(4)])  19.3 us
    all_to_all x1, blocking collectives, spread_to(): return lax.all_to_all(copies, axes, 0, 0, tiled=True)  15.6 us
    all_to_all x2, starting transfers between devices, spread_to(): return lax.all_to_all(copies, axes, 0, 0, tiled=True)  13.7 us
  transfers between devices with their start and end apart: 11, of which 9 were waited for; matrix products, arithmetic and copies ran while one was open for 3% of the time, Pallas kernels for 0%

profile of v9, /device:TPU:1, one launch (start us, length us, event | category | flops | bytes accessed | tf_op | source)
XLA Modules:
  0.0 251.5 jit_solution(1915620354385475957)
XLA Ops:
  0.6 3.6 %collective-permute-start.2 = (s32[32,3072]{1,0:T(8,128)}, s32[32,3072]{1,0:T(8,128)S(1)}, u32[]{:S(2)}, u32[]{:S(2)}) collective-permute-start(s32[32,3072]{1,0:T(8,128)} %c0.3), channel_id=1, source_target_pairs={{0,3},{1,0},{2,1},{3,2},{4,7},{5,4},{6,5},{7,6},{8,11},{9,8},{10,9... | collective-permute-start | bytes 1179656 | tf_op jit(solution)/shard_map/ppermute | solution.py:65
  4.3 0.0 collective-permute-start.1
  4.3 1.4 collective-permute-start
  5.7 0.0 collective-permute-done
  5.7 6.9 %collective-permute-done.2.c3 = s32[32,3072]{1,0:T(8,128)S(1)} collective-permute-done((s32[32,3072]{1,0:T(8,128)}, s32[32,3072]{1,0:T(8,128)S(1)}, u32[]{:S(2)}, u32[]{:S(2)}) %collective-permute-start.2) | collective-permute-done | bytes 393248 | tf_op jit(solution)/shard_map/ppermute | solution.py:65
  12.6 0.0 copy-start
  12.6 2.8 %collective-permute-done.1.c1 = s32[32,3072]{1,0:T(8,128)S(1)} collective-permute-done((s32[32,3072]{1,0:T(8,128)}, s32[32,3072]{1,0:T(8,128)S(1)}, u32[]{:S(2)}, u32[]{:S(2)}) %collective-permute-start.1) | collective-permute-done | bytes 393248 | tf_op jit(solution)/shard_map/ppermute | solution.py:65
  15.3 0.0 copy-start.1
  15.4 0.9 broadcast_in_dim.6
  16.3 8.3 %all-to-all-start = ((f32[16,32,256]{2,1,0:T(8,128)}), f32[16,32,256]{2,1,0:T(8,128)S(1)}, u32[]{:S(2)}, u32[]{:S(2)}) async-start(f32[16,32,256]{2,1,0:T(8,128)} %broadcast_in_dim.6), calls=%async_computation | async-start | bytes 1048576 | tf_op jit(solution)/shard_map/all_to_all | solution.py:53
  24.6 0.1 collective-permute-start.3
  24.6 9.7 %collective-permute-done.3.c2 = s32[32,3072]{1,0:T(8,128)S(1)} collective-permute-done((s32[32,3072]{1,0:T(8,128)S(1)}, s32[32,3072]{1,0:T(8,128)S(1)}, u32[]{:S(2)}, u32[]{:S(2)}) %collective-permute-start.3) | collective-permute-done | bytes 393248 | tf_op jit(solution)/shard_map/ppermute | solution.py:65
  34.3 0.0 copy-start.2
  34.3 0.0 all-to-all-done.first_ref
  34.3 3.1 %collective-permute-start.4 = (f32[16,32,256]{2,1,0:T(8,128)S(1)}, f32[16,32,256]{2,1,0:T(8,128)S(1)}, u32[]{:S(2)}, u32[]{:S(2)}) collective-permute-start(f32[16,32,256]{2,1,0:T(8,128)S(1)} %all-to-all-done.first_ref), channel_id=1, source_target_pairs={{0,4},{4,0},{1,5},{5,1},{2,6},{6,2},{3,7},{7,3},{8,12},{12,8},{9,1... | collective-permute-start | bytes 1572872 | tf_op jit(solution)/shard_map/ppermute | solution.py:57
  37.4 0.1 pad_add_fusion.place_ref
  37.5 1.5 collective-permute-done.4.second_ref
  38.9 0.0 copy-done
  38.9 0.0 copy-done.1
  38.9 0.0 copy-done.2
  38.9 23.7 %code_sums.1 = (f32[64,2,1152]{2,1,0:T(2,128)S(1)}, f32[64,2,1152]{2,1,0:T(2,128)S(1)}) custom-call(s32[3]{0:T(128)S(1)} %pad_add_fusion.place_ref, f32[3072,256]{1,0:T(8,128)} %pts_ref.3, f32[16,32,256]{2,1,0:T(8,128)S(1)} %all-to-all-done.first_ref, f32[16,32,256]{2,1,0:T(8,128)S(1)} %collective-permute-done.4.second_ref, s32[32,3072]{1,0:T(8,128)} %c0.3, ...), custom_call_target="tpu_custom_call" | custom-call | tf_op jit(solution)/shard_map/code_sums/pallas_call | solution.py:201
  62.6 0.5 collective-permute-start.5
  63.1 1.6 collective-permute-done.5
  64.7 0.3 add.18
  65.0 20.2 %all_to_all.25 = f32[64,2,1152]{2,1,0:T(2,128)S(1)} all-to-all(f32[64,2,1152]{2,1,0:T(2,128)S(1)} %add.18), channel_id=1, replica_groups=mesh['x'=4,'z'=4,'core'=2,'y'=4] {'y','x','z'}, dimensions={0} | all-to-all | bytes 1179648 | tf_op jit(solution)/shard_map/all_to_all | solution.py:416
  85.2 0.2 reduce_sum.18
  85.5 15.6 %all_to_all.26.mine_ref = f32[64,8,256]{2,1,0:T(8,128)S(1)} all-to-all(f32[64,8,256]{2,1,0:T(8,128)S(1)} %broadcast_in_dim.7), channel_id=1, replica_groups=mesh['x'=4,'z'=4,'core'=2,'y'=4] {'y','x','z'}, dimensions={0} | all-to-all | bytes 1048576 | tf_op jit(solution)/shard_map/all_to_all | solution.py:53
  101.1 3.4 %collective-permute-start.6 = (f32[64,8,256]{2,1,0:T(8,128)S(1)}, f32[64,8,256]{2,1,0:T(8,128)S(1)}, u32[]{:S(2)}, u32[]{:S(2)}) collective-permute-start(f32[64,8,256]{2,1,0:T(8,128)S(1)} %all_to_all.26.mine_ref), channel_id=1, source_target_pairs={{0,4},{4,0},{1,5},{5,1},{2,6},{6,2},{3,7},{7,3},{8,12},{12,8},{9,1... | collective-permute-start | bytes 1572872 | tf_op jit(solution)/shard_map/ppermute | solution.py:57
  104.5 1.5 collective-permute-done.6.other_ref
  106.0 30.0 %cross_part.1 = (f32[16,32,256]{2,1,0:T(8,128)S(1)}, f32[16,32,256]{2,1,0:T(8,128)S(1)}) custom-call(s32[3]{0:T(128)S(1)} %pad_add_fusion.place_ref, f32[3072,256]{1,0:T(8,128)} %pts_ref.3, f32[64,8,256]{2,1,0:T(8,128)S(1)} %all_to_all.26.mine_ref, f32[64,8,256]{2,1,0:T(8,128)S(1)} %collective-permute-done.6.other_ref, s32[32,3072]{1,0:T(8,128)} %c0.3, ...), custom_call_target="tpu_custom_call" | custom-call | tf_op jit(solution)/shard_map/cross_part/pallas_call | solution.py:293
  136.1 0.5 collective-permute-start.7
  136.5 1.5 collective-permute-done.7
  138.1 0.1 add.19
  138.1 13.1 %all_to_all.27 = f32[16,32,256]{2,1,0:T(8,128)S(1)} all-to-all(f32[16,32,256]{2,1,0:T(8,128)S(1)} %add.19), channel_id=1, replica_groups=mesh['x'=4,'z'=4,'core'=2,'y'=4] {'x','z'}, dimensions={0} | all-to-all | bytes 1048576 | tf_op jit(solution)/shard_map/all_to_all | solution.py:424
  151.2 1.6 broadcast_in_dim.8
  152.8 5.4 %all-to-all-start.4 = ((f32[64,32,256]{2,1,0:T(8,128)}), f32[64,32,256]{2,1,0:T(8,128)S(1)}, u32[]{:S(2)}, u32[]{:S(2)}) async-start(f32[64,32,256]{2,1,0:T(8,128)} %broadcast_in_dim.8), calls=%async_computation.4 | async-start | bytes 4194304 | tf_op jit(solution)/shard_map/all_to_all | solution.py:53
  158.3 2.6 %copy.7 = f32[16,2,256,8]{3,2,1,0:T(8,128)} copy(f32[16,2,256,8]{2,3,0,1:T(8,128)S(1)} %maximum_bitcast_fusion) | data formatting | bytes 524288 | tf_op jit(solution)/shard_map/transpose | solution.py:429
  160.9 4.6 %reshape.41 = f32[32,2048]{1,0:T(8,128)} reshape(f32[16,2,256,8]{3,2,1,0:T(8,128)} %copy.7) | data formatting | bytes 524288 | tf_op jit(solution)/shard_map/reshape | solution.py:429
  165.5 19.5 %all-to-all-done.4.mine_ref = f32[64,32,256]{2,1,0:T(8,128)S(1)} async-done(((f32[64,32,256]{2,1,0:T(8,128)}), f32[64,32,256]{2,1,0:T(8,128)S(1)}, u32[]{:S(2)}, u32[]{:S(2)}) %all-to-all-start.4) | async-done | bytes 2097184 | tf_op jit(solution)/shard_map/all_to_all | solution.py:53
  185.0 3.7 %collective-permute-start.8 = (f32[64,32,256]{2,1,0:T(8,128)S(1)}, f32[64,32,256]{2,1,0:T(8,128)S(1)}, u32[]{:S(2)}, u32[]{:S(2)}) collective-permute-start(f32[64,32,256]{2,1,0:T(8,128)S(1)} %all-to-all-done.4.mine_ref), channel_id=1, source_target_pairs={{0,4},{4,0},{1,5},{5,1},{2,6},{6,2},{3,7},{7,3},{8,12},{12,8},{9,1... | collective-permute-start | bytes 6291464 | tf_op jit(solution)/shard_map/ppermute | solution.py:57
  188.7 3.8 %collective-permute-done.8.other_ref = f32[64,32,256]{2,1,0:T(8,128)S(1)} collective-permute-done((f32[64,32,256]{2,1,0:T(8,128)S(1)}, f32[64,32,256]{2,1,0:T(8,128)S(1)}, u32[]{:S(2)}, u32[]{:S(2)}) %collective-permute-start.8) | collective-permute-done | bytes 2097184 | tf_op jit(solution)/shard_map/ppermute | solution.py:57
  192.5 58.8 %newton_schulz.1 = f32[32,256]{1,0:T(8,128)} custom-call(s32[3]{0:T(128)S(1)} %pad_add_fusion.place_ref, f32[64,32,256]{2,1,0:T(8,128)S(1)} %all-to-all-done.4.mine_ref, f32[64,32,256]{2,1,0:T(8,128)S(1)} %collective-permute-done.8.other_ref), custom_call_target="tpu_custom_call" | custom-call | tf_op jit(solution)/shard_map/newton_schulz/pallas_call | solution.py:381
  (9 shorter events, 0.2 us)
Async XLA Ops:
  0.6 11.9 %collective-permute-start.2 = (s32[32,3072]{1,0:T(8,128)}, s32[32,3072]{1,0:T(8,128)S(1)}, u32[]{:S(2)}, u32[]{:S(2)}) collective-permute-start(s32[32,3072]{1,0:T(8,128)} %c0.3), channel_id=1, source_target_pairs={{0,3},{1,0},{2,1},{3,2},{4,7},{5,4},{6,5},{7,6},{8,11},{9,8},{10,9... | collective-permute-start | bytes 1179656 | tf_op jit(solution)/shard_map/ppermute | solution.py:65
  4.3 11.1 %collective-permute-start.1 = (s32[32,3072]{1,0:T(8,128)}, s32[32,3072]{1,0:T(8,128)S(1)}, u32[]{:S(2)}, u32[]{:S(2)}) collective-permute-start(s32[32,3072]{1,0:T(8,128)} %c0.3), channel_id=1, source_target_pairs={{0,1},{1,2},{2,3},{3,0},{4,5},{5,6},{6,7},{7,4},{8,9},{9,10},{10,1... | collective-permute-start | bytes 1179656 | tf_op jit(solution)/shard_map/ppermute | solution.py:65
  4.3 1.4 collective-permute-start
  12.6 26.3 %copy-start = (s32[32,3072]{1,0:T(8,128)}, s32[32,3072]{1,0:T(8,128)S(1)}, u32[]{:S(2)}) copy-start(s32[32,3072]{1,0:T(8,128)S(1)} %collective-permute-done.2.c3) | copy-start | bytes 1179652
  15.3 23.6 %copy-start.1 = (s32[32,3072]{1,0:T(8,128)}, s32[32,3072]{1,0:T(8,128)S(1)}, u32[]{:S(2)}) copy-start(s32[32,3072]{1,0:T(8,128)S(1)} %collective-permute-done.1.c1) | copy-start | bytes 1179652
  16.3 18.1 %all-to-all-start = ((f32[16,32,256]{2,1,0:T(8,128)}), f32[16,32,256]{2,1,0:T(8,128)S(1)}, u32[]{:S(2)}, u32[]{:S(2)}) async-start(f32[16,32,256]{2,1,0:T(8,128)} %broadcast_in_dim.6), calls=%async_computation | async-start | bytes 1048576 | tf_op jit(solution)/shard_map/all_to_all | solution.py:53
  24.6 9.7 %collective-permute-start.3 = (s32[32,3072]{1,0:T(8,128)S(1)}, s32[32,3072]{1,0:T(8,128)S(1)}, u32[]{:S(2)}, u32[]{:S(2)}) collective-permute-start(s32[32,3072]{1,0:T(8,128)S(1)} %collective-permute-done.1.c1), channel_id=1, source_target_pairs={{0,1},{1,2},{2,3},{3,0},{4,5},{5,6},{6,7},{7,4},{8,9},{9,10},{10,1... | collective-permute-start | bytes 1179656 | tf_op jit(solution)/shard_map/ppermute | solution.py:65
  34.3 4.6 %copy-start.2 = (s32[32,3072]{1,0:T(8,128)}, s32[32,3072]{1,0:T(8,128)S(1)}, u32[]{:S(2)}) copy-start(s32[32,3072]{1,0:T(8,128)S(1)} %collective-permute-done.3.c2) | copy-start | bytes 1179652
  34.3 4.6 %collective-permute-start.4 = (f32[16,32,256]{2,1,0:T(8,128)S(1)}, f32[16,32,256]{2,1,0:T(8,128)S(1)}, u32[]{:S(2)}, u32[]{:S(2)}) collective-permute-start(f32[16,32,256]{2,1,0:T(8,128)S(1)} %all-to-all-done.first_ref), channel_id=1, source_target_pairs={{0,4},{4,0},{1,5},{5,1},{2,6},{6,2},{3,7},{7,3},{8,12},{12,8},{9,1... | collective-permute-start | bytes 1572872 | tf_op jit(solution)/shard_map/ppermute | solution.py:57
  62.6 2.1 collective-permute-start.5
  101.1 5.0 %collective-permute-start.6 = (f32[64,8,256]{2,1,0:T(8,128)S(1)}, f32[64,8,256]{2,1,0:T(8,128)S(1)}, u32[]{:S(2)}, u32[]{:S(2)}) collective-permute-start(f32[64,8,256]{2,1,0:T(8,128)S(1)} %all_to_all.26.mine_ref), channel_id=1, source_target_pairs={{0,4},{4,0},{1,5},{5,1},{2,6},{6,2},{3,7},{7,3},{8,12},{12,8},{9,1... | collective-permute-start | bytes 1572872 | tf_op jit(solution)/shard_map/ppermute | solution.py:57
  136.1 2.0 collective-permute-start.7
  152.8 32.2 %all-to-all-start.4 = ((f32[64,32,256]{2,1,0:T(8,128)}), f32[64,32,256]{2,1,0:T(8,128)S(1)}, u32[]{:S(2)}, u32[]{:S(2)}) async-start(f32[64,32,256]{2,1,0:T(8,128)} %broadcast_in_dim.8), calls=%async_computation.4 | async-start | bytes 4194304 | tf_op jit(solution)/shard_map/all_to_all | solution.py:53
  185.0 7.5 %collective-permute-start.8 = (f32[64,32,256]{2,1,0:T(8,128)S(1)}, f32[64,32,256]{2,1,0:T(8,128)S(1)}, u32[]{:S(2)}, u32[]{:S(2)}) collective-permute-start(f32[64,32,256]{2,1,0:T(8,128)S(1)} %all-to-all-done.4.mine_ref), channel_id=1, source_target_pairs={{0,4},{4,0},{1,5},{5,1},{2,6},{6,2},{3,7},{7,3},{8,12},{12,8},{9,1... | collective-permute-start | bytes 6291464 | tf_op jit(solution)/shard_map/ppermute | solution.py:57

commit v10 on v8

--- a/solution.py
+++ b/solution.py
@@ -192,7 +192,7 @@
         return carry
 
     lax.fori_loop(0, 4, functools.partial(eight_rows, counted=True), 0)
-    lax.fori_loop(4, M // 8, functools.partial(eight_rows, counted=False), 0)
+    lax.fori_loop(4, M // 8, functools.partial(eight_rows, counted=False), 0, unroll=2)
 
 
 def code_sums(place, points, first, second, codes):
@@ -278,7 +278,7 @@
 
         if stage == 1:
             acc_ref[...] = jnp.zeros_like(acc_ref)
-        lax.fori_loop(0, 4, part, 0)
+        lax.fori_loop(0, 4, part, 0, unroll=2 if 0 < stage < 4 else 1)
         if stage > 0:
             for h in range(4):
                 even = acc_ref[h * 64 : h * 64 + 32]

time: 246 us -> 244 us (level)
  no operation moved by 1% of the time
where the time goes in v10:
time: 244 us; the launch traced here: 243 us
  Pallas kernels  105 us (43%)
  waiting for transfers between devices  48.8 us (20%)
  blocking collectives  48.8 us (20%)
  starting transfers between devices  29.7 us (12%)
  local copies, waits for them, and re-layouts  9.81 us (4%)
    pallas_call x1, Pallas kernels, newton_schulz(): pl.pallas_call(iterate_kernel, out_shape=jax.ShapeDtypeStruct((32, 256),...  58.8 us
    pallas_call x1, Pallas kernels, code_sums(): pl.pallas_call(sums_kernel, out_shape=(half, half), in_specs=[SMEM, ANY,...  24.7 us
    pallas_call x1, Pallas kernels, cross_part(): pl.pallas_call(cross_kernel, out_shape=(half, half), in_specs=[SMEM, ANY,...  21.2 us
    all_to_all x1, blocking collectives, shards(): sums = jnp.sum(lax.all_to_all(sums, CHIPS, 0, 0, tiled=True), axis=0)  20.2 us
    all_to_all x2, waiting for transfers between devices, spread_to(): return lax.all_to_all(copies, axes, 0, 0, tiled=True)  19.5 us
    ppermute x3, waiting for transfers between devices, shift(): return lax.ppermute(value, 'y', [(s, (s + by) % 4) for s in range(4)])  19.3 us
    all_to_all x1, blocking collectives, spread_to(): return lax.all_to_all(copies, axes, 0, 0, tiled=True)  15.6 us
    all_to_all x2, starting transfers between devices, spread_to(): return lax.all_to_all(copies, axes, 0, 0, tiled=True)  13.7 us
  transfers between devices with their start and end apart: 11, of which 9 were waited for; matrix products, arithmetic and copies ran while one was open for 3% of the time, Pallas kernels for 0%

profile of v10, /device:TPU:1, one launch (start us, length us, event | category | flops | bytes accessed | tf_op | source)
XLA Modules:
  0.0 243.2 jit_solution(1094614820730951475)
XLA Ops:
  0.6 3.6 %collective-permute-start.2 = (s32[32,3072]{1,0:T(8,128)}, s32[32,3072]{1,0:T(8,128)S(1)}, u32[]{:S(2)}, u32[]{:S(2)}) collective-permute-start(s32[32,3072]{1,0:T(8,128)} %c0.3), channel_id=1, source_target_pairs={{0,3},{1,0},{2,1},{3,2},{4,7},{5,4},{6,5},{7,6},{8,11},{9,8},{10,9... | collective-permute-start | bytes 1179656 | tf_op jit(solution)/shard_map/ppermute | solution.py:65
  4.3 0.0 collective-permute-start.1
  4.3 1.4 collective-permute-start
  5.7 0.0 collective-permute-done
  5.7 6.9 %collective-permute-done.2.c3 = s32[32,3072]{1,0:T(8,128)S(1)} collective-permute-done((s32[32,3072]{1,0:T(8,128)}, s32[32,3072]{1,0:T(8,128)S(1)}, u32[]{:S(2)}, u32[]{:S(2)}) %collective-permute-start.2) | collective-permute-done | bytes 393248 | tf_op jit(solution)/shard_map/ppermute | solution.py:65
  12.6 0.0 copy-start
  12.6 2.8 %collective-permute-done.1.c1 = s32[32,3072]{1,0:T(8,128)S(1)} collective-permute-done((s32[32,3072]{1,0:T(8,128)}, s32[32,3072]{1,0:T(8,128)S(1)}, u32[]{:S(2)}, u32[]{:S(2)}) %collective-permute-start.1) | collective-permute-done | bytes 393248 | tf_op jit(solution)/shard_map/ppermute | solution.py:65
  15.3 0.0 copy-start.1
  15.4 0.9 broadcast_in_dim.6
  16.3 8.3 %all-to-all-start = ((f32[16,32,256]{2,1,0:T(8,128)}), f32[16,32,256]{2,1,0:T(8,128)S(1)}, u32[]{:S(2)}, u32[]{:S(2)}) async-start(f32[16,32,256]{2,1,0:T(8,128)} %broadcast_in_dim.6), calls=%async_computation | async-start | bytes 1048576 | tf_op jit(solution)/shard_map/all_to_all | solution.py:53
  24.6 0.1 collective-permute-start.3
  24.6 9.7 %collective-permute-done.3.c2 = s32[32,3072]{1,0:T(8,128)S(1)} collective-permute-done((s32[32,3072]{1,0:T(8,128)S(1)}, s32[32,3072]{1,0:T(8,128)S(1)}, u32[]{:S(2)}, u32[]{:S(2)}) %collective-permute-start.3) | collective-permute-done | bytes 393248 | tf_op jit(solution)/shard_map/ppermute | solution.py:65
  34.3 0.0 copy-start.2
  34.3 0.0 all-to-all-done.first_ref
  34.3 3.1 %collective-permute-start.4 = (f32[16,32,256]{2,1,0:T(8,128)S(1)}, f32[16,32,256]{2,1,0:T(8,128)S(1)}, u32[]{:S(2)}, u32[]{:S(2)}) collective-permute-start(f32[16,32,256]{2,1,0:T(8,128)S(1)} %all-to-all-done.first_ref), channel_id=1, source_target_pairs={{0,4},{4,0},{1,5},{5,1},{2,6},{6,2},{3,7},{7,3},{8,12},{12,8},{9,1... | collective-permute-start | bytes 1572872 | tf_op jit(solution)/shard_map/ppermute | solution.py:57
  37.4 0.1 pad_add_fusion.place_ref
  37.5 1.5 collective-permute-done.4.second_ref
  38.9 0.0 copy-done
  38.9 0.0 copy-done.1
  38.9 0.0 copy-done.2
  38.9 24.7 %code_sums.1 = (f32[64,2,1152]{2,1,0:T(2,128)S(1)}, f32[64,2,1152]{2,1,0:T(2,128)S(1)}) custom-call(s32[3]{0:T(128)S(1)} %pad_add_fusion.place_ref, f32[3072,256]{1,0:T(8,128)} %pts_ref.3, f32[16,32,256]{2,1,0:T(8,128)S(1)} %all-to-all-done.first_ref, f32[16,32,256]{2,1,0:T(8,128)S(1)} %collective-permute-done.4.second_ref, s32[32,3072]{1,0:T(8,128)} %c0.3, ...), custom_call_target="tpu_custom_call" | custom-call | tf_op jit(solution)/shard_map/code_sums/pallas_call | solution.py:201
  63.6 0.5 collective-permute-start.5
  64.0 1.6 collective-permute-done.5
  65.7 0.3 add.18
  66.0 20.2 %all_to_all.25 = f32[64,2,1152]{2,1,0:T(2,128)S(1)} all-to-all(f32[64,2,1152]{2,1,0:T(2,128)S(1)} %add.18), channel_id=1, replica_groups=mesh['x'=4,'z'=4,'core'=2,'y'=4] {'y','x','z'}, dimensions={0} | all-to-all | bytes 1179648 | tf_op jit(solution)/shard_map/all_to_all | solution.py:416
  86.2 0.2 reduce_sum.18
  86.5 15.6 %all_to_all.26.mine_ref = f32[64,8,256]{2,1,0:T(8,128)S(1)} all-to-all(f32[64,8,256]{2,1,0:T(8,128)S(1)} %broadcast_in_dim.7), channel_id=1, replica_groups=mesh['x'=4,'z'=4,'core'=2,'y'=4] {'y','x','z'}, dimensions={0} | all-to-all | bytes 1048576 | tf_op jit(solution)/shard_map/all_to_all | solution.py:53
  102.1 3.2 %collective-permute-start.6 = (f32[64,8,256]{2,1,0:T(8,128)S(1)}, f32[64,8,256]{2,1,0:T(8,128)S(1)}, u32[]{:S(2)}, u32[]{:S(2)}) collective-permute-start(f32[64,8,256]{2,1,0:T(8,128)S(1)} %all_to_all.26.mine_ref), channel_id=1, source_target_pairs={{0,4},{4,0},{1,5},{5,1},{2,6},{6,2},{3,7},{7,3},{8,12},{12,8},{9,1... | collective-permute-start | bytes 1572872 | tf_op jit(solution)/shard_map/ppermute | solution.py:57
  105.2 1.5 collective-permute-done.6.other_ref
  106.8 21.2 %cross_part.1 = (f32[16,32,256]{2,1,0:T(8,128)S(1)}, f32[16,32,256]{2,1,0:T(8,128)S(1)}) custom-call(s32[3]{0:T(128)S(1)} %pad_add_fusion.place_ref, f32[3072,256]{1,0:T(8,128)} %pts_ref.3, f32[64,8,256]{2,1,0:T(8,128)S(1)} %all_to_all.26.mine_ref, f32[64,8,256]{2,1,0:T(8,128)S(1)} %collective-permute-done.6.other_ref, s32[32,3072]{1,0:T(8,128)} %c0.3, ...), custom_call_target="tpu_custom_call" | custom-call | tf_op jit(solution)/shard_map/cross_part/pallas_call | solution.py:293
  128.0 0.5 collective-permute-start.7
  128.4 1.5 collective-permute-done.7
  130.0 0.1 add.19
  130.0 13.1 %all_to_all.27 = f32[16,32,256]{2,1,0:T(8,128)S(1)} all-to-all(f32[16,32,256]{2,1,0:T(8,128)S(1)} %add.19), channel_id=1, replica_groups=mesh['x'=4,'z'=4,'core'=2,'y'=4] {'x','z'}, dimensions={0} | all-to-all | bytes 1048576 | tf_op jit(solution)/shard_map/all_to_all | solution.py:424
  143.1 1.6 broadcast_in_dim.8
  144.7 5.4 %all-to-all-start.4 = ((f32[64,32,256]{2,1,0:T(8,128)}), f32[64,32,256]{2,1,0:T(8,128)S(1)}, u32[]{:S(2)}, u32[]{:S(2)}) async-start(f32[64,32,256]{2,1,0:T(8,128)} %broadcast_in_dim.8), calls=%async_computation.4 | async-start | bytes 4194304 | tf_op jit(solution)/shard_map/all_to_all | solution.py:53
  150.2 2.6 %copy.7 = f32[16,2,256,8]{3,2,1,0:T(8,128)} copy(f32[16,2,256,8]{2,3,0,1:T(8,128)S(1)} %maximum_bitcast_fusion) | data formatting | bytes 524288 | tf_op jit(solution)/shard_map/transpose | solution.py:429
  152.8 4.6 %reshape.41 = f32[32,2048]{1,0:T(8,128)} reshape(f32[16,2,256,8]{3,2,1,0:T(8,128)} %copy.7) | data formatting | bytes 524288 | tf_op jit(solution)/shard_map/reshape | solution.py:429
  157.4 19.5 %all-to-all-done.4.mine_ref = f32[64,32,256]{2,1,0:T(8,128)S(1)} async-done(((f32[64,32,256]{2,1,0:T(8,128)}), f32[64,32,256]{2,1,0:T(8,128)S(1)}, u32[]{:S(2)}, u32[]{:S(2)}) %all-to-all-start.4) | async-done | bytes 2097184 | tf_op jit(solution)/shard_map/all_to_all | solution.py:53
  176.9 3.7 %collective-permute-start.8 = (f32[64,32,256]{2,1,0:T(8,128)S(1)}, f32[64,32,256]{2,1,0:T(8,128)S(1)}, u32[]{:S(2)}, u32[]{:S(2)}) collective-permute-start(f32[64,32,256]{2,1,0:T(8,128)S(1)} %all-to-all-done.4.mine_ref), channel_id=1, source_target_pairs={{0,4},{4,0},{1,5},{5,1},{2,6},{6,2},{3,7},{7,3},{8,12},{12,8},{9,1... | collective-permute-start | bytes 6291464 | tf_op jit(solution)/shard_map/ppermute | solution.py:57
  180.6 3.8 %collective-permute-done.8.other_ref = f32[64,32,256]{2,1,0:T(8,128)S(1)} collective-permute-done((f32[64,32,256]{2,1,0:T(8,128)S(1)}, f32[64,32,256]{2,1,0:T(8,128)S(1)}, u32[]{:S(2)}, u32[]{:S(2)}) %collective-permute-start.8) | collective-permute-done | bytes 2097184 | tf_op jit(solution)/shard_map/ppermute | solution.py:57
  184.4 58.8 %newton_schulz.1 = f32[32,256]{1,0:T(8,128)} custom-call(s32[3]{0:T(128)S(1)} %pad_add_fusion.place_ref, f32[64,32,256]{2,1,0:T(8,128)S(1)} %all-to-all-done.4.mine_ref, f32[64,32,256]{2,1,0:T(8,128)S(1)} %collective-permute-done.8.other_ref), custom_call_target="tpu_custom_call" | custom-call | tf_op jit(solution)/shard_map/newton_schulz/pallas_call | solution.py:381
  (9 shorter events, 0.2 us)
Async XLA Ops:
  0.6 11.9 %collective-permute-start.2 = (s32[32,3072]{1,0:T(8,128)}, s32[32,3072]{1,0:T(8,128)S(1)}, u32[]{:S(2)}, u32[]{:S(2)}) collective-permute-start(s32[32,3072]{1,0:T(8,128)} %c0.3), channel_id=1, source_target_pairs={{0,3},{1,0},{2,1},{3,2},{4,7},{5,4},{6,5},{7,6},{8,11},{9,8},{10,9... | collective-permute-start | bytes 1179656 | tf_op jit(solution)/shard_map/ppermute | solution.py:65
  4.3 11.1 %collective-permute-start.1 = (s32[32,3072]{1,0:T(8,128)}, s32[32,3072]{1,0:T(8,128)S(1)}, u32[]{:S(2)}, u32[]{:S(2)}) collective-permute-start(s32[32,3072]{1,0:T(8,128)} %c0.3), channel_id=1, source_target_pairs={{0,1},{1,2},{2,3},{3,0},{4,5},{5,6},{6,7},{7,4},{8,9},{9,10},{10,1... | collective-permute-start | bytes 1179656 | tf_op jit(solution)/shard_map/ppermute | solution.py:65
  4.3 1.4 collective-permute-start
  12.6 26.3 %copy-start = (s32[32,3072]{1,0:T(8,128)}, s32[32,3072]{1,0:T(8,128)S(1)}, u32[]{:S(2)}) copy-start(s32[32,3072]{1,0:T(8,128)S(1)} %collective-permute-done.2.c3) | copy-start | bytes 1179652
  15.3 23.6 %copy-start.1 = (s32[32,3072]{1,0:T(8,128)}, s32[32,3072]{1,0:T(8,128)S(1)}, u32[]{:S(2)}) copy-start(s32[32,3072]{1,0:T(8,128)S(1)} %collective-permute-done.1.c1) | copy-start | bytes 1179652
  16.3 18.1 %all-to-all-start = ((f32[16,32,256]{2,1,0:T(8,128)}), f32[16,32,256]{2,1,0:T(8,128)S(1)}, u32[]{:S(2)}, u32[]{:S(2)}) async-start(f32[16,32,256]{2,1,0:T(8,128)} %broadcast_in_dim.6), calls=%async_computation | async-start | bytes 1048576 | tf_op jit(solution)/shard_map/all_to_all | solution.py:53
  24.6 9.7 %collective-permute-start.3 = (s32[32,3072]{1,0:T(8,128)S(1)}, s32[32,3072]{1,0:T(8,128)S(1)}, u32[]{:S(2)}, u32[]{:S(2)}) collective-permute-start(s32[32,3072]{1,0:T(8,128)S(1)} %collective-permute-done.1.c1), channel_id=1, source_target_pairs={{0,1},{1,2},{2,3},{3,0},{4,5},{5,6},{6,7},{7,4},{8,9},{9,10},{10,1... | collective-permute-start | bytes 1179656 | tf_op jit(solution)/shard_map/ppermute | solution.py:65
  34.3 4.6 %copy-start.2 = (s32[32,3072]{1,0:T(8,128)}, s32[32,3072]{1,0:T(8,128)S(1)}, u32[]{:S(2)}) copy-start(s32[32,3072]{1,0:T(8,128)S(1)} %collective-permute-done.3.c2) | copy-start | bytes 1179652
  34.3 4.6 %collective-permute-start.4 = (f32[16,32,256]{2,1,0:T(8,128)S(1)}, f32[16,32,256]{2,1,0:T(8,128)S(1)}, u32[]{:S(2)}, u32[]{:S(2)}) collective-permute-start(f32[16,32,256]{2,1,0:T(8,128)S(1)} %all-to-all-done.first_ref), channel_id=1, source_target_pairs={{0,4},{4,0},{1,5},{5,1},{2,6},{6,2},{3,7},{7,3},{8,12},{12,8},{9,1... | collective-permute-start | bytes 1572872 | tf_op jit(solution)/shard_map/ppermute | solution.py:57
  63.6 2.1 collective-permute-start.5
  102.1 4.7 %collective-permute-start.6 = (f32[64,8,256]{2,1,0:T(8,128)S(1)}, f32[64,8,256]{2,1,0:T(8,128)S(1)}, u32[]{:S(2)}, u32[]{:S(2)}) collective-permute-start(f32[64,8,256]{2,1,0:T(8,128)S(1)} %all_to_all.26.mine_ref), channel_id=1, source_target_pairs={{0,4},{4,0},{1,5},{5,1},{2,6},{6,2},{3,7},{7,3},{8,12},{12,8},{9,1... | collective-permute-start | bytes 1572872 | tf_op jit(solution)/shard_map/ppermute | solution.py:57
  128.0 2.0 collective-permute-start.7
  144.7 32.2 %all-to-all-start.4 = ((f32[64,32,256]{2,1,0:T(8,128)}), f32[64,32,256]{2,1,0:T(8,128)S(1)}, u32[]{:S(2)}, u32[]{:S(2)}) async-start(f32[64,32,256]{2,1,0:T(8,128)} %broadcast_in_dim.8), calls=%async_computation.4 | async-start | bytes 4194304 | tf_op jit(solution)/shard_map/all_to_all | solution.py:53
  176.9 7.5 %collective-permute-start.8 = (f32[64,32,256]{2,1,0:T(8,128)S(1)}, f32[64,32,256]{2,1,0:T(8,128)S(1)}, u32[]{:S(2)}, u32[]{:S(2)}) collective-permute-start(f32[64,32,256]{2,1,0:T(8,128)S(1)} %all-to-all-done.4.mine_ref), channel_id=1, source_target_pairs={{0,4},{4,0},{1,5},{5,1},{2,6},{6,2},{3,7},{7,3},{8,12},{12,8},{9,1... | collective-permute-start | bytes 6291464 | tf_op jit(solution)/shard_map/ppermute | solution.py:57
